TPU v7x, 256 devices: a whole 4x4x8 slice. The times are simulated.
256 devices in a mesh: pipe: 8 (over y, core), expert: 32 (over x, z).
Axes of the slice: x: 4, y: 4, z: 8, core: 2. Of those that a mesh axis runs over, the one named last changes fastest.
Arguments:
- acts: bfloat16 [8, 2, 2048, 1440], P('pipe', None, 'expert'), may hold values from -6 to 6
- hidden: bfloat16 [8, 2, 2048, 4, 1440], P('pipe', None, 'expert'), may hold values from -6 to 6
- ids: int32 [8, 2, 2048, 4], P('pipe', None, 'expert'), may hold values from 0 to 31, all different within a row; in each aligned block of 64 rows (0 to 63, 64 to 127, ..., all dimensions but the last counted through in order) at most 12 rows name the same one
- version: int32 [8, 2], P('pipe'), may hold values from 0 to 1
- router: bfloat16 [8, 2, 1440, 32], P('pipe'), may hold values from -0.078125 to 0.078125
- down: bfloat16 [8, 32, 1440, 1440], P('pipe', 'expert'), may hold values from -0.15625 to 0.15625
- grad_top: bfloat16 [2, 2048, 1440], P(None, 'expert'), may hold values from -6 to 6
Outputs:
- grad_in: bfloat16 [8, 2, 2048, 1440], P('pipe', None, 'expert')
- grad_hidden: bfloat16 [8, 2, 2048, 4, 1440], P('pipe', None, 'expert')
- grad_router: float32 [8, 1440, 32], P('pipe', 'expert')
Inputs may be any that keep to these rules, and one draw needn't show every extreme that they name: `ids`: each token names 4 different experts. In the rows of one device for one section and micro-batch (aligned blocks of 64 tokens) no expert is named by more than 12 slots, and some blocks reach 12.
All inputs are finite; a program needn't handle non-finite values.
Results may differ from a plain program's by a relative error of at most 0.019.
Values may be sent and summed in bfloat16 or wider, within the bound.
No kernel may reach another device: no remote copies, remote signals or barrier semaphores. Data moves between devices by JAX's collectives and lax.ppermute only.
A program may use at most 64 MiB of HBM per device.

v0:
```python
import functools

import jax
import jax.numpy as jnp
from jax import lax
from jax.experimental import pallas as pl
from jax.experimental.pallas import tpu as pltpu
from jax.sharding import PartitionSpec as P

BF = jnp.bfloat16
F32 = jnp.float32
I32 = jnp.int32
NN = (((1,), (0,)), ((), ()))
NT = (((1,), (1,)), ((), ()))
TN = (((0,), (0,)), ((), ()))
VM = pl.BlockSpec(memory_space=pltpu.VMEM)
SM = pl.BlockSpec(memory_space=pltpu.SMEM)

N, T, K, E, HALF = 128, 64, 4, 32, 12
ROWS = 2 * HALF
ALL = E * ROWS
W = 256
MIBS = (20, 20, 32, 12, 12, 20, 24, 20)
LATER = 224


def dot(a, b, dims):
    return lax.dot_general(a, b, dims, preferred_element_type=F32)


def iota(shape, dim):
    return lax.broadcasted_iota(I32, shape, dim)


def one(mask):
    return jnp.where(mask, 1.0, 0.0).astype(BF)


def divided(x, by):
    return ((x.astype(F32) + 0.5) * (1.0 / by)).astype(I32)


def split(x):
    high = x.astype(BF)
    return high, (x - high.astype(F32)).astype(BF)


def slot_codes(ids_ref):
    named = []
    for k in range(K):
        row = jnp.concatenate([ids_ref[0, k : k + 1, :], ids_ref[1, k : k + 1, :]], axis=1)
        named.append(row == iota((E, N), 0))
    marks = sum(jnp.where(hit, 1.0, 0.0) for hit in named).astype(BF)
    first, second = iota((N, N), 0), iota((N, N), 1)
    earlier = one((first < second) & ((first >> 6) == (second >> 6)))
    place = dot(marks, earlier, NN) + (HALF * (iota((E, N), 1) >> 6)).astype(F32)
    return [jnp.where(hit, place, -1.0) for hit in named]


def token_major(codes):
    lane = iota((N, N * K), 1)
    spread = one((lane >> 2) == iota((N, N * K), 0))
    which = iota((E, N * K), 1) & (K - 1)
    out = jnp.zeros((E, N * K), F32)
    for k in range(K):
        out = jnp.where(which == k, dot(codes[k].astype(BF), spread, NN), out)
    return out


def rows_by_slots(code):
    expand = one(divided(iota((ALL, E), 0), ROWS) == iota((ALL, E), 1))
    row = iota((ALL, code.shape[1]), 0)
    inner = (row - ROWS * divided(row, ROWS)).astype(F32)
    return one(dot(expand, code.astype(BF), NN) == inner)


def slots_by_rows(code):
    expand = one(divided(iota((E, ALL), 1), ROWS) == iota((E, ALL), 0))
    row = iota((code.shape[1], ALL), 1)
    inner = (row - ROWS * divided(row, ROWS)).astype(F32)
    return one(dot(code.astype(BF), expand, TN) == inner)


def first_half(rows, width, start=0):
    row = iota((rows, width), 0) + start
    return (row - ROWS * divided(row, ROWS)) < HALF


def dispatch_kernel(ids_ref, hid_ref, grad_ref, out_ref):
    codes = slot_codes(ids_ref)
    pick = rows_by_slots(token_major(codes))
    tokens = rows_by_slots(functools.reduce(jnp.maximum, codes))
    width = grad_ref.shape[1]
    for start in range(0, width, 256):
        cols = slice(start, min(start + 256, width))
        size = cols.stop - start
        grad = dot(tokens, grad_ref[:, cols], NN)
        hid = dot(pick, hid_ref[:, :, cols].reshape(N * K, size), NN)
        for lanes in range(0, size, 128):
            at = 2 * ROWS * ((start + lanes) // 128)
            cut = min(lanes + 128, size)
            left = grad[:, lanes:cut].reshape(E, ROWS, cut - lanes)
            right = hid[:, lanes:cut].reshape(E, ROWS, cut - lanes)
            if cut - lanes == 128:
                out_ref[:, at : at + ROWS, :] = left.astype(BF)
                out_ref[:, at + ROWS : at + 2 * ROWS, :] = right.astype(BF)
            else:
                tail = [
                    left[:, 0:16],
                    jnp.concatenate([left[:, 16:24], right[:, 0:8]], axis=1),
                    right[:, 8:24],
                    jnp.zeros((E, 16, 32), F32),
                ]
                out_ref[:, at : at + 16, :] = jnp.concatenate(tail, axis=2).astype(BF)


def tables_kernel(*refs):
    held, down_ref, tab_ref, back_ref, ids_ref = refs[:8], refs[8], refs[9], refs[10], refs[11]
    for b in range(8):
        for m in range(2):
            tab_ref[m * W + b * E : m * W + (b + 1) * E, :] = held[b][m * E : (m + 1) * E, :]
    rows = jnp.concatenate([held[b][2 * E : 2 * E + 8, 0:N].astype(F32) for b in range(8)], axis=0)
    for j in range(K):
        for b in range(8):
            ids_ref[8 * j + b : 8 * j + b + 1, :] = rows[8 * b + j : 8 * b + j + 1, :]
    for m in range(2):
        back_ref[m * W : (m + 1) * W, :] = dot(
            tab_ref[m * W : (m + 1) * W, :], down_ref[...], NT
        ).astype(BF)


def expert_kernel(got_ref, down_ref, back_ref, base_ref, out_ref, grad_ref, hid_ref):
    inner = down_ref.shape[0]
    full = 128 * (inner // 128)
    for lanes in range(0, full, 128):
        at = 2 * ROWS * (lanes // 128)
        cols = slice(lanes, lanes + 128)
        grad_ref[:, cols] = got_ref[:, at : at + ROWS, :].reshape(ALL, 128)
        hid_ref[:, cols] = got_ref[:, at + ROWS : at + 2 * ROWS, :].reshape(ALL, 128)
    at = 2 * ROWS * (full // 128)
    tail = got_ref[:, at : at + 16, :].astype(F32)
    middle = tail[:, :, 32:64]
    grad = jnp.concatenate([tail[:, :, 0:32], middle[:, 0:8]], axis=1)
    hid = jnp.concatenate([middle[:, 8:16], tail[:, :, 64:96]], axis=1)
    grad_ref[:, full:inner] = grad.astype(BF).reshape(ALL, 32)
    hid_ref[:, full:inner] = hid.astype(BF).reshape(ALL, 32)
    total = jnp.zeros((ALL, 1), F32)
    for start in range(0, inner, 256):
        cols = slice(start, min(start + 256, inner))
        base = dot(grad_ref[...], down_ref[cols, :], NT)
        base_ref[:, cols] = base
        total = total + jnp.sum(hid_ref[:, cols].astype(F32) * base, axis=1, keepdims=True)
    high, low = split(total)
    left = dot(hid_ref[...], back_ref[0:W, :], NT)
    right = dot(hid_ref[...], back_ref[W : 2 * W, :], NT)
    proj = jnp.where(first_half(ALL, W), left, right)
    lane = iota((ALL, W), 1)
    tail = jnp.where(lane == LATER, high.astype(F32), low.astype(F32))
    tail = jnp.where(lane < LATER + 2, tail, 0.0)
    out_ref[...] = jnp.where(lane < LATER, proj, tail).astype(BF)


def id_masks(ids_ref):
    spread = one(divided(iota((8, W), 1), E) == iota((8, W), 0))
    lane = iota((N, W), 1) & (E - 1)
    masks = []
    for j in range(K):
        wide = dot(ids_ref[8 * j : 8 * j + 8, :].astype(BF), spread, TN)
        masks.append(wide == lane.astype(F32))
    return masks, spread


def blocks_kernel(got_ref, row_ref, ids_ref, gate_ref, out_ref):
    pick = slots_by_rows(jnp.concatenate(slot_codes(row_ref), axis=1))
    slots = dot(pick, got_ref[...], NN)
    gates = [gate_ref[:, k : k + 1] for k in range(K)]
    parts = [slots[k * N : (k + 1) * N] for k in range(K)]
    lane = iota((N, W), 1)
    full = []
    for part in parts:
        dots = part[:, LATER : LATER + 1] + part[:, LATER + 1 : LATER + 2]
        full.append(jnp.where(lane < LATER, part, dots))
    mean = sum(gates[k] * full[k] for k in range(K))
    masks, spread = id_masks(ids_ref)
    rows = []
    for k in range(K):
        value = gates[k] * (full[k] - mean)
        high, low = split(value)
        for j in range(K):
            source = jnp.where(masks[j] & (lane < LATER), high.astype(F32), 0.0)
            if j < 2:
                extra = high if j == 0 else low
                source = jnp.where(lane == LATER, extra.astype(F32), source)
            rows.append(source.astype(BF))
    packed = dot(spread, jnp.concatenate(rows, axis=0), NT).astype(BF)
    for d in range(8):
        out_ref[d] = packed


def solve_kernel(at_ref, got_ref, row_ref, ids_ref, gate_ref, out_ref, coef_ref):
    at = at_ref[0]
    depth = iota((8, K * N), 0)
    found = jnp.zeros((8, K * N), F32)
    for back in range(7, -1, -1):
        where = jnp.minimum(at + back, 7)
        valid = (at + back <= 7).astype(F32)
        block = got_ref[where].astype(F32)
        fresh = []
        for k in range(K):
            part = block[:, k * K * N : (k + 1) * K * N]
            fixed = part[7:8, 0:N] + part[7:8, N : 2 * N]
            terms = jnp.sum(part * found, axis=0, keepdims=True)
            total = fixed
            for j in range(K):
                total = total + terms[:, j * N : (j + 1) * N]
            fresh.append(total * valid)
        fresh = jnp.concatenate(fresh, axis=1)
        if back:
            found = jnp.where(depth == 0, fresh, pltpu.roll(found, 1, 0))
        else:
            found = jnp.where(depth == 7, fresh, found)
    masks, spread = id_masks(ids_ref)
    high, low = split(found)
    coef = jnp.zeros((N, W), F32)
    for j in range(K):
        cut = slice(j * N, (j + 1) * N)
        wide = dot(high[:, cut], spread, TN) + dot(low[:, cut], spread, TN)
        coef = jnp.where(masks[j], wide, coef)
    coef_ref[...] = coef.astype(BF)
    lane = iota((N, W), 1)
    rows = []
    for k in range(K):
        gate = gate_ref[:, k : k + 1]
        up, rest = split(gate)
        tail = jnp.where(lane == LATER, up.astype(F32), rest.astype(F32))
        tail = jnp.where(lane < LATER + 2, tail, 0.0)
        rows.append(jnp.where(lane < LATER, gate * coef, tail).astype(BF))
    pick = rows_by_slots(jnp.concatenate(slot_codes(row_ref), axis=1))
    out_ref[...] = dot(pick, jnp.concatenate(rows, axis=0), NN).astype(BF)


def passed_kernel(coef_ref, tab_ref, grad_ref, acts_ref, pass_ref, part_ref):
    for m in range(2):
        rows = slice(m * T, (m + 1) * T)
        moved = dot(coef_ref[rows, :], tab_ref[m * W : (m + 1) * W, :], NN)
        pass_ref[rows, :] = (grad_ref[rows, :].astype(F32) + moved).astype(BF)
    own = coef_ref[:, LATER:W]
    width = acts_ref.shape[1]
    router = (dot(acts_ref[...], own, TN) / T).astype(BF)
    each = width // E
    row, col = iota((ALL, width), 0), iota((ALL, width), 1)
    peer = divided(row, ROWS)
    inner = row - ROWS * peer
    source = peer * each + inner
    first = dot(one(source == col), router, NN)
    second = dot(one((source + ROWS == col) & (inner + ROWS < each)), router, NN)
    part_ref[:, 0:E] = first.astype(BF)
    part_ref[:, E : 2 * E] = second.astype(BF)


def answer_kernel(got_ref, base_ref, back_ref, part_ref, out_ref):
    width = base_ref.shape[1]
    got = got_ref[...].astype(F32)
    gate = got[:, LATER : LATER + 1] + got[:, LATER + 1 : LATER + 2]
    coef = jnp.where(iota((ALL, W), 1) < LATER, got, 0.0)
    half = first_half(ALL, W)
    left = jnp.where(half, coef, 0.0).astype(BF)
    right = jnp.where(half, 0.0, coef).astype(BF)
    for start in range(0, width, 256):
        cols = slice(start, min(start + 256, width))
        moved = dot(left, back_ref[0:W, cols], NN) + dot(right, back_ref[W : 2 * W, cols], NN)
        out_ref[:, cols] = (gate * base_ref[:, cols] + moved).astype(BF)
    out_ref[:, width : width + 2 * E] = part_ref[...]
    out_ref[:, width + 2 * E :] = jnp.zeros((ALL, out_ref.shape[1] - width - 2 * E), BF)


def combine_kernel(got_ref, ids_ref, out_ref, router_ref):
    pick = slots_by_rows(token_major(slot_codes(ids_ref)))
    width = out_ref.shape[2]
    for start in range(0, width, 256):
        cols = slice(start, min(start + 256, width))
        own = dot(pick, got_ref[:, cols], NN).astype(BF)
        out_ref[:, :, cols] = own.reshape(N, K, cols.stop - start)
    parts = got_ref[:, width : width + 2 * E].astype(F32).reshape(E, ROWS, 2 * E)
    total = jnp.sum(parts, axis=0)
    each = width // E
    turn = iota((E, 2 * E), 1) - iota((E, 2 * E), 0)
    flipped = [jnp.zeros((E, ROWS), F32)] * 2
    for _ in range(3):
        piece = total.astype(BF)
        total = total - piece.astype(F32)
        flipped = [flipped[q] + dot(one(turn == q * E), piece, NT) for q in range(2)]
    router_ref[:, 0:ROWS] = flipped[0]
    router_ref[:, ROWS:each] = flipped[1][:, 0 : each - ROWS]


def call(body, shapes, args, mib, smem=0, scratch=()):
    return pl.pallas_call(
        body,
        out_shape=[jax.ShapeDtypeStruct(s, d) for s, d in shapes],
        in_specs=[SM] * smem + [VM] * (len(args) - smem),
        out_specs=[VM] * len(shapes),
        scratch_shapes=list(scratch),
        compiler_params=pltpu.CompilerParams(vmem_limit_bytes=mib << 20),
    )(*args)


def exchange(x, axis):
    return lax.all_to_all(x, axis, split_axis=0, concat_axis=0, tiled=True)


def on_device(acts, hidden, ids, version, router, down, grad_top):
    pipe = lax.axis_size("pipe")
    section = lax.axis_index("pipe")
    width = acts.shape[-1]
    inner = hidden.shape[-1]
    inputs = acts[0]
    routes = ids[0]
    mats = down[0, 0]
    grads = grad_top.reshape(N, width)
    turned = routes.transpose(0, 2, 1)
    tall = 2 * ROWS * (inner // 128) + 16

    (sent,) = call(
        dispatch_kernel,
        [((E, tall, 128), BF)],
        (turned, hidden[0].reshape(N, K, inner), grads),
        MIBS[0],
    )
    arrived = exchange(sent, "expert")

    picked_version = version[0][:, None, None] == 1
    tables = jnp.where(picked_version, router[0, 1][None], router[0, 0][None])
    flipped = tables.transpose(0, 2, 1).reshape(2 * E, width)
    id_rows = jnp.pad(
        turned.transpose(1, 0, 2).reshape(K, N).astype(BF), ((0, 8 - K), (0, width - N))
    )
    own = jnp.concatenate([flipped, id_rows], axis=0)
    held = [
        lax.ppermute(own, "pipe", [(i, i - by) for i in range(by, pipe)]) for by in range(1, pipe)
    ] + [own]
    table_rows, back, id_all = call(
        tables_kernel,
        [((2 * W, width), BF), ((2 * W, inner), BF), ((K * 8, N), F32)],
        (*held, mats),
        MIBS[1],
    )

    logits = jnp.einsum("mtd,mde->mte", inputs, tables, preferred_element_type=F32)
    labels = jnp.arange(E, dtype=I32)
    picked = routes[:, :, :, None] == labels
    chosen = jnp.sum(jnp.where(picked, logits[:, :, None, :], 0.0), axis=3)
    scores = jnp.exp(chosen)
    gating = (scores / jnp.sum(scores, axis=2, keepdims=True)).reshape(N, K)

    base, proj = call(
        expert_kernel,
        [((ALL, inner), F32), ((ALL, W), BF)],
        (arrived, mats, back),
        MIBS[2],
        scratch=[pltpu.VMEM((ALL, inner), BF)] * 2,
    )
    proj, gating = lax.optimization_barrier((proj, gating))
    returned = exchange(proj.reshape(E, ROWS, W), "expert").reshape(ALL, W)
    (blocks,) = call(
        blocks_kernel,
        [((8, 8, K * K * N), BF)],
        (returned, turned, id_all, gating),
        MIBS[3],
    )
    gathered = exchange(blocks, "pipe")
    coef_sent, coef = call(
        solve_kernel,
        [((ALL, W), BF), ((N, W), BF)],
        (section.reshape(1), gathered, turned, id_all, gating),
        MIBS[4],
        smem=1,
    )
    coef_got = exchange(coef_sent.reshape(E, ROWS, W), "expert").reshape(ALL, W)
    passed, parts = call(
        passed_kernel,
        [((N, width), BF), ((ALL, 2 * E), BF)],
        (coef, table_rows, grads, inputs.reshape(N, width)),
        MIBS[5],
    )
    wide = 128 * pl.cdiv(inner + 2 * E, 128)
    (answer,) = call(
        answer_kernel, [((ALL, wide), BF)], (coef_got, base, back, parts), MIBS[6]
    )
    answered = exchange(answer.reshape(E, ROWS, wide), "expert").reshape(ALL, wide)
    hidden_grads, grad_router = call(
        combine_kernel, [((N, K, inner), BF), ((E, width // E), F32)], (answered, turned), MIBS[7]
    )
    return (
        passed.reshape(1, 2, T, width),
        hidden_grads.reshape(1, 2, T, K, inner),
        grad_router.T[None],
    )


def solution(mesh):
    placed = (
        P("pipe", None, "expert", None),
        P("pipe", None, "expert", None, None),
        P("pipe", None, "expert", None),
        P("pipe", None),
        P("pipe", None, None, None),
        P("pipe", "expert", None, None),
        P(None, "expert", None),
    )
    return jax.shard_map(
        on_device,
        mesh=mesh,
        in_specs=placed,
        out_specs=(
            P("pipe", None, "expert", None),
            P("pipe", None, "expert", None, None),
            P("pipe", "expert", None),
        ),
        check_vma=False,
    )
```

profile of v0, /device:TPU:32, one launch (start us, length us, event | category | flops | bytes accessed | tf_op | source)
XLA Modules:
  0.0 261.6 jit_solution(5686584337049960713)
XLA Ops:
  0.6 1.4 copy-done.7
  2.0 1.0 copy-done.8
  3.0 0.7 copy-done.23
  3.7 3.1 %shard_map.94 = bf16[32,544,128]{2,1,0:T(8,128)(2,1)S(1)} custom-call(s32[2,4,64]{2,1,0:T(4,128)S(1)} %bitcast.57, bf16[128,4,1440]{2,1,0:T(4,128)(2,1)S(1)} %bitcast.52, bf16[128,1440]{1,0:T(8,128)(2,1)S(1)} %bitcast.53), custom_call_target="tpu_custom_call" | custom-call | tf_op jit(solution)/shard_map/pallas_call | solution.py:298
  6.9 2.1 copy-done
  9.0 11.4 %all-to-all-start = ((bf16[32,544,128]{2,1,0:T(8,128)(2,1)}), bf16[32,544,128]{2,1,0:T(8,128)(2,1)}, u32[]{:S(2)}, u32[]{:S(2)}) async-start(bf16[32,544,128]{2,1,0:T(8,128)(2,1)} %copy-done), calls=%async_computation | async-start | bytes 8912896 | tf_op jit(solution)/shard_map/all_to_all | solution.py:309
  20.8 1.3 collective-permute-start.6
  22.1 1.3 collective-permute-start.5
  23.4 1.3 collective-permute-start.4
  24.7 1.3 collective-permute-start.3
  26.0 1.3 collective-permute-start.2
  27.8 1.9 collective-permute-done.6.refs_6_
  30.4 1.3 collective-permute-start.1
  31.7 11.3 %collective-permute-done.5.refs_5_ = bf16[72,1440]{1,0:T(8,128)(2,1)S(1)} collective-permute-done((bf16[72,1440]{1,0:T(8,128)(2,1)S(1)}, bf16[72,1440]{1,0:T(8,128)(2,1)S(1)}, u32[]{:S(2)}, u32[]{:S(2)}) %collective-permute-start.5) | collective-permute-done | bytes 207392 | tf_op jit(solution)/shard_map/ppermute | solution.py:340
  43.0 0.7 copy-done.13
  43.7 1.3 collective-permute-start
  45.7 0.7 copy-done.17
  46.4 0.7 copy-done.19
  47.7 2.3 copy-done.1
  50.0 0.9 copy-done.12
  50.9 0.9 copy-done.14
  51.9 0.9 copy-done.16
  52.8 0.9 copy-done.18
  53.7 0.9 copy-done.20
  54.7 2.6 %shard_map.95 = (bf16[512,1440]{1,0:T(8,128)(2,1)S(1)}, bf16[512,1440]{1,0:T(8,128)(2,1)S(1)}, f32[32,128]{1,0:T(8,128)S(1)}) custom-call(bf16[72,1440]{1,0:T(8,128)(2,1)S(1)} %collective-permute-done.refs_0_, bf16[72,1440]{1,0:T(8,128)(2,1)S(1)} %collective-permute-done.1.refs_1_, bf16[72,1440]{1,0:T(8,128)(2,1)S(1)} %copy-done.20, ...), custom_call_target="tpu_custom_call" | custom-call | tf_op jit(solution)/shard_map/pallas_call | solution.py:298
  57.3 63.5 %all-to-all-done.got_ref = bf16[32,544,128]{2,1,0:T(8,128)(2,1)} async-done(((bf16[32,544,128]{2,1,0:T(8,128)(2,1)}), bf16[32,544,128]{2,1,0:T(8,128)(2,1)}, u32[]{:S(2)}, u32[]{:S(2)}) %all-to-all-start) | async-done | bytes 4456480 | tf_op jit(solution)/shard_map/all_to_all | solution.py:309
  120.8 2.3 copy-done.2
  123.0 7.4 %shard_map.96 = (f32[768,1440]{1,0:T(8,128)S(1)}, bf16[768,256]{1,0:T(8,128)(2,1)S(1)}) custom-call(bf16[32,544,128]{2,1,0:T(8,128)(2,1)} %all-to-all-done.got_ref, bf16[1440,1440]{1,0:T(8,128)(2,1)S(1)} %bitcast.46, bf16[512,1440]{1,0:T(8,128)(2,1)S(1)} %get-tuple-element.16.back_ref), custom_call_target="tpu_custom_call" | custom-call | tf_op jit(solution)/shard_map/pallas_call | solution.py:298
  130.5 2.1 copy-done.3
  132.6 23.4 %all_to_all.25 = bf16[32,24,256]{2,1,0:T(8,128)(2,1)S(1)} all-to-all(bf16[32,24,256]{2,1,0:T(8,128)(2,1)S(1)} %bitcast.56), channel_id=1, replica_groups=mesh['pipe'=8,'expert'=32] {'expert'}, dimensions={0} | all-to-all | bytes 786432 | tf_op jit(solution)/shard_map/all_to_all | solution.py:309
  156.0 2.3 shard_map.97
  158.3 4.5 %all-to-all-start.2 = ((bf16[8,8,2048]{2,1,0:T(8,128)(2,1)}), bf16[8,8,2048]{2,1,0:T(8,128)(2,1)S(1)}, u32[]{:S(2)}, u32[]{:S(2)}) async-start(bf16[8,8,2048]{2,1,0:T(8,128)(2,1)} %shard_map.97), calls=%async_computation.2 | async-start | bytes 524288 | tf_op jit(solution)/shard_map/all_to_all | solution.py:309
  162.8 7.5 %all-to-all-done.2.got_ref = bf16[8,8,2048]{2,1,0:T(8,128)(2,1)S(1)} async-done(((bf16[8,8,2048]{2,1,0:T(8,128)(2,1)}), bf16[8,8,2048]{2,1,0:T(8,128)(2,1)S(1)}, u32[]{:S(2)}, u32[]{:S(2)}) %all-to-all-start.2) | async-done | bytes 262176 | tf_op jit(solution)/shard_map/all_to_all | solution.py:309
  170.3 0.7 copy-done.28
  171.0 1.2 shard_map.98
  172.9 0.7 copy-done.10
  173.6 4.8 %all-to-all-start.3 = ((bf16[32,24,256]{2,1,0:T(8,128)(2,1)}), bf16[32,24,256]{2,1,0:T(8,128)(2,1)S(1)}, u32[]{:S(2)}, u32[]{:S(2)}) async-start(bf16[32,24,256]{2,1,0:T(8,128)(2,1)} %bitcast.55), calls=%async_computation.3 | async-start | bytes 786432 | tf_op jit(solution)/shard_map/all_to_all | solution.py:309
  178.4 1.0 copy-done.6
  179.4 1.0 copy-done.9
  180.4 0.8 copy-done.26
  181.2 2.0 shard_map.99
  183.2 0.7 copy-done.21
  183.9 9.1 %all-to-all-done.3 = bf16[32,24,256]{2,1,0:T(8,128)(2,1)S(1)} async-done(((bf16[32,24,256]{2,1,0:T(8,128)(2,1)}), bf16[32,24,256]{2,1,0:T(8,128)(2,1)S(1)}, u32[]{:S(2)}, u32[]{:S(2)}) %all-to-all-start.3) | async-done | bytes 393248 | tf_op jit(solution)/shard_map/all_to_all | solution.py:309
  193.0 2.3 copy-done.4
  195.4 0.9 copy-done.22
  196.3 1.4 shard_map.100
  197.7 60.7 %all_to_all.26 = bf16[32,24,1536]{2,1,0:T(8,128)(2,1)S(1)} all-to-all(bf16[32,24,1536]{2,1,0:T(8,128)(2,1)S(1)} %bitcast.47), channel_id=1, replica_groups=mesh['pipe'=8,'expert'=32] {'expert'}, dimensions={0} | all-to-all | bytes 4718592 | tf_op jit(solution)/shard_map/all_to_all | solution.py:309
  258.5 3.2 %shard_map.101 = (bf16[128,4,1440]{2,1,0:T(4,128)(2,1)}, f32[32,45]{1,0:T(8,128)}) custom-call(bf16[768,1536]{1,0:T(8,128)(2,1)S(1)} %bitcast.48, s32[2,4,64]{2,1,0:T(4,128)S(1)} %bitcast.61), custom_call_target="tpu_custom_call" | custom-call | tf_op jit(solution)/shard_map/pallas_call | solution.py:298
  (59 shorter events, 3.7 us)
Async XLA Ops:
  0.6 1.4 copy-start.7
  2.0 1.0 copy-start.8
  3.0 0.7 copy-start.23
  6.8 2.1 copy-start
  9.0 11.4 %copy-start.30 = (s32[1,2]{1,0:T(1,128)S(1)}, s32[1,2]{1,0:T(1,128)}, u32[]{:S(2)}) copy-start(s32[1,2]{1,0:T(1,128)} %param.10) | copy-start | bytes 28
  9.0 11.6 %copy-start.24 = (s32[1,2,64,4]{2,3,1,0:T(4,128)S(1)}, s32[1,2,64,4]{2,3,1,0:T(4,128)}, u32[]{:S(2)}) copy-start(s32[1,2,64,4]{2,3,1,0:T(4,128)} %param.9) | copy-start | bytes 6148
  9.0 11.7 %copy-start.29 = (bf16[1,2,1440,32]{2,3,1,0:T(8,128)(2,1)S(1)}, bf16[1,2,1440,32]{2,3,1,0:T(8,128)(2,1)}, u32[]{:S(2)}) copy-start(bf16[1,2,1440,32]{2,3,1,0:T(8,128)(2,1)} %param.11) | copy-start | bytes 552964
  9.0 18.3 %copy-start.5 = (bf16[1,2,64,1440]{3,2,1,0:T(8,128)(2,1)S(1)}, bf16[1,2,64,1440]{3,2,1,0:T(8,128)(2,1)}, u32[]{:S(2)}) copy-start(bf16[1,2,64,1440]{3,2,1,0:T(8,128)(2,1)} %param.7) | copy-start | bytes 1105924
  9.0 111.8 %all-to-all-start = ((bf16[32,544,128]{2,1,0:T(8,128)(2,1)}), bf16[32,544,128]{2,1,0:T(8,128)(2,1)}, u32[]{:S(2)}, u32[]{:S(2)}) async-start(bf16[32,544,128]{2,1,0:T(8,128)(2,1)} %copy-done), calls=%async_computation | async-start | bytes 8912896 | tf_op jit(solution)/shard_map/all_to_all | solution.py:309
  20.8 9.0 %collective-permute-start.6 = (bf16[72,1440]{1,0:T(8,128)(2,1)S(1)}, bf16[72,1440]{1,0:T(8,128)(2,1)S(1)}, u32[]{:S(2)}, u32[]{:S(2)}) collective-permute-start(bf16[72,1440]{1,0:T(8,128)(2,1)S(1)} %fusion.2.refs_7_), channel_id=1, source_target_pairs={{224,0},{225,1},{226,2},{227,3},{228,4},{229,5},{230,6},{231,7},{2... | collective-permute-start | bytes 622088 | tf_op jit(solution)/shard_map/ppermute | solution.py:340
  22.1 20.9 %collective-permute-start.5 = (bf16[72,1440]{1,0:T(8,128)(2,1)S(1)}, bf16[72,1440]{1,0:T(8,128)(2,1)S(1)}, u32[]{:S(2)}, u32[]{:S(2)}) collective-permute-start(bf16[72,1440]{1,0:T(8,128)(2,1)S(1)} %fusion.2.refs_7_), channel_id=1, source_target_pairs={{192,0},{224,32},{193,1},{225,33},{194,2},{226,34},{195,3},{227,35... | collective-permute-start | bytes 622088 | tf_op jit(solution)/shard_map/ppermute | solution.py:340
  23.4 21.7 %collective-permute-start.4 = (bf16[72,1440]{1,0:T(8,128)(2,1)S(1)}, bf16[72,1440]{1,0:T(8,128)(2,1)S(1)}, u32[]{:S(2)}, u32[]{:S(2)}) collective-permute-start(bf16[72,1440]{1,0:T(8,128)(2,1)S(1)} %fusion.2.refs_7_), channel_id=1, source_target_pairs={{160,0},{192,32},{224,64},{161,1},{193,33},{225,65},{162,2},{194,3... | collective-permute-start | bytes 622088 | tf_op jit(solution)/shard_map/ppermute | solution.py:340
  24.7 21.1 %collective-permute-start.3 = (bf16[72,1440]{1,0:T(8,128)(2,1)S(1)}, bf16[72,1440]{1,0:T(8,128)(2,1)S(1)}, u32[]{:S(2)}, u32[]{:S(2)}) collective-permute-start(bf16[72,1440]{1,0:T(8,128)(2,1)S(1)} %fusion.2.refs_7_), channel_id=1, source_target_pairs={{128,0},{160,32},{192,64},{224,96},{129,1},{161,33},{193,65},{225,... | collective-permute-start | bytes 622088 | tf_op jit(solution)/shard_map/ppermute | solution.py:340
  26.0 20.4 %collective-permute-start.2 = (bf16[72,1440]{1,0:T(8,128)(2,1)S(1)}, bf16[72,1440]{1,0:T(8,128)(2,1)S(1)}, u32[]{:S(2)}, u32[]{:S(2)}) collective-permute-start(bf16[72,1440]{1,0:T(8,128)(2,1)S(1)} %fusion.2.refs_7_), channel_id=1, source_target_pairs={{96,0},{128,32},{160,64},{192,96},{224,128},{97,1},{129,33},{161,6... | collective-permute-start | bytes 622088 | tf_op jit(solution)/shard_map/ppermute | solution.py:340
  29.8 0.7 copy-start.11
  30.4 16.7 %collective-permute-start.1 = (bf16[72,1440]{1,0:T(8,128)(2,1)S(1)}, bf16[72,1440]{1,0:T(8,128)(2,1)S(1)}, u32[]{:S(2)}, u32[]{:S(2)}) collective-permute-start(bf16[72,1440]{1,0:T(8,128)(2,1)S(1)} %fusion.2.refs_7_), channel_id=1, source_target_pairs={{64,0},{96,32},{128,64},{160,96},{192,128},{224,160},{65,1},{97,33... | collective-permute-start | bytes 622088 | tf_op jit(solution)/shard_map/ppermute | solution.py:340
  43.0 0.7 copy-start.13
  43.7 4.1 %collective-permute-start = (bf16[72,1440]{1,0:T(8,128)(2,1)S(1)}, bf16[72,1440]{1,0:T(8,128)(2,1)S(1)}, u32[]{:S(2)}, u32[]{:S(2)}) collective-permute-start(bf16[72,1440]{1,0:T(8,128)(2,1)S(1)} %fusion.2.refs_7_), channel_id=1, source_target_pairs={{32,0},{64,32},{96,64},{128,96},{160,128},{192,160},{224,192},{33,... | collective-permute-start | bytes 622088 | tf_op jit(solution)/shard_map/ppermute | solution.py:340
  45.1 0.7 copy-start.15
  45.7 0.7 copy-start.17
  46.4 0.7 copy-start.19
  47.7 2.3 copy-start.1
  50.0 0.9 copy-start.12
  50.9 0.9 copy-start.14
  51.9 0.9 copy-start.16
  52.8 0.9 copy-start.18
  53.7 0.9 copy-start.20
  57.3 98.7 %copy-start.27 = (f32[32,128]{1,0:T(8,128)}, f32[32,128]{1,0:T(8,128)S(1)}, u32[]{:S(2)}) copy-start(f32[32,128]{1,0:T(8,128)S(1)} %get-tuple-element.19.ids_ref) | copy-start | bytes 49156
  120.8 2.3 copy-start.2
  130.5 2.1 copy-start.3
  158.3 12.0 %all-to-all-start.2 = ((bf16[8,8,2048]{2,1,0:T(8,128)(2,1)}), bf16[8,8,2048]{2,1,0:T(8,128)(2,1)S(1)}, u32[]{:S(2)}, u32[]{:S(2)}) async-start(bf16[8,8,2048]{2,1,0:T(8,128)(2,1)} %shard_map.97), calls=%async_computation.2 | async-start | bytes 524288 | tf_op jit(solution)/shard_map/all_to_all | solution.py:309
  170.3 0.7 copy-start.28
  172.2 0.6 copy-start.25
  172.9 0.7 copy-start.10
  173.6 19.4 %all-to-all-start.3 = ((bf16[32,24,256]{2,1,0:T(8,128)(2,1)}), bf16[32,24,256]{2,1,0:T(8,128)(2,1)S(1)}, u32[]{:S(2)}, u32[]{:S(2)}) async-start(bf16[32,24,256]{2,1,0:T(8,128)(2,1)} %bitcast.55), calls=%async_computation.3 | async-start | bytes 786432 | tf_op jit(solution)/shard_map/all_to_all | solution.py:309
  178.4 1.0 copy-start.6
  179.4 1.0 copy-start.9
  180.4 0.8 copy-start.26
  183.2 0.7 copy-start.21
  193.0 2.3 copy-start.4
  195.4 0.9 copy-start.22
where the time goes:
time: 263 us; the launch traced here: 262 us
  waiting for transfers between devices  93.8 us (36%)
  blocking collectives  84.1 us (32%)
  starting transfers between devices  29.6 us (11%)
  local copies, waits for them, and re-layouts  29.3 us (11%)
  Pallas kernels  23.3 us (9%)
    all_to_all x2, blocking collectives, exchange(): return lax.all_to_all(x, axis, split_axis=0, concat_axis=0, tiled=True)  84.1 us
    all_to_all x3, waiting for transfers between devices, exchange(): return lax.all_to_all(x, axis, split_axis=0, concat_axis=0, tiled=True)  80.1 us
    unnamed x62, local copies, waits for them, and re-layouts  28.8 us
    pallas_call x8, Pallas kernels, call(): pl.pallas_call(body, out_shape=[jax.ShapeDtypeStruct(s, d) for s, d in sh...  23.3 us
    all_to_all x3, starting transfers between devices, exchange(): return lax.all_to_all(x, axis, split_axis=0, concat_axis=0, tiled=True)  20.6 us
    ppermute x7, waiting for transfers between devices, on_device(): lax.ppermute(own, 'pipe', [(i, i - by) for i in range(by, pipe)])  13.8 us
    ppermute x7, starting transfers between devices, on_device(): lax.ppermute(own, 'pipe', [(i, i - by) for i in range(by, pipe)])  9.02 us
  transfers between devices with their start and end apart: 10, of which 6 were waited for; matrix products, arithmetic and copies ran while one was open for 0% of the time, Pallas kernels for 2%

commit v1 on v0

--- a/solution.py
+++ b/solution.py
@@ -20,7 +20,7 @@
 ROWS = 2 * HALF
 ALL = E * ROWS
 W = 256
-MIBS = (20, 20, 32, 12, 12, 20, 24, 20)
+MIBS = (58, 20, 58, 12, 12, 20, 62, 58)
 LATER = 224
 
 
@@ -86,32 +86,36 @@
     return (row - ROWS * divided(row, ROWS)) < HALF
 
 
-def dispatch_kernel(ids_ref, hid_ref, grad_ref, out_ref):
-    codes = slot_codes(ids_ref)
-    pick = rows_by_slots(token_major(codes))
-    tokens = rows_by_slots(functools.reduce(jnp.maximum, codes))
-    width = grad_ref.shape[1]
-    for start in range(0, width, 256):
-        cols = slice(start, min(start + 256, width))
-        size = cols.stop - start
-        grad = dot(tokens, grad_ref[:, cols], NN)
-        hid = dot(pick, hid_ref[:, :, cols].reshape(N * K, size), NN)
-        for lanes in range(0, size, 128):
-            at = 2 * ROWS * ((start + lanes) // 128)
-            cut = min(lanes + 128, size)
-            left = grad[:, lanes:cut].reshape(E, ROWS, cut - lanes)
-            right = hid[:, lanes:cut].reshape(E, ROWS, cut - lanes)
-            if cut - lanes == 128:
-                out_ref[:, at : at + ROWS, :] = left.astype(BF)
-                out_ref[:, at + ROWS : at + 2 * ROWS, :] = right.astype(BF)
-            else:
-                tail = [
-                    left[:, 0:16],
-                    jnp.concatenate([left[:, 16:24], right[:, 0:8]], axis=1),
-                    right[:, 8:24],
-                    jnp.zeros((E, 16, 32), F32),
-                ]
-                out_ref[:, at : at + 16, :] = jnp.concatenate(tail, axis=2).astype(BF)
+def dispatch_kernel(ids_ref, hid_ref, grad_ref, out_ref, pick_ref, token_ref):
+    step = pl.program_id(0)
+
+    @pl.when(step == 0)
+    def _():
+        codes = slot_codes(ids_ref)
+        pick_ref[...] = rows_by_slots(token_major(codes))
+        token_ref[...] = rows_by_slots(functools.reduce(jnp.maximum, codes))
+
+    size = grad_ref.shape[1]
+    grad = dot(token_ref[...], grad_ref[...], NN).reshape(E, ROWS, size)
+    hid = dot(pick_ref[...], hid_ref[...].reshape(N * K, size), NN).reshape(E, ROWS, size)
+    out_ref[:, 0:ROWS, :] = grad[:, :, 0:128].astype(BF)
+    out_ref[:, ROWS : 2 * ROWS, :] = hid[:, :, 0:128].astype(BF)
+
+    @pl.when(step < pl.num_programs(0) - 1)
+    def _():
+        out_ref[:, 2 * ROWS : 3 * ROWS, :] = grad[:, :, 128:256].astype(BF)
+        out_ref[:, 3 * ROWS : 4 * ROWS, :] = hid[:, :, 128:256].astype(BF)
+
+    @pl.when(step == pl.num_programs(0) - 1)
+    def _():
+        left, right = grad[:, :, 128:160], hid[:, :, 128:160]
+        tail = [
+            left[:, 0:16],
+            jnp.concatenate([left[:, 16:24], right[:, 0:8]], axis=1),
+            right[:, 8:24],
+            jnp.zeros((E, 16, 32), F32),
+        ]
+        out_ref[:, 2 * ROWS : 2 * ROWS + 16, :] = jnp.concatenate(tail, axis=2).astype(BF)
 
 
 def tables_kernel(*refs):
@@ -129,35 +133,48 @@
         ).astype(BF)
 
 
-def expert_kernel(got_ref, down_ref, back_ref, base_ref, out_ref, grad_ref, hid_ref):
-    inner = down_ref.shape[0]
+def expert_kernel(got_ref, down_ref, back_ref, base_ref, out_ref, grad_ref, hid_ref, sum_ref):
+    step = pl.program_id(0)
+    inner = grad_ref.shape[1]
     full = 128 * (inner // 128)
-    for lanes in range(0, full, 128):
-        at = 2 * ROWS * (lanes // 128)
-        cols = slice(lanes, lanes + 128)
-        grad_ref[:, cols] = got_ref[:, at : at + ROWS, :].reshape(ALL, 128)
-        hid_ref[:, cols] = got_ref[:, at + ROWS : at + 2 * ROWS, :].reshape(ALL, 128)
-    at = 2 * ROWS * (full // 128)
-    tail = got_ref[:, at : at + 16, :].astype(F32)
-    middle = tail[:, :, 32:64]
-    grad = jnp.concatenate([tail[:, :, 0:32], middle[:, 0:8]], axis=1)
-    hid = jnp.concatenate([middle[:, 8:16], tail[:, :, 64:96]], axis=1)
-    grad_ref[:, full:inner] = grad.astype(BF).reshape(ALL, 32)
-    hid_ref[:, full:inner] = hid.astype(BF).reshape(ALL, 32)
-    total = jnp.zeros((ALL, 1), F32)
-    for start in range(0, inner, 256):
-        cols = slice(start, min(start + 256, inner))
-        base = dot(grad_ref[...], down_ref[cols, :], NT)
-        base_ref[:, cols] = base
-        total = total + jnp.sum(hid_ref[:, cols].astype(F32) * base, axis=1, keepdims=True)
-    high, low = split(total)
-    left = dot(hid_ref[...], back_ref[0:W, :], NT)
-    right = dot(hid_ref[...], back_ref[W : 2 * W, :], NT)
-    proj = jnp.where(first_half(ALL, W), left, right)
-    lane = iota((ALL, W), 1)
-    tail = jnp.where(lane == LATER, high.astype(F32), low.astype(F32))
-    tail = jnp.where(lane < LATER + 2, tail, 0.0)
-    out_ref[...] = jnp.where(lane < LATER, proj, tail).astype(BF)
+
+    @pl.when(step == 0)
+    def _():
+        for lanes in range(0, full, 128):
+            at = 2 * ROWS * (lanes // 128)
+            cols = slice(lanes, lanes + 128)
+            grad_ref[:, cols] = got_ref[:, at : at + ROWS, :].reshape(ALL, 128)
+            hid_ref[:, cols] = got_ref[:, at + ROWS : at + 2 * ROWS, :].reshape(ALL, 128)
+        at = 2 * ROWS * (full // 128)
+        tail = got_ref[:, at : at + 16, :].astype(F32)
+        middle = tail[:, :, 32:64]
+        grad = jnp.concatenate([tail[:, :, 0:32], middle[:, 0:8]], axis=1)
+        hid = jnp.concatenate([middle[:, 8:16], tail[:, :, 64:96]], axis=1)
+        grad_ref[:, full:inner] = grad.astype(BF).reshape(ALL, 32)
+        hid_ref[:, full:] = jnp.zeros((ALL, hid_ref.shape[1] - full), BF)
+        hid_ref[:, full:inner] = hid.astype(BF).reshape(ALL, 32)
+        sum_ref[...] = jnp.zeros((ALL, 1), F32)
+
+    base = dot(grad_ref[...], down_ref[...], NT)
+    base = jnp.where(iota((ALL, 256), 1) < inner - 256 * step, base, 0.0)
+    base_ref[...] = base.astype(BF)
+    hid = hid_ref[:, pl.ds(pl.multiple_of(256 * step, 256), 256)].astype(F32)
+    sum_ref[...] += jnp.sum(hid * base, axis=1, keepdims=True)
+
+    @pl.when(step == 1)
+    def _():
+        left = dot(hid_ref[:, 0:inner], back_ref[0:W, :], NT)
+        right = dot(hid_ref[:, 0:inner], back_ref[W : 2 * W, :], NT)
+        out_ref[...] = jnp.where(first_half(ALL, W), left, right).astype(BF)
+
+    @pl.when(step == pl.num_programs(0) - 1)
+    def _():
+        high, low = split(sum_ref[...])
+        lane = iota((ALL, 128), 1) + 128
+        tail = jnp.where(lane == LATER, high.astype(F32), low.astype(F32))
+        tail = jnp.where(lane < LATER + 2, tail, 0.0)
+        proj = out_ref[:, 128:256].astype(F32)
+        out_ref[:, 128:256] = jnp.where(lane < LATER, proj, tail).astype(BF)
 
 
 def id_masks(ids_ref):
@@ -258,40 +275,51 @@
     part_ref[:, E : 2 * E] = second.astype(BF)
 
 
-def answer_kernel(got_ref, base_ref, back_ref, part_ref, out_ref):
-    width = base_ref.shape[1]
-    got = got_ref[...].astype(F32)
-    gate = got[:, LATER : LATER + 1] + got[:, LATER + 1 : LATER + 2]
-    coef = jnp.where(iota((ALL, W), 1) < LATER, got, 0.0)
-    half = first_half(ALL, W)
-    left = jnp.where(half, coef, 0.0).astype(BF)
-    right = jnp.where(half, 0.0, coef).astype(BF)
-    for start in range(0, width, 256):
-        cols = slice(start, min(start + 256, width))
-        moved = dot(left, back_ref[0:W, cols], NN) + dot(right, back_ref[W : 2 * W, cols], NN)
-        out_ref[:, cols] = (gate * base_ref[:, cols] + moved).astype(BF)
-    out_ref[:, width : width + 2 * E] = part_ref[...]
-    out_ref[:, width + 2 * E :] = jnp.zeros((ALL, out_ref.shape[1] - width - 2 * E), BF)
-
-
-def combine_kernel(got_ref, ids_ref, out_ref, router_ref):
-    pick = slots_by_rows(token_major(slot_codes(ids_ref)))
-    width = out_ref.shape[2]
-    for start in range(0, width, 256):
-        cols = slice(start, min(start + 256, width))
-        own = dot(pick, got_ref[:, cols], NN).astype(BF)
-        out_ref[:, :, cols] = own.reshape(N, K, cols.stop - start)
-    parts = got_ref[:, width : width + 2 * E].astype(F32).reshape(E, ROWS, 2 * E)
-    total = jnp.sum(parts, axis=0)
-    each = width // E
-    turn = iota((E, 2 * E), 1) - iota((E, 2 * E), 0)
-    flipped = [jnp.zeros((E, ROWS), F32)] * 2
-    for _ in range(3):
-        piece = total.astype(BF)
-        total = total - piece.astype(F32)
-        flipped = [flipped[q] + dot(one(turn == q * E), piece, NT) for q in range(2)]
-    router_ref[:, 0:ROWS] = flipped[0]
-    router_ref[:, ROWS:each] = flipped[1][:, 0 : each - ROWS]
+def answer_kernel(got_ref, base_ref, back_ref, part_ref, out_ref, left_ref, right_ref, gate_ref):
+    step = pl.program_id(0)
+
+    @pl.when(step == 0)
+    def _():
+        got = got_ref[...].astype(F32)
+        gate = got[:, LATER : LATER + 1] + got[:, LATER + 1 : LATER + 2]
+        gate_ref[...] = jnp.broadcast_to(gate, (ALL, W))
+        coef = jnp.where(iota((ALL, W), 1) < LATER, got, 0.0)
+        half = first_half(ALL, W)
+        left_ref[...] = jnp.where(half, coef, 0.0).astype(BF)
+        right_ref[...] = jnp.where(half, 0.0, coef).astype(BF)
+
+    moved = dot(left_ref[...], back_ref[0:W, :], NN) + dot(right_ref[...], back_ref[W : 2 * W, :], NN)
+    out_ref[...] = (gate_ref[...] * base_ref[...].astype(F32) + moved).astype(BF)
+
+    @pl.when(step == pl.num_programs(0) - 1)
+    def _():
+        out_ref[:, 160 : 160 + 2 * E] = part_ref[...]
+        out_ref[:, 160 + 2 * E :] = jnp.zeros((ALL, 96 - 2 * E), BF)
+
+
+def combine_kernel(got_ref, ids_ref, out_ref, router_ref, pick_ref):
+    step = pl.program_id(0)
+
+    @pl.when(step == 0)
+    def _():
+        pick_ref[...] = slots_by_rows(token_major(slot_codes(ids_ref)))
+
+    own = dot(pick_ref[...], got_ref[...], NN).astype(BF)
+    out_ref[...] = own.reshape(N, K, got_ref.shape[1])
+
+    @pl.when(step == pl.num_programs(0) - 1)
+    def _():
+        parts = got_ref[:, 160 : 160 + 2 * E].astype(F32).reshape(E, ROWS, 2 * E)
+        total = jnp.sum(parts, axis=0)
+        each = router_ref.shape[1]
+        turn = iota((E, 2 * E), 1) - iota((E, 2 * E), 0)
+        flipped = [jnp.zeros((E, ROWS), F32)] * 2
+        for _ in range(3):
+            piece = total.astype(BF)
+            total = total - piece.astype(F32)
+            flipped = [flipped[q] + dot(one(turn == q * E), piece, NT) for q in range(2)]
+        router_ref[:, 0:ROWS] = flipped[0]
+        router_ref[:, ROWS:each] = flipped[1][:, 0 : each - ROWS]
 
 
 def call(body, shapes, args, mib, smem=0, scratch=()):
@@ -302,6 +330,31 @@
         out_specs=[VM] * len(shapes),
         scratch_shapes=list(scratch),
         compiler_params=pltpu.CompilerParams(vmem_limit_bytes=mib << 20),
+    )(*args)
+
+
+def fixed(shape, once=False):
+    at = (0,) * len(shape)
+    if once:
+        return pl.BlockSpec(shape, lambda i: at, pipeline_mode=pl.Buffered(1))
+    return pl.BlockSpec(shape, lambda i: at)
+
+
+def along(shape, dim):
+    return pl.BlockSpec(shape, lambda i: tuple(i if d == dim else 0 for d in range(len(shape))))
+
+
+def looped(body, steps, shapes, ins, outs, args, mib, scratch):
+    return pl.pallas_call(
+        body,
+        grid=(steps,),
+        out_shape=[jax.ShapeDtypeStruct(s, d) for s, d in shapes],
+        in_specs=ins,
+        out_specs=outs,
+        scratch_shapes=[pltpu.VMEM(s, d) for s, d in scratch],
+        compiler_params=pltpu.CompilerParams(
+            vmem_limit_bytes=mib << 20, dimension_semantics=("arbitrary",)
+        ),
     )(*args)
 
 
@@ -321,11 +374,17 @@
     turned = routes.transpose(0, 2, 1)
     tall = 2 * ROWS * (inner // 128) + 16
 
-    (sent,) = call(
+    steps = pl.cdiv(inner, 256)
+
+    (sent,) = looped(
         dispatch_kernel,
+        steps,
         [((E, tall, 128), BF)],
+        [fixed((2, K, T)), along((N, K, 256), 2), along((N, 256), 1)],
+        [along((E, 4 * ROWS, 128), 1)],
         (turned, hidden[0].reshape(N, K, inner), grads),
         MIBS[0],
+        [((ALL, N * K), BF), ((ALL, N), BF)],
     )
     arrived = exchange(sent, "expert")
 
@@ -353,12 +412,19 @@
     scores = jnp.exp(chosen)
     gating = (scores / jnp.sum(scores, axis=2, keepdims=True)).reshape(N, K)
 
-    base, proj = call(
+    base, proj = looped(
         expert_kernel,
-        [((ALL, inner), F32), ((ALL, W), BF)],
+        steps,
+        [((ALL, 256 * steps), BF), ((ALL, W), BF)],
+        [
+            fixed((E, tall, 128), True),
+            along((256, width), 0),
+            fixed((2 * W, inner), True),
+        ],
+        [along((ALL, 256), 1), fixed((ALL, W))],
         (arrived, mats, back),
         MIBS[2],
-        scratch=[pltpu.VMEM((ALL, inner), BF)] * 2,
+        [((ALL, inner), BF), ((ALL, 256 * steps), BF), ((ALL, 1), F32)],
     )
     proj, gating = lax.optimization_barrier((proj, gating))
     returned = exchange(proj.reshape(E, ROWS, W), "expert").reshape(ALL, W)
@@ -368,11 +434,12 @@
         (returned, turned, id_all, gating),
         MIBS[3],
     )
+    blocks, where = lax.optimization_barrier((blocks, section.reshape(1)))
     gathered = exchange(blocks, "pipe")
     coef_sent, coef = call(
         solve_kernel,
         [((ALL, W), BF), ((N, W), BF)],
-        (section.reshape(1), gathered, turned, id_all, gating),
+        (where, gathered, turned, id_all, gating),
         MIBS[4],
         smem=1,
     )
@@ -383,13 +450,27 @@
         (coef, table_rows, grads, inputs.reshape(N, width)),
         MIBS[5],
     )
-    wide = 128 * pl.cdiv(inner + 2 * E, 128)
-    (answer,) = call(
-        answer_kernel, [((ALL, wide), BF)], (coef_got, base, back, parts), MIBS[6]
+    wide = 256 * steps
+    (answer,) = looped(
+        answer_kernel,
+        steps,
+        [((ALL, wide), BF)],
+        [fixed((ALL, W)), along((ALL, 256), 1), along((2 * W, 256), 1), fixed((ALL, 2 * E))],
+        [along((ALL, 256), 1)],
+        (coef_got, base, back, parts),
+        MIBS[6],
+        [((ALL, W), BF), ((ALL, W), BF), ((ALL, W), F32)],
     )
     answered = exchange(answer.reshape(E, ROWS, wide), "expert").reshape(ALL, wide)
-    hidden_grads, grad_router = call(
-        combine_kernel, [((N, K, inner), BF), ((E, width // E), F32)], (answered, turned), MIBS[7]
+    hidden_grads, grad_router = looped(
+        combine_kernel,
+        steps,
+        [((N, K, inner), BF), ((E, width // E), F32)],
+        [along((ALL, 256), 1), fixed((2, K, T))],
+        [along((N, K, 256), 2), fixed((E, width // E))],
+        (answered, turned),
+        MIBS[7],
+        [((N * K, ALL), BF)],
     )
     return (
         passed.reshape(1, 2, T, width),

time: 263 us -> 267 us (1.015)
  local copies, waits for them, and re-layouts: 29.3 us -> 5.31 us
  Pallas kernels: 23.3 us -> 41.7 us
  waiting for transfers between devices: 93.8 us -> 111 us
  blocking collectives: 84.1 us -> 72.8 us
  starting transfers between devices: 29.6 us -> 34.1 us
    pallas_call x0 -> x4, Pallas kernels: none -> 33.5 us  [looped(): pl.pallas_call(body, grid=(steps,), out_shape=[jax.ShapeDtypeStruct(s, d)...]
    unnamed x62 -> x18, local copies, waits for them, and re-layouts: 28.8 us -> 4.84 us
    pallas_call x8 -> x4, Pallas kernels: 23.3 us -> 8.16 us  [call(): pl.pallas_call(body, out_shape=[jax.ShapeDtypeStruct(s, d) for s, d in sh...]
    all_to_all x2, blocking collectives: 84.1 us -> 72.8 us  [exchange(): return lax.all_to_all(x, axis, split_axis=0, concat_axis=0, tiled=True)]
    all_to_all x3, waiting for transfers between devices: 80.1 us -> 90.8 us  [exchange(): return lax.all_to_all(x, axis, split_axis=0, concat_axis=0, tiled=True)]
    ppermute x7, waiting for transfers between devices: 13.8 us -> 20.2 us  [on_device(): lax.ppermute(own, 'pipe', [(i, i - by) for i in range(by, pipe)])]
    all_to_all x3, starting transfers between devices: 20.6 us -> 25.1 us  [exchange(): return lax.all_to_all(x, axis, split_axis=0, concat_axis=0, tiled=True)]
  transfers between devices with their start and end apart: 10 -> 10, of which waited for: 6 -> 9; matrix products, arithmetic and copies ran while one was open for 0% -> 0% of each run, Pallas kernels for 2% -> 2%
where the time goes in v1:
time: 267 us; the launch traced here: 266 us
  waiting for transfers between devices  111 us (42%)
  blocking collectives  72.8 us (27%)
  Pallas kernels  41.7 us (16%)
  starting transfers between devices  34.1 us (13%)
  local copies, waits for them, and re-layouts  5.31 us (2%)
    all_to_all x3, waiting for transfers between devices, exchange(): return lax.all_to_all(x, axis, split_axis=0, concat_axis=0, tiled=True)  90.8 us
    all_to_all x2, blocking collectives, exchange(): return lax.all_to_all(x, axis, split_axis=0, concat_axis=0, tiled=True)  72.8 us
    pallas_call x4, Pallas kernels, looped(): pl.pallas_call(body, grid=(steps,), out_shape=[jax.ShapeDtypeStruct(s, d)...  33.5 us
    all_to_all x3, starting transfers between devices, exchange(): return lax.all_to_all(x, axis, split_axis=0, concat_axis=0, tiled=True)  25.1 us
    ppermute x7, waiting for transfers between devices, on_device(): lax.ppermute(own, 'pipe', [(i, i - by) for i in range(by, pipe)])  20.2 us
    ppermute x7, starting transfers between devices, on_device(): lax.ppermute(own, 'pipe', [(i, i - by) for i in range(by, pipe)])  9.03 us
    pallas_call x4, Pallas kernels, call(): pl.pallas_call(body, out_shape=[jax.ShapeDtypeStruct(s, d) for s, d in sh...  8.16 us
  transfers between devices with their start and end apart: 10, of which 9 were waited for; matrix products, arithmetic and copies ran while one was open for 0% of the time, Pallas kernels for 2%

profile of v1, /device:TPU:32, one launch (start us, length us, event | category | flops | bytes accessed | tf_op | source)
XLA Modules:
  0.0 266.3 jit_solution(6606186576414343512)
XLA Ops:
  0.6 7.4 %shard_map.94 = bf16[32,544,128]{2,1,0:T(8,128)(2,1)} custom-call(s32[2,4,64]{2,1,0:T(4,128)} %bitcast.51, bf16[128,4,1440]{2,1,0:T(4,128)(2,1)} %bitcast.58, bf16[128,1440]{1,0:T(8,128)(2,1)} %bitcast.49), custom_call_target="tpu_custom_call" | custom-call | tf_op jit(solution)/shard_map/pallas_call | solution.py:348
  8.0 0.0 copy-start.2
  8.0 11.4 %all-to-all-start = ((bf16[32,544,128]{2,1,0:T(8,128)(2,1)}), bf16[32,544,128]{2,1,0:T(8,128)(2,1)}, u32[]{:S(2)}, u32[]{:S(2)}) async-start(bf16[32,544,128]{2,1,0:T(8,128)(2,1)} %shard_map.94), calls=%async_computation | async-start | bytes 8912896 | tf_op jit(solution)/shard_map/all_to_all | solution.py:362
  19.4 0.0 copy-done.5
  19.4 0.1 convert_element_type.13
  19.5 0.0 copy-done.8
  19.5 0.1 broadcast_in_dim.64
  19.6 0.1 broadcast_in_dim.65
  19.7 0.0 copy-done.7
  19.7 0.1 bitcast_select_fusion
  19.9 1.3 collective-permute-start
  21.1 1.3 collective-permute-start.1
  22.4 1.3 collective-permute-start.2
  23.8 1.3 collective-permute-start.3
  25.1 1.3 collective-permute-start.4
  26.4 0.0 copy-done.2
  26.4 0.3 convolution_bitcast_fusion
  26.7 0.1 copy.16
  26.8 0.1 div.11
  26.9 0.0 collective-permute-done.refs_0_
  26.9 1.3 collective-permute-start.5
  28.2 4.3 %collective-permute-done.1.refs_1_ = bf16[72,1440]{1,0:T(8,128)(2,1)S(1)} collective-permute-done((bf16[72,1440]{1,0:T(8,128)(2,1)S(1)}, bf16[72,1440]{1,0:T(8,128)(2,1)S(1)}, u32[]{:S(2)}, u32[]{:S(2)}) %collective-permute-start.1) | collective-permute-done | bytes 207392 | tf_op jit(solution)/shard_map/ppermute | solution.py:399
  32.5 1.3 collective-permute-start.6
  33.7 0.1 bitcast_divide_fusion.gate_ref
  33.8 0.5 collective-permute-done.2.refs_2_
  34.4 5.3 %collective-permute-done.3.refs_3_ = bf16[72,1440]{1,0:T(8,128)(2,1)S(1)} collective-permute-done((bf16[72,1440]{1,0:T(8,128)(2,1)S(1)}, bf16[72,1440]{1,0:T(8,128)(2,1)S(1)}, u32[]{:S(2)}, u32[]{:S(2)}) %collective-permute-start.3) | collective-permute-done | bytes 207392 | tf_op jit(solution)/shard_map/ppermute | solution.py:399
  39.6 0.7 collective-permute-done.4.refs_4_
  40.4 9.3 %collective-permute-done.5.refs_5_ = bf16[72,1440]{1,0:T(8,128)(2,1)S(1)} collective-permute-done((bf16[72,1440]{1,0:T(8,128)(2,1)S(1)}, bf16[72,1440]{1,0:T(8,128)(2,1)S(1)}, u32[]{:S(2)}, u32[]{:S(2)}) %collective-permute-start.5) | collective-permute-done | bytes 207392 | tf_op jit(solution)/shard_map/ppermute | solution.py:399
  49.6 0.1 collective-permute-done.6.refs_6_
  49.7 2.3 copy-done
  52.0 2.6 shard_map.95
  54.7 0.0 copy-start.1
  54.7 1.1 copy-done.1
  55.8 64.0 %all-to-all-done.got_ref = bf16[32,544,128]{2,1,0:T(8,128)(2,1)} async-done(((bf16[32,544,128]{2,1,0:T(8,128)(2,1)}), bf16[32,544,128]{2,1,0:T(8,128)(2,1)}, u32[]{:S(2)}, u32[]{:S(2)}) %all-to-all-start) | async-done | bytes 4456480 | tf_op jit(solution)/shard_map/all_to_all | solution.py:362
  119.8 12.4 %shard_map.96 = (bf16[768,1536]{1,0:T(8,128)(2,1)}, bf16[768,256]{1,0:T(8,128)(2,1)}) custom-call(bf16[32,544,128]{2,1,0:T(8,128)(2,1)} %all-to-all-done.got_ref, bf16[1440,1440]{1,0:T(8,128)(2,1)} %bitcast.45, bf16[512,1440]{1,0:T(8,128)(2,1)} %copy-done.1), custom_call_target="tpu_custom_call" | custom-call | tf_op jit(solution)/shard_map/pallas_call | solution.py:348
  132.3 8.9 %all-to-all-start.1 = ((bf16[32,24,256]{2,1,0:T(8,128)(2,1)}), bf16[32,24,256]{2,1,0:T(8,128)(2,1)S(1)}, u32[]{:S(2)}, u32[]{:S(2)}) async-start(bf16[32,24,256]{2,1,0:T(8,128)(2,1)} %bitcast.60), calls=%async_computation.1 | async-start | bytes 786432 | tf_op jit(solution)/shard_map/all_to_all | solution.py:362
  141.2 14.8 %all-to-all-done.1 = bf16[32,24,256]{2,1,0:T(8,128)(2,1)S(1)} async-done(((bf16[32,24,256]{2,1,0:T(8,128)(2,1)}), bf16[32,24,256]{2,1,0:T(8,128)(2,1)S(1)}, u32[]{:S(2)}, u32[]{:S(2)}) %all-to-all-start.1) | async-done | bytes 393248 | tf_op jit(solution)/shard_map/all_to_all | solution.py:362
  156.0 1.6 shard_map.97
  157.6 11.8 %all_to_all.25.got_ref = bf16[8,8,2048]{2,1,0:T(8,128)(2,1)S(1)} all-to-all(bf16[8,8,2048]{2,1,0:T(8,128)(2,1)S(1)} %shard_map.97), channel_id=1, replica_groups=mesh['pipe'=8,'expert'=32] {'pipe'}, dimensions={0} | all-to-all | bytes 524288 | tf_op jit(solution)/shard_map/all_to_all | solution.py:362
  169.4 2.0 shard_map.98
  171.3 4.8 %all-to-all-start.3 = ((bf16[32,24,256]{2,1,0:T(8,128)(2,1)}), bf16[32,24,256]{2,1,0:T(8,128)(2,1)S(1)}, u32[]{:S(2)}, u32[]{:S(2)}) async-start(bf16[32,24,256]{2,1,0:T(8,128)(2,1)} %bitcast.21), calls=%async_computation.3 | async-start | bytes 786432 | tf_op jit(solution)/shard_map/all_to_all | solution.py:362
  176.1 2.0 shard_map.99
  178.1 0.7 copy-done.4
  178.8 11.9 %all-to-all-done.3 = bf16[32,24,256]{2,1,0:T(8,128)(2,1)S(1)} async-done(((bf16[32,24,256]{2,1,0:T(8,128)(2,1)}), bf16[32,24,256]{2,1,0:T(8,128)(2,1)S(1)}, u32[]{:S(2)}, u32[]{:S(2)}) %all-to-all-start.3) | async-done | bytes 393248 | tf_op jit(solution)/shard_map/all_to_all | solution.py:362
  190.7 0.8 copy-done.6
  191.5 6.9 %shard_map.100 = bf16[768,1536]{1,0:T(8,128)(2,1)} custom-call(bf16[768,256]{1,0:T(8,128)(2,1)} %bitcast.59, bf16[768,1536]{1,0:T(8,128)(2,1)} %get-tuple-element.29.base_ref, bf16[512,1440]{1,0:T(8,128)(2,1)} %copy-done.1, bf16[768,64]{1,0:T(8,128)(2,1)} %copy-done.4), custom_call_target="tpu_custom_call" | custom-call | tf_op jit(solution)/shard_map/pallas_call | solution.py:348
  198.4 61.0 %all_to_all.26 = bf16[32,24,1536]{2,1,0:T(8,128)(2,1)} all-to-all(bf16[32,24,1536]{2,1,0:T(8,128)(2,1)} %bitcast.56), channel_id=1, replica_groups=mesh['pipe'=8,'expert'=32] {'expert'}, dimensions={0} | all-to-all | bytes 4718592 | tf_op jit(solution)/shard_map/all_to_all | solution.py:362
  259.5 6.8 %shard_map.101 = (bf16[128,4,1440]{2,1,0:T(4,128)(2,1)}, f32[32,45]{1,0:T(8,128)}) custom-call(bf16[768,1536]{1,0:T(8,128)(2,1)} %bitcast.57, s32[2,4,64]{2,1,0:T(4,128)} %bitcast.52), custom_call_target="tpu_custom_call" | custom-call | tf_op jit(solution)/shard_map/pallas_call | solution.py:348
  (15 shorter events, 0.1 us)
Async XLA Ops:
  8.0 11.4 %copy-start.5 = (s32[1,2,64,4]{2,3,1,0:T(4,128)S(1)}, s32[1,2,64,4]{2,3,1,0:T(4,128)}, u32[]{:S(2)}) copy-start(s32[1,2,64,4]{2,3,1,0:T(4,128)} %param.9) | copy-start | bytes 6148
  8.0 11.5 %copy-start.8 = (s32[1,2]{1,0:T(1,128)S(1)}, s32[1,2]{1,0:T(1,128)}, u32[]{:S(2)}) copy-start(s32[1,2]{1,0:T(1,128)} %param.10) | copy-start | bytes 28
  8.0 11.7 %copy-start.7 = (bf16[1,2,1440,32]{2,3,1,0:T(8,128)(2,1)S(1)}, bf16[1,2,1440,32]{2,3,1,0:T(8,128)(2,1)}, u32[]{:S(2)}) copy-start(bf16[1,2,1440,32]{2,3,1,0:T(8,128)(2,1)} %param.11) | copy-start | bytes 552964
  8.0 18.3 %copy-start.2 = (bf16[1,2,64,1440]{3,2,1,0:T(8,128)(2,1)S(1)}, bf16[1,2,64,1440]{3,2,1,0:T(8,128)(2,1)}, u32[]{:S(2)}) copy-start(bf16[1,2,64,1440]{3,2,1,0:T(8,128)(2,1)} %param.7) | copy-start | bytes 1105924
  8.0 111.8 %all-to-all-start = ((bf16[32,544,128]{2,1,0:T(8,128)(2,1)}), bf16[32,544,128]{2,1,0:T(8,128)(2,1)}, u32[]{:S(2)}, u32[]{:S(2)}) async-start(bf16[32,544,128]{2,1,0:T(8,128)(2,1)} %shard_map.94), calls=%async_computation | async-start | bytes 8912896 | tf_op jit(solution)/shard_map/all_to_all | solution.py:362
  19.9 7.1 %collective-permute-start = (bf16[72,1440]{1,0:T(8,128)(2,1)S(1)}, bf16[72,1440]{1,0:T(8,128)(2,1)S(1)}, u32[]{:S(2)}, u32[]{:S(2)}) collective-permute-start(bf16[72,1440]{1,0:T(8,128)(2,1)S(1)} %fusion.2.refs_7_), channel_id=1, source_target_pairs={{32,0},{64,32},{96,64},{128,96},{160,128},{192,160},{224,192},{33,... | collective-permute-start | bytes 622088 | tf_op jit(solution)/shard_map/ppermute | solution.py:399
  21.1 11.3 %collective-permute-start.1 = (bf16[72,1440]{1,0:T(8,128)(2,1)S(1)}, bf16[72,1440]{1,0:T(8,128)(2,1)S(1)}, u32[]{:S(2)}, u32[]{:S(2)}) collective-permute-start(bf16[72,1440]{1,0:T(8,128)(2,1)S(1)} %fusion.2.refs_7_), channel_id=1, source_target_pairs={{64,0},{96,32},{128,64},{160,96},{192,128},{224,160},{65,1},{97,33... | collective-permute-start | bytes 622088 | tf_op jit(solution)/shard_map/ppermute | solution.py:399
  22.4 11.9 %collective-permute-start.2 = (bf16[72,1440]{1,0:T(8,128)(2,1)S(1)}, bf16[72,1440]{1,0:T(8,128)(2,1)S(1)}, u32[]{:S(2)}, u32[]{:S(2)}) collective-permute-start(bf16[72,1440]{1,0:T(8,128)(2,1)S(1)} %fusion.2.refs_7_), channel_id=1, source_target_pairs={{96,0},{128,32},{160,64},{192,96},{224,128},{97,1},{129,33},{161,6... | collective-permute-start | bytes 622088 | tf_op jit(solution)/shard_map/ppermute | solution.py:399
  23.8 15.9 %collective-permute-start.3 = (bf16[72,1440]{1,0:T(8,128)(2,1)S(1)}, bf16[72,1440]{1,0:T(8,128)(2,1)S(1)}, u32[]{:S(2)}, u32[]{:S(2)}) collective-permute-start(bf16[72,1440]{1,0:T(8,128)(2,1)S(1)} %fusion.2.refs_7_), channel_id=1, source_target_pairs={{128,0},{160,32},{192,64},{224,96},{129,1},{161,33},{193,65},{225,... | collective-permute-start | bytes 622088 | tf_op jit(solution)/shard_map/ppermute | solution.py:399
  25.1 15.3 %collective-permute-start.4 = (bf16[72,1440]{1,0:T(8,128)(2,1)S(1)}, bf16[72,1440]{1,0:T(8,128)(2,1)S(1)}, u32[]{:S(2)}, u32[]{:S(2)}) collective-permute-start(bf16[72,1440]{1,0:T(8,128)(2,1)S(1)} %fusion.2.refs_7_), channel_id=1, source_target_pairs={{160,0},{192,32},{224,64},{161,1},{193,33},{225,65},{162,2},{194,3... | collective-permute-start | bytes 622088 | tf_op jit(solution)/shard_map/ppermute | solution.py:399
  26.9 22.7 %collective-permute-start.5 = (bf16[72,1440]{1,0:T(8,128)(2,1)S(1)}, bf16[72,1440]{1,0:T(8,128)(2,1)S(1)}, u32[]{:S(2)}, u32[]{:S(2)}) collective-permute-start(bf16[72,1440]{1,0:T(8,128)(2,1)S(1)} %fusion.2.refs_7_), channel_id=1, source_target_pairs={{192,0},{224,32},{193,1},{225,33},{194,2},{226,34},{195,3},{227,35... | collective-permute-start | bytes 622088 | tf_op jit(solution)/shard_map/ppermute | solution.py:399
  32.5 17.3 %collective-permute-start.6 = (bf16[72,1440]{1,0:T(8,128)(2,1)S(1)}, bf16[72,1440]{1,0:T(8,128)(2,1)S(1)}, u32[]{:S(2)}, u32[]{:S(2)}) collective-permute-start(bf16[72,1440]{1,0:T(8,128)(2,1)S(1)} %fusion.2.refs_7_), channel_id=1, source_target_pairs={{224,0},{225,1},{226,2},{227,3},{228,4},{229,5},{230,6},{231,7},{2... | collective-permute-start | bytes 622088 | tf_op jit(solution)/shard_map/ppermute | solution.py:399
  49.7 2.3 copy-start
  54.7 1.1 copy-start.1
  132.3 43.9 %copy-start.3 = (bf16[2,64,1440]{2,1,0:T(8,128)(2,1)S(1)}, bf16[2,64,1440]{2,1,0:T(8,128)(2,1)}, u32[]{:S(2)}) copy-start(bf16[2,64,1440]{2,1,0:T(8,128)(2,1)} %param.13) | copy-start | bytes 1105924
  132.3 23.8 %all-to-all-start.1 = ((bf16[32,24,256]{2,1,0:T(8,128)(2,1)}), bf16[32,24,256]{2,1,0:T(8,128)(2,1)S(1)}, u32[]{:S(2)}, u32[]{:S(2)}) async-start(bf16[32,24,256]{2,1,0:T(8,128)(2,1)} %bitcast.60), calls=%async_computation.1 | async-start | bytes 786432 | tf_op jit(solution)/shard_map/all_to_all | solution.py:362
  171.3 19.4 %all-to-all-start.3 = ((bf16[32,24,256]{2,1,0:T(8,128)(2,1)}), bf16[32,24,256]{2,1,0:T(8,128)(2,1)S(1)}, u32[]{:S(2)}, u32[]{:S(2)}) async-start(bf16[32,24,256]{2,1,0:T(8,128)(2,1)} %bitcast.21), calls=%async_computation.3 | async-start | bytes 786432 | tf_op jit(solution)/shard_map/all_to_all | solution.py:362
  178.1 0.7 copy-start.4
  190.7 0.8 copy-start.6

commit v2 on v0

--- a/solution.py
+++ b/solution.py
@@ -14,13 +14,14 @@
 NT = (((1,), (1,)), ((), ()))
 TN = (((0,), (0,)), ((), ()))
 VM = pl.BlockSpec(memory_space=pltpu.VMEM)
+HB = pl.BlockSpec(memory_space=pltpu.HBM)
 SM = pl.BlockSpec(memory_space=pltpu.SMEM)
 
 N, T, K, E, HALF = 128, 64, 4, 32, 12
 ROWS = 2 * HALF
 ALL = E * ROWS
 W = 256
-MIBS = (20, 20, 32, 12, 12, 20, 24, 20)
+MIBS = (62, 20, 62, 12, 12, 20, 62, 20)
 LATER = 224
 
 
@@ -86,16 +87,26 @@
     return (row - ROWS * divided(row, ROWS)) < HALF
 
 
-def dispatch_kernel(ids_ref, hid_ref, grad_ref, out_ref):
+def dispatch_kernel(ids_ref, hid_hbm, grad_hbm, out_hbm, hid_ref, grad_ref, out_ref, sems):
+    loads = [
+        pltpu.make_async_copy(grad_hbm, grad_ref, sems.at[0]),
+        pltpu.make_async_copy(hid_hbm, hid_ref, sems.at[1]),
+    ]
+    for load in loads:
+        load.start()
     codes = slot_codes(ids_ref)
+    tokens = rows_by_slots(functools.reduce(jnp.maximum, codes))
     pick = rows_by_slots(token_major(codes))
-    tokens = rows_by_slots(functools.reduce(jnp.maximum, codes))
+    for load in loads:
+        load.wait()
     width = grad_ref.shape[1]
+    stores = []
     for start in range(0, width, 256):
         cols = slice(start, min(start + 256, width))
         size = cols.stop - start
         grad = dot(tokens, grad_ref[:, cols], NN)
         hid = dot(pick, hid_ref[:, :, cols].reshape(N * K, size), NN)
+        first = 2 * ROWS * (start // 128)
         for lanes in range(0, size, 128):
             at = 2 * ROWS * ((start + lanes) // 128)
             cut = min(lanes + 128, size)
@@ -104,6 +115,7 @@
             if cut - lanes == 128:
                 out_ref[:, at : at + ROWS, :] = left.astype(BF)
                 out_ref[:, at + ROWS : at + 2 * ROWS, :] = right.astype(BF)
+                last = at + 2 * ROWS
             else:
                 tail = [
                     left[:, 0:16],
@@ -112,6 +124,15 @@
                     jnp.zeros((E, 16, 32), F32),
                 ]
                 out_ref[:, at : at + 16, :] = jnp.concatenate(tail, axis=2).astype(BF)
+                last = at + 16
+        part = pl.ds(first, last - first)
+        store = pltpu.make_async_copy(
+            out_ref.at[:, part, :], out_hbm.at[:, part, :], sems.at[2 + len(stores)]
+        )
+        store.start()
+        stores.append(store)
+    for store in stores:
+        store.wait()
 
 
 def tables_kernel(*refs):
@@ -129,8 +150,27 @@
         ).astype(BF)
 
 
-def expert_kernel(got_ref, down_ref, back_ref, base_ref, out_ref, grad_ref, hid_ref):
+def expert_kernel(
+    got_hbm, down_hbm, back_hbm, base_hbm, out_ref,
+    got_ref, down_ref, back_ref, base_ref, grad_ref, hid_ref, sems,
+):
     inner = down_ref.shape[0]
+    starts = range(0, inner, 256)
+    load = pltpu.make_async_copy(got_hbm, got_ref, sems.at[0])
+    load.start()
+    mats = []
+    for start in starts:
+        rows = pl.ds(start, min(256, inner - start))
+        mats.append(
+            pltpu.make_async_copy(
+                down_hbm.at[rows, :], down_ref.at[rows, :], sems.at[2 + len(mats)]
+            )
+        )
+    for copy in mats:
+        copy.start()
+    backs = pltpu.make_async_copy(back_hbm, back_ref, sems.at[1])
+    backs.start()
+    load.wait()
     full = 128 * (inner // 128)
     for lanes in range(0, full, 128):
         at = 2 * ROWS * (lanes // 128)
@@ -145,12 +185,21 @@
     grad_ref[:, full:inner] = grad.astype(BF).reshape(ALL, 32)
     hid_ref[:, full:inner] = hid.astype(BF).reshape(ALL, 32)
     total = jnp.zeros((ALL, 1), F32)
-    for start in range(0, inner, 256):
+    stores = []
+    for c, start in enumerate(starts):
         cols = slice(start, min(start + 256, inner))
+        size = cols.stop - start
+        mats[c].wait()
         base = dot(grad_ref[...], down_ref[cols, :], NT)
-        base_ref[:, cols] = base
+        base_ref[c, :, 0:size] = base.astype(BF)
+        if size < 256:
+            base_ref[c, :, size:] = jnp.zeros((ALL, 256 - size), BF)
+        store = pltpu.make_async_copy(base_ref.at[c], base_hbm.at[c], sems.at[2 + len(mats) + c])
+        store.start()
+        stores.append(store)
         total = total + jnp.sum(hid_ref[:, cols].astype(F32) * base, axis=1, keepdims=True)
     high, low = split(total)
+    backs.wait()
     left = dot(hid_ref[...], back_ref[0:W, :], NT)
     right = dot(hid_ref[...], back_ref[W : 2 * W, :], NT)
     proj = jnp.where(first_half(ALL, W), left, right)
@@ -158,6 +207,8 @@
     tail = jnp.where(lane == LATER, high.astype(F32), low.astype(F32))
     tail = jnp.where(lane < LATER + 2, tail, 0.0)
     out_ref[...] = jnp.where(lane < LATER, proj, tail).astype(BF)
+    for store in stores:
+        store.wait()
 
 
 def id_masks(ids_ref):
@@ -258,30 +309,61 @@
     part_ref[:, E : 2 * E] = second.astype(BF)
 
 
-def answer_kernel(got_ref, base_ref, back_ref, part_ref, out_ref):
-    width = base_ref.shape[1]
+def answer_kernel(got_ref, base_hbm, back_hbm, part_ref, out_hbm, base_ref, back_ref, out_ref, sems):
+    width = back_ref.shape[1]
+    count = base_ref.shape[0]
+    backs = pltpu.make_async_copy(back_hbm, back_ref, sems.at[0])
+    backs.start()
+    loads = []
+    for c in range(count):
+        load = pltpu.make_async_copy(base_hbm.at[c], base_ref.at[c], sems.at[1 + c])
+        load.start()
+        loads.append(load)
     got = got_ref[...].astype(F32)
     gate = got[:, LATER : LATER + 1] + got[:, LATER + 1 : LATER + 2]
     coef = jnp.where(iota((ALL, W), 1) < LATER, got, 0.0)
     half = first_half(ALL, W)
     left = jnp.where(half, coef, 0.0).astype(BF)
     right = jnp.where(half, 0.0, coef).astype(BF)
-    for start in range(0, width, 256):
-        cols = slice(start, min(start + 256, width))
+    backs.wait()
+    stores = []
+    for c in range(count):
+        cols = slice(256 * c, min(256 * c + 256, width))
         moved = dot(left, back_ref[0:W, cols], NN) + dot(right, back_ref[W : 2 * W, cols], NN)
-        out_ref[:, cols] = (gate * base_ref[:, cols] + moved).astype(BF)
-    out_ref[:, width : width + 2 * E] = part_ref[...]
-    out_ref[:, width + 2 * E :] = jnp.zeros((ALL, out_ref.shape[1] - width - 2 * E), BF)
+        loads[c].wait()
+        base = base_ref[c, :, 0 : cols.stop - cols.start].astype(F32)
+        value = gate * base + moved
+        if c == count - 1:
+            spare = jnp.zeros((ALL, 96 - 2 * E), F32)
+            value = jnp.concatenate([value, part_ref[...].astype(F32), spare], axis=1)
+        for half_at in range(2):
+            tile = value[:, 128 * half_at : 128 * half_at + 128].astype(BF)
+            at = ROWS * (2 * c + half_at)
+            out_ref[:, at : at + ROWS, :] = tile.reshape(E, ROWS, 128)
+        part = pl.ds(2 * ROWS * c, 2 * ROWS)
+        store = pltpu.make_async_copy(
+            out_ref.at[:, part, :], out_hbm.at[:, part, :], sems.at[1 + count + c]
+        )
+        store.start()
+        stores.append(store)
+    for store in stores:
+        store.wait()
 
 
 def combine_kernel(got_ref, ids_ref, out_ref, router_ref):
     pick = slots_by_rows(token_major(slot_codes(ids_ref)))
     width = out_ref.shape[2]
+
+    def tile(t):
+        return got_ref[:, ROWS * t : ROWS * t + ROWS, :].reshape(ALL, 128)
+
     for start in range(0, width, 256):
         cols = slice(start, min(start + 256, width))
-        own = dot(pick, got_ref[:, cols], NN).astype(BF)
+        t = start // 128
+        both = jnp.concatenate([tile(t), tile(t + 1)], axis=1)
+        own = dot(pick, both, NN).astype(BF)[:, 0 : cols.stop - start]
         out_ref[:, :, cols] = own.reshape(N, K, cols.stop - start)
-    parts = got_ref[:, width : width + 2 * E].astype(F32).reshape(E, ROWS, 2 * E)
+    parts = tile(width // 128).astype(F32)[:, 32 : 32 + 2 * E].reshape(E, ROWS, 2 * E)
     total = jnp.sum(parts, axis=0)
     each = width // E
     turn = iota((E, 2 * E), 1) - iota((E, 2 * E), 0)
@@ -294,13 +376,18 @@
     router_ref[:, ROWS:each] = flipped[1][:, 0 : each - ROWS]
 
 
-def call(body, shapes, args, mib, smem=0, scratch=()):
+def call(body, shapes, args, mib, smem=0, scratch=(), sems=0, far=(), far_out=()):
+    ins = [SM] * smem + [VM] * (len(args) - smem)
+    ins = [HB if i in far else spec for i, spec in enumerate(ins)]
+    held = [pltpu.VMEM(s, d) for s, d in scratch]
+    if sems:
+        held.append(pltpu.SemaphoreType.DMA((sems,)))
     return pl.pallas_call(
         body,
         out_shape=[jax.ShapeDtypeStruct(s, d) for s, d in shapes],
-        in_specs=[SM] * smem + [VM] * (len(args) - smem),
-        out_specs=[VM] * len(shapes),
-        scratch_shapes=list(scratch),
+        in_specs=ins,
+        out_specs=[HB if i in far_out else VM for i in range(len(shapes))],
+        scratch_shapes=held,
         compiler_params=pltpu.CompilerParams(vmem_limit_bytes=mib << 20),
     )(*args)
 
@@ -321,11 +408,17 @@
     turned = routes.transpose(0, 2, 1)
     tall = 2 * ROWS * (inner // 128) + 16
 
+    steps = pl.cdiv(inner, 256)
+
     (sent,) = call(
         dispatch_kernel,
         [((E, tall, 128), BF)],
         (turned, hidden[0].reshape(N, K, inner), grads),
         MIBS[0],
+        scratch=[((N, K, inner), BF), ((N, width), BF), ((E, tall, 128), BF)],
+        sems=2 + steps,
+        far=(1, 2),
+        far_out=(0,),
     )
     arrived = exchange(sent, "expert")
 
@@ -355,10 +448,20 @@
 
     base, proj = call(
         expert_kernel,
-        [((ALL, inner), F32), ((ALL, W), BF)],
+        [((steps, ALL, 256), BF), ((ALL, W), BF)],
         (arrived, mats, back),
         MIBS[2],
-        scratch=[pltpu.VMEM((ALL, inner), BF)] * 2,
+        scratch=[
+            ((E, tall, 128), BF),
+            ((inner, width), BF),
+            ((2 * W, inner), BF),
+            ((steps, ALL, 256), BF),
+            ((ALL, width), BF),
+            ((ALL, inner), BF),
+        ],
+        sems=2 + 2 * steps,
+        far=(0, 1, 2),
+        far_out=(0,),
     )
     proj, gating = lax.optimization_barrier((proj, gating))
     returned = exchange(proj.reshape(E, ROWS, W), "expert").reshape(ALL, W)
@@ -368,11 +471,12 @@
         (returned, turned, id_all, gating),
         MIBS[3],
     )
+    blocks, where = lax.optimization_barrier((blocks, section.reshape(1)))
     gathered = exchange(blocks, "pipe")
     coef_sent, coef = call(
         solve_kernel,
         [((ALL, W), BF), ((N, W), BF)],
-        (section.reshape(1), gathered, turned, id_all, gating),
+        (where, gathered, turned, id_all, gating),
         MIBS[4],
         smem=1,
     )
@@ -383,11 +487,18 @@
         (coef, table_rows, grads, inputs.reshape(N, width)),
         MIBS[5],
     )
-    wide = 128 * pl.cdiv(inner + 2 * E, 128)
+    back_tall = 2 * ROWS * steps
     (answer,) = call(
-        answer_kernel, [((ALL, wide), BF)], (coef_got, base, back, parts), MIBS[6]
-    )
-    answered = exchange(answer.reshape(E, ROWS, wide), "expert").reshape(ALL, wide)
+        answer_kernel,
+        [((E, back_tall, 128), BF)],
+        (coef_got, base, back, parts),
+        MIBS[6],
+        scratch=[((steps, ALL, 256), BF), ((2 * W, inner), BF), ((E, back_tall, 128), BF)],
+        sems=1 + 2 * steps,
+        far=(1, 2),
+        far_out=(0,),
+    )
+    answered = exchange(answer, "expert")
     hidden_grads, grad_router = call(
         combine_kernel, [((N, K, inner), BF), ((E, width // E), F32)], (answered, turned), MIBS[7]
     )

time: 263 us -> 265 us (level)
  local copies, waits for them, and re-layouts: 29.3 us -> 6.56 us
  waiting for transfers between devices: 93.8 us -> 111 us
  Pallas kernels: 23.3 us -> 38.7 us
  blocking collectives: 84.1 us -> 72.8 us
  starting transfers between devices: 29.6 us -> 34.1 us
    unnamed x62 -> x24, local copies, waits for them, and re-layouts: 28.8 us -> 6.1 us
    pallas_call x8, Pallas kernels: 23.3 us -> 38.7 us  [call(): pl.pallas_call(body, out_shape=[jax.ShapeDtypeStruct(s, d) for s, d in sh...]
    all_to_all x2, blocking collectives: 84.1 us -> 72.8 us  [exchange(): return lax.all_to_all(x, axis, split_axis=0, concat_axis=0, tiled=True)]
    all_to_all x3, waiting for transfers between devices: 80.1 us -> 90.4 us  [exchange(): return lax.all_to_all(x, axis, split_axis=0, concat_axis=0, tiled=True)]
    ppermute x7, waiting for transfers between devices: 13.8 us -> 20.2 us  [on_device(): lax.ppermute(own, 'pipe', [(i, i - by) for i in range(by, pipe)])]
    all_to_all x3, starting transfers between devices: 20.6 us -> 25.1 us  [exchange(): return lax.all_to_all(x, axis, split_axis=0, concat_axis=0, tiled=True)]
  transfers between devices with their start and end apart: 10 -> 10, of which waited for: 6 -> 9; matrix products, arithmetic and copies ran while one was open for 0% -> 0% of each run, Pallas kernels for 2% -> 2%
where the time goes in v2:
time: 265 us; the launch traced here: 264 us
  waiting for transfers between devices  111 us (42%)
  blocking collectives  72.8 us (27%)
  Pallas kernels  38.7 us (15%)
  starting transfers between devices  34.1 us (13%)
  local copies, waits for them, and re-layouts  6.56 us (2%)
    all_to_all x3, waiting for transfers between devices, exchange(): return lax.all_to_all(x, axis, split_axis=0, concat_axis=0, tiled=True)  90.4 us
    all_to_all x2, blocking collectives, exchange(): return lax.all_to_all(x, axis, split_axis=0, concat_axis=0, tiled=True)  72.8 us
    pallas_call x8, Pallas kernels, call(): pl.pallas_call(body, out_shape=[jax.ShapeDtypeStruct(s, d) for s, d in sh...  38.7 us
    all_to_all x3, starting transfers between devices, exchange(): return lax.all_to_all(x, axis, split_axis=0, concat_axis=0, tiled=True)  25.1 us
    ppermute x7, waiting for transfers between devices, on_device(): lax.ppermute(own, 'pipe', [(i, i - by) for i in range(by, pipe)])  20.2 us
    ppermute x7, starting transfers between devices, on_device(): lax.ppermute(own, 'pipe', [(i, i - by) for i in range(by, pipe)])  9.03 us
    unnamed x24, local copies, waits for them, and re-layouts  6.1 us
  transfers between devices with their start and end apart: 10, of which 9 were waited for; matrix products, arithmetic and copies ran while one was open for 0% of the time, Pallas kernels for 2%

profile of v2, /device:TPU:32, one launch (start us, length us, event | category | flops | bytes accessed | tf_op | source)
XLA Modules:
  0.0 264.1 jit_solution(15021247855295293801)
XLA Ops:
  0.6 5.6 %shard_map.94 = bf16[32,544,128]{2,1,0:T(8,128)(2,1)} custom-call(s32[2,4,64]{2,1,0:T(4,128)} %bitcast.49, bf16[128,4,1440]{2,1,0:T(4,128)(2,1)} %bitcast.54, bf16[128,1440]{1,0:T(8,128)(2,1)} %bitcast.47), custom_call_target="tpu_custom_call" | custom-call | tf_op jit(solution)/shard_map/pallas_call | solution.py:385
  6.3 0.0 copy-start.5
  6.3 0.0 copy-start.11
  6.3 0.0 copy-start.2
  6.3 11.4 %all-to-all-start = ((bf16[32,544,128]{2,1,0:T(8,128)(2,1)}), bf16[32,544,128]{2,1,0:T(8,128)(2,1)}, u32[]{:S(2)}, u32[]{:S(2)}) async-start(bf16[32,544,128]{2,1,0:T(8,128)(2,1)} %shard_map.94), calls=%async_computation | async-start | bytes 8912896 | tf_op jit(solution)/shard_map/all_to_all | solution.py:396
  17.7 0.1 convert_element_type.13
  17.8 0.1 broadcast_in_dim.64
  17.9 0.1 broadcast_in_dim.65
  18.0 0.1 bitcast_select_fusion
  18.1 1.3 collective-permute-start
  19.4 1.3 collective-permute-start.1
  20.7 1.3 collective-permute-start.2
  22.0 1.3 collective-permute-start.3
  23.3 1.3 collective-permute-start.4
  24.6 0.3 convolution_bitcast_fusion
  25.0 0.1 copy.16
  25.1 0.1 div.11
  25.2 1.3 collective-permute-start.5
  26.5 4.3 %collective-permute-done.1.refs_1_ = bf16[72,1440]{1,0:T(8,128)(2,1)S(1)} collective-permute-done((bf16[72,1440]{1,0:T(8,128)(2,1)S(1)}, bf16[72,1440]{1,0:T(8,128)(2,1)S(1)}, u32[]{:S(2)}, u32[]{:S(2)}) %collective-permute-start.1) | collective-permute-done | bytes 207392 | tf_op jit(solution)/shard_map/ppermute | solution.py:433
  30.8 1.3 collective-permute-start.6
  32.0 0.1 bitcast_divide_fusion.gate_ref
  32.1 0.5 collective-permute-done.2.refs_2_
  32.6 5.3 %collective-permute-done.3.refs_3_ = bf16[72,1440]{1,0:T(8,128)(2,1)S(1)} collective-permute-done((bf16[72,1440]{1,0:T(8,128)(2,1)S(1)}, bf16[72,1440]{1,0:T(8,128)(2,1)S(1)}, u32[]{:S(2)}, u32[]{:S(2)}) %collective-permute-start.3) | collective-permute-done | bytes 207392 | tf_op jit(solution)/shard_map/ppermute | solution.py:433
  37.9 0.7 collective-permute-done.4.refs_4_
  38.6 9.3 %collective-permute-done.5.refs_5_ = bf16[72,1440]{1,0:T(8,128)(2,1)S(1)} collective-permute-done((bf16[72,1440]{1,0:T(8,128)(2,1)S(1)}, bf16[72,1440]{1,0:T(8,128)(2,1)S(1)}, u32[]{:S(2)}, u32[]{:S(2)}) %collective-permute-start.5) | collective-permute-done | bytes 207392 | tf_op jit(solution)/shard_map/ppermute | solution.py:433
  47.9 0.1 collective-permute-done.6.refs_6_
  48.0 2.3 copy-done
  50.3 2.6 shard_map.95
  52.9 1.1 copy-done.1
  54.1 0.6 copy-done.8
  54.7 63.5 %all-to-all-done.got_hbm = bf16[32,544,128]{2,1,0:T(8,128)(2,1)} async-done(((bf16[32,544,128]{2,1,0:T(8,128)(2,1)}), bf16[32,544,128]{2,1,0:T(8,128)(2,1)}, u32[]{:S(2)}, u32[]{:S(2)}) %all-to-all-start) | async-done | bytes 4456480 | tf_op jit(solution)/shard_map/all_to_all | solution.py:396
  118.2 14.4 %shard_map.96 = (bf16[6,768,256]{2,1,0:T(8,128)(2,1)}, bf16[768,256]{1,0:T(8,128)(2,1)}) custom-call(bf16[32,544,128]{2,1,0:T(8,128)(2,1)} %all-to-all-done.got_hbm, bf16[1440,1440]{1,0:T(8,128)(2,1)} %bitcast.43, bf16[512,1440]{1,0:T(8,128)(2,1)} %copy-done.1), custom_call_target="tpu_custom_call" | custom-call | tf_op jit(solution)/shard_map/pallas_call | solution.py:385
  132.6 0.0 copy-start.3
  132.6 8.9 %all-to-all-start.1 = ((bf16[32,24,256]{2,1,0:T(8,128)(2,1)}), bf16[32,24,256]{2,1,0:T(8,128)(2,1)S(1)}, u32[]{:S(2)}, u32[]{:S(2)}) async-start(bf16[32,24,256]{2,1,0:T(8,128)(2,1)} %bitcast.55), calls=%async_computation.1 | async-start | bytes 786432 | tf_op jit(solution)/shard_map/all_to_all | solution.py:396
  141.5 14.8 %all-to-all-done.1 = bf16[32,24,256]{2,1,0:T(8,128)(2,1)S(1)} async-done(((bf16[32,24,256]{2,1,0:T(8,128)(2,1)}), bf16[32,24,256]{2,1,0:T(8,128)(2,1)S(1)}, u32[]{:S(2)}, u32[]{:S(2)}) %all-to-all-start.1) | async-done | bytes 393248 | tf_op jit(solution)/shard_map/all_to_all | solution.py:396
  156.3 0.7 copy-done.6
  157.0 0.7 copy-done.9
  157.7 1.6 shard_map.97
  159.3 11.8 %all_to_all.25.got_ref = bf16[8,8,2048]{2,1,0:T(8,128)(2,1)S(1)} all-to-all(bf16[8,8,2048]{2,1,0:T(8,128)(2,1)S(1)} %shard_map.97), channel_id=1, replica_groups=mesh['pipe'=8,'expert'=32] {'pipe'}, dimensions={0} | all-to-all | bytes 524288 | tf_op jit(solution)/shard_map/all_to_all | solution.py:396
  171.1 1.9 shard_map.98
  173.0 4.8 %all-to-all-start.3 = ((bf16[32,24,256]{2,1,0:T(8,128)(2,1)}), bf16[32,24,256]{2,1,0:T(8,128)(2,1)}, u32[]{:S(2)}, u32[]{:S(2)}) async-start(bf16[32,24,256]{2,1,0:T(8,128)(2,1)} %bitcast.21), calls=%async_computation.3 | async-start | bytes 786432 | tf_op jit(solution)/shard_map/all_to_all | solution.py:396
  177.9 2.0 shard_map.99
  179.8 0.7 copy-done.4
  180.5 12.0 %all-to-all-done.3 = bf16[32,24,256]{2,1,0:T(8,128)(2,1)} async-done(((bf16[32,24,256]{2,1,0:T(8,128)(2,1)}), bf16[32,24,256]{2,1,0:T(8,128)(2,1)}, u32[]{:S(2)}, u32[]{:S(2)}) %all-to-all-start.3) | async-done | bytes 393248 | tf_op jit(solution)/shard_map/all_to_all | solution.py:396
  192.5 7.4 %shard_map.100 = bf16[32,288,128]{2,1,0:T(8,128)(2,1)} custom-call(bf16[768,256]{1,0:T(8,128)(2,1)} %bitcast.22.got_ref, bf16[6,768,256]{2,1,0:T(8,128)(2,1)} %get-tuple-element.29.base_hbm, bf16[512,1440]{1,0:T(8,128)(2,1)} %copy-done.1, bf16[768,64]{1,0:T(8,128)(2,1)} %copy-done.4), custom_call_target="tpu_custom_call" | custom-call | tf_op jit(solution)/shard_map/pallas_call | solution.py:385
  199.9 0.0 copy-start.7
  199.9 61.0 %all_to_all.26.got_ref = bf16[32,288,128]{2,1,0:T(8,128)(2,1)S(1)} all-to-all(bf16[32,288,128]{2,1,0:T(8,128)(2,1)} %shard_map.100), channel_id=1, replica_groups=mesh['pipe'=8,'expert'=32] {'expert'}, dimensions={0} | all-to-all | bytes 4718592 | tf_op jit(solution)/shard_map/all_to_all | solution.py:396
  260.9 3.2 %shard_map.101 = (bf16[128,4,1440]{2,1,0:T(4,128)(2,1)}, f32[32,45]{1,0:T(8,128)}) custom-call(bf16[32,288,128]{2,1,0:T(8,128)(2,1)S(1)} %all_to_all.26.got_ref, s32[2,4,64]{2,1,0:T(4,128)S(1)} %bitcast.53), custom_call_target="tpu_custom_call" | custom-call | tf_op jit(solution)/shard_map/pallas_call | solution.py:385
  (21 shorter events, 0.2 us)
Async XLA Ops:
  6.3 11.4 %copy-start.5 = (s32[1,2,64,4]{2,3,1,0:T(4,128)S(1)}, s32[1,2,64,4]{2,3,1,0:T(4,128)}, u32[]{:S(2)}) copy-start(s32[1,2,64,4]{2,3,1,0:T(4,128)} %param.9) | copy-start | bytes 6148
  6.3 11.5 %copy-start.11 = (s32[1,2]{1,0:T(1,128)S(1)}, s32[1,2]{1,0:T(1,128)}, u32[]{:S(2)}) copy-start(s32[1,2]{1,0:T(1,128)} %param.10) | copy-start | bytes 28
  6.3 11.7 %copy-start.10 = (bf16[1,2,1440,32]{2,3,1,0:T(8,128)(2,1)S(1)}, bf16[1,2,1440,32]{2,3,1,0:T(8,128)(2,1)}, u32[]{:S(2)}) copy-start(bf16[1,2,1440,32]{2,3,1,0:T(8,128)(2,1)} %param.11) | copy-start | bytes 552964
  6.3 18.3 %copy-start.2 = (bf16[1,2,64,1440]{3,2,1,0:T(8,128)(2,1)S(1)}, bf16[1,2,64,1440]{3,2,1,0:T(8,128)(2,1)}, u32[]{:S(2)}) copy-start(bf16[1,2,64,1440]{3,2,1,0:T(8,128)(2,1)} %param.7) | copy-start | bytes 1105924
  6.3 111.9 %all-to-all-start = ((bf16[32,544,128]{2,1,0:T(8,128)(2,1)}), bf16[32,544,128]{2,1,0:T(8,128)(2,1)}, u32[]{:S(2)}, u32[]{:S(2)}) async-start(bf16[32,544,128]{2,1,0:T(8,128)(2,1)} %shard_map.94), calls=%async_computation | async-start | bytes 8912896 | tf_op jit(solution)/shard_map/all_to_all | solution.py:396
  18.1 7.1 %collective-permute-start = (bf16[72,1440]{1,0:T(8,128)(2,1)S(1)}, bf16[72,1440]{1,0:T(8,128)(2,1)S(1)}, u32[]{:S(2)}, u32[]{:S(2)}) collective-permute-start(bf16[72,1440]{1,0:T(8,128)(2,1)S(1)} %fusion.2.refs_7_), channel_id=1, source_target_pairs={{32,0},{64,32},{96,64},{128,96},{160,128},{192,160},{224,192},{33,... | collective-permute-start | bytes 622088 | tf_op jit(solution)/shard_map/ppermute | solution.py:433
  19.4 11.3 %collective-permute-start.1 = (bf16[72,1440]{1,0:T(8,128)(2,1)S(1)}, bf16[72,1440]{1,0:T(8,128)(2,1)S(1)}, u32[]{:S(2)}, u32[]{:S(2)}) collective-permute-start(bf16[72,1440]{1,0:T(8,128)(2,1)S(1)} %fusion.2.refs_7_), channel_id=1, source_target_pairs={{64,0},{96,32},{128,64},{160,96},{192,128},{224,160},{65,1},{97,33... | collective-permute-start | bytes 622088 | tf_op jit(solution)/shard_map/ppermute | solution.py:433
  20.7 11.9 %collective-permute-start.2 = (bf16[72,1440]{1,0:T(8,128)(2,1)S(1)}, bf16[72,1440]{1,0:T(8,128)(2,1)S(1)}, u32[]{:S(2)}, u32[]{:S(2)}) collective-permute-start(bf16[72,1440]{1,0:T(8,128)(2,1)S(1)} %fusion.2.refs_7_), channel_id=1, source_target_pairs={{96,0},{128,32},{160,64},{192,96},{224,128},{97,1},{129,33},{161,6... | collective-permute-start | bytes 622088 | tf_op jit(solution)/shard_map/ppermute | solution.py:433
  22.0 15.9 %collective-permute-start.3 = (bf16[72,1440]{1,0:T(8,128)(2,1)S(1)}, bf16[72,1440]{1,0:T(8,128)(2,1)S(1)}, u32[]{:S(2)}, u32[]{:S(2)}) collective-permute-start(bf16[72,1440]{1,0:T(8,128)(2,1)S(1)} %fusion.2.refs_7_), channel_id=1, source_target_pairs={{128,0},{160,32},{192,64},{224,96},{129,1},{161,33},{193,65},{225,... | collective-permute-start | bytes 622088 | tf_op jit(solution)/shard_map/ppermute | solution.py:433
  23.3 15.3 %collective-permute-start.4 = (bf16[72,1440]{1,0:T(8,128)(2,1)S(1)}, bf16[72,1440]{1,0:T(8,128)(2,1)S(1)}, u32[]{:S(2)}, u32[]{:S(2)}) collective-permute-start(bf16[72,1440]{1,0:T(8,128)(2,1)S(1)} %fusion.2.refs_7_), channel_id=1, source_target_pairs={{160,0},{192,32},{224,64},{161,1},{193,33},{225,65},{162,2},{194,3... | collective-permute-start | bytes 622088 | tf_op jit(solution)/shard_map/ppermute | solution.py:433
  25.2 22.7 %collective-permute-start.5 = (bf16[72,1440]{1,0:T(8,128)(2,1)S(1)}, bf16[72,1440]{1,0:T(8,128)(2,1)S(1)}, u32[]{:S(2)}, u32[]{:S(2)}) collective-permute-start(bf16[72,1440]{1,0:T(8,128)(2,1)S(1)} %fusion.2.refs_7_), channel_id=1, source_target_pairs={{192,0},{224,32},{193,1},{225,33},{194,2},{226,34},{195,3},{227,35... | collective-permute-start | bytes 622088 | tf_op jit(solution)/shard_map/ppermute | solution.py:433
  30.8 17.3 %collective-permute-start.6 = (bf16[72,1440]{1,0:T(8,128)(2,1)S(1)}, bf16[72,1440]{1,0:T(8,128)(2,1)S(1)}, u32[]{:S(2)}, u32[]{:S(2)}) collective-permute-start(bf16[72,1440]{1,0:T(8,128)(2,1)S(1)} %fusion.2.refs_7_), channel_id=1, source_target_pairs={{224,0},{225,1},{226,2},{227,3},{228,4},{229,5},{230,6},{231,7},{2... | collective-permute-start | bytes 622088 | tf_op jit(solution)/shard_map/ppermute | solution.py:433
  48.0 2.3 copy-start
  52.9 1.1 copy-start.1
  54.1 0.6 copy-start.8
  132.6 45.3 %copy-start.3 = (bf16[2,64,1440]{2,1,0:T(8,128)(2,1)S(1)}, bf16[2,64,1440]{2,1,0:T(8,128)(2,1)}, u32[]{:S(2)}) copy-start(bf16[2,64,1440]{2,1,0:T(8,128)(2,1)} %param.13) | copy-start | bytes 1105924
  132.6 23.7 %all-to-all-start.1 = ((bf16[32,24,256]{2,1,0:T(8,128)(2,1)}), bf16[32,24,256]{2,1,0:T(8,128)(2,1)S(1)}, u32[]{:S(2)}, u32[]{:S(2)}) async-start(bf16[32,24,256]{2,1,0:T(8,128)(2,1)} %bitcast.55), calls=%async_computation.1 | async-start | bytes 786432 | tf_op jit(solution)/shard_map/all_to_all | solution.py:396
  156.3 0.7 copy-start.6
  157.0 0.7 copy-start.9
  173.0 19.5 %all-to-all-start.3 = ((bf16[32,24,256]{2,1,0:T(8,128)(2,1)}), bf16[32,24,256]{2,1,0:T(8,128)(2,1)}, u32[]{:S(2)}, u32[]{:S(2)}) async-start(bf16[32,24,256]{2,1,0:T(8,128)(2,1)} %bitcast.21), calls=%async_computation.3 | async-start | bytes 786432 | tf_op jit(solution)/shard_map/all_to_all | solution.py:396
  179.8 0.7 copy-start.4
  199.9 61.0 %copy-start.7 = (s32[1,2,64,4]{2,3,1,0:T(4,128)S(1)}, s32[1,2,64,4]{2,3,1,0:T(4,128)}, u32[]{:S(2)}) copy-start(s32[1,2,64,4]{2,3,1,0:T(4,128)} %param.9) | copy-start | bytes 6148

commit v3 on v0

--- a/solution.py
+++ b/solution.py
@@ -14,13 +14,14 @@
 NT = (((1,), (1,)), ((), ()))
 TN = (((0,), (0,)), ((), ()))
 VM = pl.BlockSpec(memory_space=pltpu.VMEM)
+HB = pl.BlockSpec(memory_space=pltpu.HBM)
 SM = pl.BlockSpec(memory_space=pltpu.SMEM)
 
 N, T, K, E, HALF = 128, 64, 4, 32, 12
 ROWS = 2 * HALF
 ALL = E * ROWS
 W = 256
-MIBS = (20, 20, 32, 12, 12, 20, 24, 20)
+MIBS = (62, 20, 24, 12, 12, 16, 16, 20)
 LATER = 224
 
 
@@ -86,16 +87,26 @@
     return (row - ROWS * divided(row, ROWS)) < HALF
 
 
-def dispatch_kernel(ids_ref, hid_ref, grad_ref, out_ref):
+def dispatch_kernel(ids_ref, hid_hbm, grad_hbm, out_hbm, hid_ref, grad_ref, out_ref, sems):
+    loads = [
+        pltpu.make_async_copy(grad_hbm, grad_ref, sems.at[0]),
+        pltpu.make_async_copy(hid_hbm, hid_ref, sems.at[1]),
+    ]
+    for load in loads:
+        load.start()
     codes = slot_codes(ids_ref)
+    tokens = rows_by_slots(functools.reduce(jnp.maximum, codes))
     pick = rows_by_slots(token_major(codes))
-    tokens = rows_by_slots(functools.reduce(jnp.maximum, codes))
+    for load in loads:
+        load.wait()
     width = grad_ref.shape[1]
+    stores = []
     for start in range(0, width, 256):
         cols = slice(start, min(start + 256, width))
         size = cols.stop - start
         grad = dot(tokens, grad_ref[:, cols], NN)
         hid = dot(pick, hid_ref[:, :, cols].reshape(N * K, size), NN)
+        first = 2 * ROWS * (start // 128)
         for lanes in range(0, size, 128):
             at = 2 * ROWS * ((start + lanes) // 128)
             cut = min(lanes + 128, size)
@@ -104,6 +115,7 @@
             if cut - lanes == 128:
                 out_ref[:, at : at + ROWS, :] = left.astype(BF)
                 out_ref[:, at + ROWS : at + 2 * ROWS, :] = right.astype(BF)
+                last = at + 2 * ROWS
             else:
                 tail = [
                     left[:, 0:16],
@@ -112,6 +124,15 @@
                     jnp.zeros((E, 16, 32), F32),
                 ]
                 out_ref[:, at : at + 16, :] = jnp.concatenate(tail, axis=2).astype(BF)
+                last = at + 16
+        part = pl.ds(first, last - first)
+        store = pltpu.make_async_copy(
+            out_ref.at[:, part, :], out_hbm.at[:, part, :], sems.at[2 + len(stores)]
+        )
+        store.start()
+        stores.append(store)
+    for store in stores:
+        store.wait()
 
 
 def tables_kernel(*refs):
@@ -148,7 +169,7 @@
     for start in range(0, inner, 256):
         cols = slice(start, min(start + 256, inner))
         base = dot(grad_ref[...], down_ref[cols, :], NT)
-        base_ref[:, cols] = base
+        base_ref[:, cols] = base.astype(BF)
         total = total + jnp.sum(hid_ref[:, cols].astype(F32) * base, axis=1, keepdims=True)
     high, low = split(total)
     left = dot(hid_ref[...], back_ref[0:W, :], NT)
@@ -269,7 +290,7 @@
     for start in range(0, width, 256):
         cols = slice(start, min(start + 256, width))
         moved = dot(left, back_ref[0:W, cols], NN) + dot(right, back_ref[W : 2 * W, cols], NN)
-        out_ref[:, cols] = (gate * base_ref[:, cols] + moved).astype(BF)
+        out_ref[:, cols] = (gate * base_ref[:, cols].astype(F32) + moved).astype(BF)
     out_ref[:, width : width + 2 * E] = part_ref[...]
     out_ref[:, width + 2 * E :] = jnp.zeros((ALL, out_ref.shape[1] - width - 2 * E), BF)
 
@@ -294,13 +315,18 @@
     router_ref[:, ROWS:each] = flipped[1][:, 0 : each - ROWS]
 
 
-def call(body, shapes, args, mib, smem=0, scratch=()):
+def call(body, shapes, args, mib, smem=0, scratch=(), sems=0, far=(), far_out=()):
+    ins = [SM] * smem + [VM] * (len(args) - smem)
+    ins = [HB if i in far else spec for i, spec in enumerate(ins)]
+    held = [pltpu.VMEM(s, d) for s, d in scratch]
+    if sems:
+        held.append(pltpu.SemaphoreType.DMA((sems,)))
     return pl.pallas_call(
         body,
         out_shape=[jax.ShapeDtypeStruct(s, d) for s, d in shapes],
-        in_specs=[SM] * smem + [VM] * (len(args) - smem),
-        out_specs=[VM] * len(shapes),
-        scratch_shapes=list(scratch),
+        in_specs=ins,
+        out_specs=[HB if i in far_out else VM for i in range(len(shapes))],
+        scratch_shapes=held,
         compiler_params=pltpu.CompilerParams(vmem_limit_bytes=mib << 20),
     )(*args)
 
@@ -321,11 +347,17 @@
     turned = routes.transpose(0, 2, 1)
     tall = 2 * ROWS * (inner // 128) + 16
 
+    steps = pl.cdiv(inner, 256)
+
     (sent,) = call(
         dispatch_kernel,
         [((E, tall, 128), BF)],
         (turned, hidden[0].reshape(N, K, inner), grads),
         MIBS[0],
+        scratch=[((N, K, inner), BF), ((N, width), BF), ((E, tall, 128), BF)],
+        sems=2 + steps,
+        far=(1, 2),
+        far_out=(0,),
     )
     arrived = exchange(sent, "expert")
 
@@ -355,35 +387,44 @@
 
     base, proj = call(
         expert_kernel,
-        [((ALL, inner), F32), ((ALL, W), BF)],
+        [((ALL, inner), BF), ((ALL, W), BF)],
         (arrived, mats, back),
         MIBS[2],
-        scratch=[pltpu.VMEM((ALL, inner), BF)] * 2,
-    )
-    proj, gating = lax.optimization_barrier((proj, gating))
+        scratch=[((ALL, width), BF), ((ALL, inner), BF)],
+    )
+    rest = (gating, turned, id_all, section.reshape(1), grads, inputs, table_rows, back, base)
+    proj, rest = lax.optimization_barrier((proj, rest))
     returned = exchange(proj.reshape(E, ROWS, W), "expert").reshape(ALL, W)
+    returned, rest = lax.optimization_barrier((returned, rest))
+    gating, turned, id_all, where, grads, inputs, table_rows, back, base = rest
     (blocks,) = call(
         blocks_kernel,
         [((8, 8, K * K * N), BF)],
         (returned, turned, id_all, gating),
         MIBS[3],
     )
+    blocks, rest = lax.optimization_barrier((blocks, rest))
     gathered = exchange(blocks, "pipe")
+    gathered, rest = lax.optimization_barrier((gathered, rest))
+    gating, turned, id_all, where, grads, inputs, table_rows, back, base = rest
     coef_sent, coef = call(
         solve_kernel,
         [((ALL, W), BF), ((N, W), BF)],
-        (section.reshape(1), gathered, turned, id_all, gating),
+        (where, gathered, turned, id_all, gating),
         MIBS[4],
         smem=1,
     )
+    coef_sent, coef, rest = lax.optimization_barrier((coef_sent, coef, rest))
     coef_got = exchange(coef_sent.reshape(E, ROWS, W), "expert").reshape(ALL, W)
+    coef_got, coef, rest = lax.optimization_barrier((coef_got, coef, rest))
+    gating, turned, id_all, where, grads, inputs, table_rows, back, base = rest
     passed, parts = call(
         passed_kernel,
         [((N, width), BF), ((ALL, 2 * E), BF)],
         (coef, table_rows, grads, inputs.reshape(N, width)),
         MIBS[5],
     )
-    wide = 128 * pl.cdiv(inner + 2 * E, 128)
+    wide = 256 * steps
     (answer,) = call(
         answer_kernel, [((ALL, wide), BF)], (coef_got, base, back, parts), MIBS[6]
     )

time: 263 us -> 253 us (0.962)
  blocking collectives: 84.1 us -> 115 us
  waiting for transfers between devices: 93.8 us -> 75.1 us
  local copies, waits for them, and re-layouts: 29.3 us -> 14.7 us
  starting transfers between devices: 29.6 us -> 20.4 us
    all_to_all x2 -> x4, blocking collectives: 84.1 us -> 115 us  [exchange(): return lax.all_to_all(x, axis, split_axis=0, concat_axis=0, tiled=True)]
    all_to_all x3 -> x1, waiting for transfers between devices: 80.1 us -> 59 us  [exchange(): return lax.all_to_all(x, axis, split_axis=0, concat_axis=0, tiled=True)]
    unnamed x62 -> x44, local copies, waits for them, and re-layouts: 28.8 us -> 14.2 us
    all_to_all x3 -> x1, starting transfers between devices: 20.6 us -> 11.4 us  [exchange(): return lax.all_to_all(x, axis, split_axis=0, concat_axis=0, tiled=True)]
  transfers between devices with their start and end apart: 10 -> 8, of which waited for: 6 -> 6; matrix products, arithmetic and copies ran while one was open for 0% -> 1% of each run, Pallas kernels for 2% -> 1%
where the time goes in v3:
time: 253 us
  blocking collectives  115 us (45%)
  waiting for transfers between devices  75.1 us (30%)
  Pallas kernels  25.2 us (10%)
  starting transfers between devices  20.4 us (8%)
  local copies, waits for them, and re-layouts  14.7 us (6%)
    all_to_all x4, blocking collectives, exchange(): return lax.all_to_all(x, axis, split_axis=0, concat_axis=0, tiled=True)  115 us
    all_to_all x1, waiting for transfers between devices, exchange(): return lax.all_to_all(x, axis, split_axis=0, concat_axis=0, tiled=True)  59 us
    pallas_call x8, Pallas kernels, call(): pl.pallas_call(body, out_shape=[jax.ShapeDtypeStruct(s, d) for s, d in sh...  25.2 us
    ppermute x7, waiting for transfers between devices, on_device(): lax.ppermute(own, 'pipe', [(i, i - by) for i in range(by, pipe)])  16.1 us
    unnamed x44, local copies, waits for them, and re-layouts  14.2 us
    all_to_all x1, starting transfers between devices, exchange(): return lax.all_to_all(x, axis, split_axis=0, concat_axis=0, tiled=True)  11.4 us
    ppermute x7, starting transfers between devices, on_device(): lax.ppermute(own, 'pipe', [(i, i - by) for i in range(by, pipe)])  9.02 us
  transfers between devices with their start and end apart: 8, of which 6 were waited for; matrix products, arithmetic and copies ran while one was open for 1% of the time, Pallas kernels for 1%

profile of v3, /device:TPU:32, one launch (start us, length us, event | category | flops | bytes accessed | tf_op | source)
XLA Modules:
  0.0 252.7 jit_solution(4646878171780706086)
XLA Ops:
  0.6 5.6 %shard_map.94 = bf16[32,544,128]{2,1,0:T(8,128)(2,1)} custom-call(s32[2,4,64]{2,1,0:T(4,128)} %bitcast.56, bf16[128,4,1440]{2,1,0:T(4,128)(2,1)} %bitcast.61, bf16[128,1440]{1,0:T(8,128)(2,1)} %bitcast.51), custom_call_target="tpu_custom_call" | custom-call | tf_op jit(solution)/shard_map/pallas_call | solution.py:324
  6.3 11.4 %all-to-all-start = ((bf16[32,544,128]{2,1,0:T(8,128)(2,1)}), bf16[32,544,128]{2,1,0:T(8,128)(2,1)}, u32[]{:S(2)}, u32[]{:S(2)}) async-start(bf16[32,544,128]{2,1,0:T(8,128)(2,1)} %shard_map.94), calls=%async_computation | async-start | bytes 8912896 | tf_op jit(solution)/shard_map/all_to_all | solution.py:335
  17.7 0.1 convert_element_type.13
  17.8 0.1 broadcast_in_dim.64
  17.9 0.1 broadcast_in_dim.65
  18.0 0.1 bitcast_select_fusion
  18.1 1.3 collective-permute-start
  19.4 1.3 collective-permute-start.1
  20.7 1.3 collective-permute-start.2
  22.0 1.3 collective-permute-start.3
  23.3 1.3 collective-permute-start.4
  24.6 0.3 convolution_bitcast_fusion
  25.0 0.1 copy.16
  25.1 0.1 div.11
  25.2 0.7 copy-done.7
  25.9 1.3 collective-permute-start.5
  27.2 3.6 %collective-permute-done.1.refs_1_ = bf16[72,1440]{1,0:T(8,128)(2,1)S(1)} collective-permute-done((bf16[72,1440]{1,0:T(8,128)(2,1)S(1)}, bf16[72,1440]{1,0:T(8,128)(2,1)S(1)}, u32[]{:S(2)}, u32[]{:S(2)}) %collective-permute-start.1) | collective-permute-done | bytes 207392 | tf_op jit(solution)/shard_map/ppermute | solution.py:372
  30.7 0.7 copy-done.9
  31.4 1.3 collective-permute-start.6
  32.7 0.7 bitcast_divide_fusion.gate_ref
  33.4 0.7 copy-done.11
  34.1 3.8 %collective-permute-done.3.refs_3_ = bf16[72,1440]{1,0:T(8,128)(2,1)S(1)} collective-permute-done((bf16[72,1440]{1,0:T(8,128)(2,1)S(1)}, bf16[72,1440]{1,0:T(8,128)(2,1)S(1)}, u32[]{:S(2)}, u32[]{:S(2)}) %collective-permute-start.3) | collective-permute-done | bytes 207392 | tf_op jit(solution)/shard_map/ppermute | solution.py:372
  37.9 0.7 copy-done.13
  38.6 0.1 collective-permute-done.4.refs_4_
  38.6 0.7 copy-done.15
  39.3 8.6 %collective-permute-done.5.refs_5_ = bf16[72,1440]{1,0:T(8,128)(2,1)S(1)} collective-permute-done((bf16[72,1440]{1,0:T(8,128)(2,1)S(1)}, bf16[72,1440]{1,0:T(8,128)(2,1)S(1)}, u32[]{:S(2)}, u32[]{:S(2)}) %collective-permute-start.5) | collective-permute-done | bytes 207392 | tf_op jit(solution)/shard_map/ppermute | solution.py:372
  47.9 0.1 collective-permute-done.6.refs_6_
  48.0 2.3 copy-done
  50.3 0.9 copy-done.5
  51.2 0.9 copy-done.8
  52.1 0.9 copy-done.10
  53.1 0.9 copy-done.12
  54.0 0.9 copy-done.14
  55.0 0.9 copy-done.16
  55.9 2.6 %shard_map.95 = (bf16[512,1440]{1,0:T(8,128)(2,1)S(1)}, bf16[512,1440]{1,0:T(8,128)(2,1)S(1)}, f32[32,128]{1,0:T(8,128)S(1)}) custom-call(bf16[72,1440]{1,0:T(8,128)(2,1)S(1)} %copy-done.8, bf16[72,1440]{1,0:T(8,128)(2,1)S(1)} %copy-done.10, bf16[72,1440]{1,0:T(8,128)(2,1)S(1)} %copy-done.12, bf16[72,1440]{1,0:T(8,128)(2,1)S(1)} %copy-done.14, ...), custom_call_target="tpu_custom_call" | custom-call | tf_op jit(solution)/shard_map/pallas_call | solution.py:324
  58.6 0.6 copy-done.18
  59.2 59.0 %all-to-all-done.got_ref = bf16[32,544,128]{2,1,0:T(8,128)(2,1)} async-done(((bf16[32,544,128]{2,1,0:T(8,128)(2,1)}), bf16[32,544,128]{2,1,0:T(8,128)(2,1)}, u32[]{:S(2)}, u32[]{:S(2)}) %all-to-all-start) | async-done | bytes 4456480 | tf_op jit(solution)/shard_map/all_to_all | solution.py:335
  118.2 2.3 copy-done.1
  120.4 7.5 %shard_map.96 = (bf16[768,1440]{1,0:T(8,128)(2,1)S(1)}, bf16[768,256]{1,0:T(8,128)(2,1)S(1)}) custom-call(bf16[32,544,128]{2,1,0:T(8,128)(2,1)} %all-to-all-done.got_ref, bf16[1440,1440]{1,0:T(8,128)(2,1)S(1)} %bitcast.46, bf16[512,1440]{1,0:T(8,128)(2,1)S(1)} %get-tuple-element.132.back_ref), custom_call_target="tpu_custom_call" | custom-call | tf_op jit(solution)/shard_map/pallas_call | solution.py:324
  128.0 23.5 %all_to_all.25 = bf16[32,24,256]{2,1,0:T(8,128)(2,1)S(1)} all-to-all(bf16[32,24,256]{2,1,0:T(8,128)(2,1)S(1)} %bitcast.55), channel_id=1, replica_groups=mesh['pipe'=8,'expert'=32] {'expert'}, dimensions={0} | all-to-all | bytes 786432 | tf_op jit(solution)/shard_map/all_to_all | solution.py:335
  151.5 1.6 shard_map.97
  153.1 11.8 %all_to_all.26.got_ref = bf16[8,8,2048]{2,1,0:T(8,128)(2,1)S(1)} all-to-all(bf16[8,8,2048]{2,1,0:T(8,128)(2,1)S(1)} %shard_map.97), channel_id=1, replica_groups=mesh['pipe'=8,'expert'=32] {'pipe'}, dimensions={0} | all-to-all | bytes 524288 | tf_op jit(solution)/shard_map/all_to_all | solution.py:335
  164.9 1.2 shard_map.98
  166.1 19.2 %all_to_all.27 = bf16[32,24,256]{2,1,0:T(8,128)(2,1)S(1)} all-to-all(bf16[32,24,256]{2,1,0:T(8,128)(2,1)S(1)} %bitcast.54), channel_id=1, replica_groups=mesh['pipe'=8,'expert'=32] {'expert'}, dimensions={0} | all-to-all | bytes 786432 | tf_op jit(solution)/shard_map/all_to_all | solution.py:335
  185.3 2.0 shard_map.99
  187.2 1.5 shard_map.100
  188.7 60.8 %all_to_all.28 = bf16[32,24,1536]{2,1,0:T(8,128)(2,1)S(1)} all-to-all(bf16[32,24,1536]{2,1,0:T(8,128)(2,1)S(1)} %bitcast.47), channel_id=1, replica_groups=mesh['pipe'=8,'expert'=32] {'expert'}, dimensions={0} | all-to-all | bytes 4718592 | tf_op jit(solution)/shard_map/all_to_all | solution.py:335
  249.5 3.2 %shard_map.101 = (bf16[128,4,1440]{2,1,0:T(4,128)(2,1)}, f32[32,45]{1,0:T(8,128)}) custom-call(bf16[768,1536]{1,0:T(8,128)(2,1)S(1)} %bitcast.48, s32[2,4,64]{2,1,0:T(4,128)S(1)} %bitcast.60), custom_call_target="tpu_custom_call" | custom-call | tf_op jit(solution)/shard_map/pallas_call | solution.py:324
  (39 shorter events, 0.2 us)
Async XLA Ops:
  6.2 11.4 %copy-start.17 = (s32[1,2,64,4]{2,3,1,0:T(4,128)S(1)}, s32[1,2,64,4]{2,3,1,0:T(4,128)}, u32[]{:S(2)}) copy-start(s32[1,2,64,4]{2,3,1,0:T(4,128)} %param.9) | copy-start | bytes 6148
  6.2 11.5 %copy-start.21 = (s32[1,2]{1,0:T(1,128)S(1)}, s32[1,2]{1,0:T(1,128)}, u32[]{:S(2)}) copy-start(s32[1,2]{1,0:T(1,128)} %param.10) | copy-start | bytes 28
  6.3 11.7 %copy-start.20 = (bf16[1,2,1440,32]{2,3,1,0:T(8,128)(2,1)S(1)}, bf16[1,2,1440,32]{2,3,1,0:T(8,128)(2,1)}, u32[]{:S(2)}) copy-start(bf16[1,2,1440,32]{2,3,1,0:T(8,128)(2,1)} %param.11) | copy-start | bytes 552964
  6.3 18.4 %copy-start.2 = (bf16[1,2,64,1440]{3,2,1,0:T(8,128)(2,1)S(1)}, bf16[1,2,64,1440]{3,2,1,0:T(8,128)(2,1)}, u32[]{:S(2)}) copy-start(bf16[1,2,64,1440]{3,2,1,0:T(8,128)(2,1)} %param.7) | copy-start | bytes 1105924
  6.3 111.9 %all-to-all-start = ((bf16[32,544,128]{2,1,0:T(8,128)(2,1)}), bf16[32,544,128]{2,1,0:T(8,128)(2,1)}, u32[]{:S(2)}, u32[]{:S(2)}) async-start(bf16[32,544,128]{2,1,0:T(8,128)(2,1)} %shard_map.94), calls=%async_computation | async-start | bytes 8912896 | tf_op jit(solution)/shard_map/all_to_all | solution.py:335
  18.1 29.9 %copy-start.4 = (bf16[72,1440]{1,0:T(8,128)(2,1)}, bf16[72,1440]{1,0:T(8,128)(2,1)S(1)}, u32[]{:S(2)}) copy-start(bf16[72,1440]{1,0:T(8,128)(2,1)S(1)} %fusion.1.refs_7_) | copy-start | bytes 622084
  18.1 7.1 %collective-permute-start = (bf16[72,1440]{1,0:T(8,128)(2,1)S(1)}, bf16[72,1440]{1,0:T(8,128)(2,1)S(1)}, u32[]{:S(2)}, u32[]{:S(2)}) collective-permute-start(bf16[72,1440]{1,0:T(8,128)(2,1)S(1)} %fusion.1.refs_7_), channel_id=1, source_target_pairs={{32,0},{64,32},{96,64},{128,96},{160,128},{192,160},{224,192},{33,... | collective-permute-start | bytes 622088 | tf_op jit(solution)/shard_map/ppermute | solution.py:372
  19.4 11.3 %collective-permute-start.1 = (bf16[72,1440]{1,0:T(8,128)(2,1)S(1)}, bf16[72,1440]{1,0:T(8,128)(2,1)S(1)}, u32[]{:S(2)}, u32[]{:S(2)}) collective-permute-start(bf16[72,1440]{1,0:T(8,128)(2,1)S(1)} %fusion.1.refs_7_), channel_id=1, source_target_pairs={{64,0},{96,32},{128,64},{160,96},{192,128},{224,160},{65,1},{97,33... | collective-permute-start | bytes 622088 | tf_op jit(solution)/shard_map/ppermute | solution.py:372
  20.7 12.7 %collective-permute-start.2 = (bf16[72,1440]{1,0:T(8,128)(2,1)S(1)}, bf16[72,1440]{1,0:T(8,128)(2,1)S(1)}, u32[]{:S(2)}, u32[]{:S(2)}) collective-permute-start(bf16[72,1440]{1,0:T(8,128)(2,1)S(1)} %fusion.1.refs_7_), channel_id=1, source_target_pairs={{96,0},{128,32},{160,64},{192,96},{224,128},{97,1},{129,33},{161,6... | collective-permute-start | bytes 622088 | tf_op jit(solution)/shard_map/ppermute | solution.py:372
  22.0 15.9 %collective-permute-start.3 = (bf16[72,1440]{1,0:T(8,128)(2,1)S(1)}, bf16[72,1440]{1,0:T(8,128)(2,1)S(1)}, u32[]{:S(2)}, u32[]{:S(2)}) collective-permute-start(bf16[72,1440]{1,0:T(8,128)(2,1)S(1)} %fusion.1.refs_7_), channel_id=1, source_target_pairs={{128,0},{160,32},{192,64},{224,96},{129,1},{161,33},{193,65},{225,... | collective-permute-start | bytes 622088 | tf_op jit(solution)/shard_map/ppermute | solution.py:372
  23.3 15.3 %collective-permute-start.4 = (bf16[72,1440]{1,0:T(8,128)(2,1)S(1)}, bf16[72,1440]{1,0:T(8,128)(2,1)S(1)}, u32[]{:S(2)}, u32[]{:S(2)}) collective-permute-start(bf16[72,1440]{1,0:T(8,128)(2,1)S(1)} %fusion.1.refs_7_), channel_id=1, source_target_pairs={{160,0},{192,32},{224,64},{161,1},{193,33},{225,65},{162,2},{194,3... | collective-permute-start | bytes 622088 | tf_op jit(solution)/shard_map/ppermute | solution.py:372
  25.2 0.7 copy-start.7
  25.9 22.0 %collective-permute-start.5 = (bf16[72,1440]{1,0:T(8,128)(2,1)S(1)}, bf16[72,1440]{1,0:T(8,128)(2,1)S(1)}, u32[]{:S(2)}, u32[]{:S(2)}) collective-permute-start(bf16[72,1440]{1,0:T(8,128)(2,1)S(1)} %fusion.1.refs_7_), channel_id=1, source_target_pairs={{192,0},{224,32},{193,1},{225,33},{194,2},{226,34},{195,3},{227,35... | collective-permute-start | bytes 622088 | tf_op jit(solution)/shard_map/ppermute | solution.py:372
  30.7 0.7 copy-start.9
  31.4 16.6 %collective-permute-start.6 = (bf16[72,1440]{1,0:T(8,128)(2,1)S(1)}, bf16[72,1440]{1,0:T(8,128)(2,1)S(1)}, u32[]{:S(2)}, u32[]{:S(2)}) collective-permute-start(bf16[72,1440]{1,0:T(8,128)(2,1)S(1)} %fusion.1.refs_7_), channel_id=1, source_target_pairs={{224,0},{225,1},{226,2},{227,3},{228,4},{229,5},{230,6},{231,7},{2... | collective-permute-start | bytes 622088 | tf_op jit(solution)/shard_map/ppermute | solution.py:372
  33.4 0.7 copy-start.11
  37.9 0.7 copy-start.13
  38.6 0.7 copy-start.15
  48.0 2.3 copy-start
  50.3 0.9 copy-start.5
  51.2 0.9 copy-start.8
  52.1 0.9 copy-start.10
  53.1 0.9 copy-start.12
  54.0 0.9 copy-start.14
  55.0 0.9 copy-start.16
  58.5 0.6 copy-start.18
  118.2 2.3 copy-start.1
  120.4 31.0 %copy-start.6 = (f32[128,4]{1,0:T(8,128)S(1)}, f32[128,4]{1,0:T(8,128)}, u32[]{:S(2)}) copy-start(f32[128,4]{1,0:T(8,128)} %bitcast_divide_fusion.gate_ref) | copy-start | bytes 6148
  120.4 31.0 %copy-start.19 = (f32[32,128]{1,0:T(8,128)S(1)}, f32[32,128]{1,0:T(8,128)}, u32[]{:S(2)}) copy-start(f32[32,128]{1,0:T(8,128)} %copy-done.18) | copy-start | bytes 49156
  128.0 57.3 %copy-start.3 = (bf16[2,64,1440]{2,1,0:T(8,128)(2,1)S(1)}, bf16[2,64,1440]{2,1,0:T(8,128)(2,1)}, u32[]{:S(2)}) copy-start(bf16[2,64,1440]{2,1,0:T(8,128)(2,1)} %param.13) | copy-start | bytes 1105924

commit v4 on v3

--- a/solution.py
+++ b/solution.py
@@ -136,21 +136,58 @@
 
 
 def tables_kernel(*refs):
-    held, down_ref, tab_ref, back_ref, ids_ref = refs[:8], refs[8], refs[9], refs[10], refs[11]
+    held, down_ref, tab_ref, back_ref = refs[:8], refs[8], refs[9], refs[10]
     for b in range(8):
         for m in range(2):
             tab_ref[m * W + b * E : m * W + (b + 1) * E, :] = held[b][m * E : (m + 1) * E, :]
-    rows = jnp.concatenate([held[b][2 * E : 2 * E + 8, 0:N].astype(F32) for b in range(8)], axis=0)
-    for j in range(K):
-        for b in range(8):
-            ids_ref[8 * j + b : 8 * j + b + 1, :] = rows[8 * b + j : 8 * b + j + 1, :]
     for m in range(2):
         back_ref[m * W : (m + 1) * W, :] = dot(
             tab_ref[m * W : (m + 1) * W, :], down_ref[...], NT
         ).astype(BF)
 
 
-def expert_kernel(got_ref, down_ref, back_ref, base_ref, out_ref, grad_ref, hid_ref):
+def names_kernel(me_ref, all_ref, out_ref):
+    me = me_ref[0].astype(F32)
+    blocks = all_ref[...].astype(F32).reshape(E, K * 8, N)
+    marks = jnp.zeros((E, N), F32)
+    for j in range(K):
+        marks = jnp.where(blocks[:, 8 * j + 7, :] == me, 1.0, marks)
+    first, second = iota((N, N), 0), iota((N, N), 1)
+    earlier = one((first < second) & ((first >> 6) == (second >> 6)))
+    place = dot(marks.astype(BF), earlier, NN) + (HALF * (iota((E, N), 1) >> 6)).astype(F32)
+    pick = rows_by_slots(jnp.where(marks > 0.5, place, -1.0))
+    for e in range(E):
+        rows = slice(e * ROWS, (e + 1) * ROWS)
+        block = all_ref[e * 8 * K : (e + 1) * 8 * K, :]
+        out_ref[rows, :] = dot(pick[rows], block, NT).astype(BF)
+
+
+def packed(x):
+    x = x.reshape(E, ROWS, 32)
+    parts = [x[:, 0:8], x[:, 8:16], x[:, 16:24], jnp.zeros((E, 8, 32), x.dtype)]
+    return jnp.concatenate(parts, axis=2).astype(BF)
+
+
+def unpacked(ref):
+    x = ref[...].astype(F32)
+    parts = [x[:, :, 32 * q : 32 * q + 32] for q in range(3)]
+    return jnp.concatenate(parts, axis=1).reshape(ALL, 32)
+
+
+def row_masks(names_ref):
+    spread = one((iota((8, W), 1) >> 5) == iota((8, W), 0))
+    lane = (iota((ALL, W), 1) & (E - 1)).astype(F32)
+    return [dot(names_ref[:, 8 * j : 8 * j + 8], spread, NN) == lane for j in range(K)]
+
+
+def section_columns(j):
+    row, col = iota((W, 32), 0), iota((W, 32), 1)
+    return one((row < LATER) & ((row >> 5) + 8 * j == col))
+
+
+def expert_kernel(
+    got_ref, down_ref, back_ref, names_ref, base_ref, out_ref, grad_ref, hid_ref
+):
     inner = down_ref.shape[0]
     full = 128 * (inner // 128)
     for lanes in range(0, full, 128):
@@ -175,10 +212,14 @@
     left = dot(hid_ref[...], back_ref[0:W, :], NT)
     right = dot(hid_ref[...], back_ref[W : 2 * W, :], NT)
     proj = jnp.where(first_half(ALL, W), left, right)
-    lane = iota((ALL, W), 1)
-    tail = jnp.where(lane == LATER, high.astype(F32), low.astype(F32))
-    tail = jnp.where(lane < LATER + 2, tail, 0.0)
-    out_ref[...] = jnp.where(lane < LATER, proj, tail).astype(BF)
+    chosen = jnp.zeros((ALL, 32), F32)
+    for j, mask in enumerate(row_masks(names_ref)):
+        kept = jnp.where(mask, proj, 0.0).astype(BF)
+        chosen = chosen + dot(kept, section_columns(j), NN)
+    col = iota((ALL, 32), 1)
+    chosen = jnp.where(col == 7, high.astype(F32), chosen)
+    chosen = jnp.where(col == 15, low.astype(F32), chosen)
+    out_ref[...] = packed(chosen)
 
 
 def id_masks(ids_ref):
@@ -191,31 +232,29 @@
     return masks, spread
 
 
-def blocks_kernel(got_ref, row_ref, ids_ref, gate_ref, out_ref):
+def blocks_kernel(got_ref, row_ref, gate_ref, out_ref):
     pick = slots_by_rows(jnp.concatenate(slot_codes(row_ref), axis=1))
-    slots = dot(pick, got_ref[...], NN)
+    slots = dot(pick, unpacked(got_ref).astype(BF), NN)
     gates = [gate_ref[:, k : k + 1] for k in range(K)]
-    parts = [slots[k * N : (k + 1) * N] for k in range(K)]
-    lane = iota((N, W), 1)
+    col = iota((N, 32), 1)
     full = []
-    for part in parts:
-        dots = part[:, LATER : LATER + 1] + part[:, LATER + 1 : LATER + 2]
-        full.append(jnp.where(lane < LATER, part, dots))
+    for k in range(K):
+        part = slots[k * N : (k + 1) * N]
+        dots = part[:, 7:8] + part[:, 15:16]
+        full.append(jnp.where(col == 7, dots, part))
     mean = sum(gates[k] * full[k] for k in range(K))
-    masks, spread = id_masks(ids_ref)
-    rows = []
+    same = one(iota((32, 32), 0) == iota((32, 32), 1))
+    cells = []
     for k in range(K):
         value = gates[k] * (full[k] - mean)
-        high, low = split(value)
-        for j in range(K):
-            source = jnp.where(masks[j] & (lane < LATER), high.astype(F32), 0.0)
-            if j < 2:
-                extra = high if j == 0 else low
-                source = jnp.where(lane == LATER, extra.astype(F32), source)
-            rows.append(source.astype(BF))
-    packed = dot(spread, jnp.concatenate(rows, axis=0), NT).astype(BF)
+        high, low = split(value[:, 7:8])
+        value = jnp.where(col == 7, high.astype(F32), value)
+        value = jnp.where(col == 15, low.astype(F32), value).astype(BF)
+        turned = dot(same, value, NT).astype(BF)
+        cells += [turned[8 * j : 8 * j + 8, :] for j in range(K)]
+    block = jnp.concatenate(cells, axis=1)
     for d in range(8):
-        out_ref[d] = packed
+        out_ref[d] = block
 
 
 def solve_kernel(at_ref, got_ref, row_ref, ids_ref, gate_ref, out_ref, coef_ref):
@@ -248,16 +287,19 @@
         wide = dot(high[:, cut], spread, TN) + dot(low[:, cut], spread, TN)
         coef = jnp.where(masks[j], wide, coef)
     coef_ref[...] = coef.astype(BF)
-    lane = iota((N, W), 1)
+    same = one(iota((32, 32), 0) == iota((32, 32), 1))
+    tall_high = jnp.concatenate([high[:, j * N : (j + 1) * N] for j in range(K)], axis=0)
+    tall_low = jnp.concatenate([low[:, j * N : (j + 1) * N] for j in range(K)], axis=0)
+    short = dot(tall_high, same, TN) + dot(tall_low, same, TN)
+    col = iota((N, 32), 1)
     rows = []
     for k in range(K):
         gate = gate_ref[:, k : k + 1]
         up, rest = split(gate)
-        tail = jnp.where(lane == LATER, up.astype(F32), rest.astype(F32))
-        tail = jnp.where(lane < LATER + 2, tail, 0.0)
-        rows.append(jnp.where(lane < LATER, gate * coef, tail).astype(BF))
+        value = jnp.where(col == 7, up.astype(F32), gate * short)
+        rows.append(jnp.where(col == 15, rest.astype(F32), value).astype(BF))
     pick = rows_by_slots(jnp.concatenate(slot_codes(row_ref), axis=1))
-    out_ref[...] = dot(pick, jnp.concatenate(rows, axis=0), NN).astype(BF)
+    out_ref[...] = packed(dot(pick, jnp.concatenate(rows, axis=0), NN))
 
 
 def passed_kernel(coef_ref, tab_ref, grad_ref, acts_ref, pass_ref, part_ref):
@@ -279,11 +321,13 @@
     part_ref[:, E : 2 * E] = second.astype(BF)
 
 
-def answer_kernel(got_ref, base_ref, back_ref, part_ref, out_ref):
+def answer_kernel(got_ref, base_ref, back_ref, part_ref, names_ref, out_ref):
     width = base_ref.shape[1]
-    got = got_ref[...].astype(F32)
-    gate = got[:, LATER : LATER + 1] + got[:, LATER + 1 : LATER + 2]
-    coef = jnp.where(iota((ALL, W), 1) < LATER, got, 0.0)
+    got = unpacked(got_ref)
+    gate = got[:, 7:8] + got[:, 15:16]
+    coef = jnp.zeros((ALL, W), F32)
+    for j, mask in enumerate(row_masks(names_ref)):
+        coef = jnp.where(mask, coef + dot(got.astype(BF), section_columns(j), NT), coef)
     half = first_half(ALL, W)
     left = jnp.where(half, coef, 0.0).astype(BF)
     right = jnp.where(half, 0.0, coef).astype(BF)
@@ -371,9 +415,21 @@
     held = [
         lax.ppermute(own, "pipe", [(i, i - by) for i in range(by, pipe)]) for by in range(1, pipe)
     ] + [own]
-    table_rows, back, id_all = call(
+    near = jnp.stack([h[2 * E : 2 * E + K, 0:N] for h in held], axis=1).reshape(K * 8, N)
+    id_all = near.astype(F32)
+    place = lax.axis_index("expert")
+    for bit in range(5):
+        other = lax.ppermute(near, "expert", [(i, i ^ (1 << bit)) for i in range(E)])
+        upper = ((place >> bit) & 1) == 1
+        near = jnp.where(
+            upper,
+            jnp.concatenate([other, near], axis=0),
+            jnp.concatenate([near, other], axis=0),
+        )
+    (names,) = call(names_kernel, [((ALL, K * 8), BF)], (place.reshape(1), near), 12, smem=1)
+    table_rows, back = call(
         tables_kernel,
-        [((2 * W, width), BF), ((2 * W, inner), BF), ((K * 8, N), F32)],
+        [((2 * W, width), BF), ((2 * W, inner), BF)],
         (*held, mats),
         MIBS[1],
     )
@@ -387,37 +443,37 @@
 
     base, proj = call(
         expert_kernel,
-        [((ALL, inner), BF), ((ALL, W), BF)],
-        (arrived, mats, back),
+        [((ALL, inner), BF), ((E, 8, 128), BF)],
+        (arrived, mats, back, names),
         MIBS[2],
         scratch=[((ALL, width), BF), ((ALL, inner), BF)],
     )
-    rest = (gating, turned, id_all, section.reshape(1), grads, inputs, table_rows, back, base)
+    rest = (gating, turned, id_all, section.reshape(1), grads, inputs, table_rows, back, base, names)
     proj, rest = lax.optimization_barrier((proj, rest))
-    returned = exchange(proj.reshape(E, ROWS, W), "expert").reshape(ALL, W)
+    returned = exchange(proj, "expert")
     returned, rest = lax.optimization_barrier((returned, rest))
-    gating, turned, id_all, where, grads, inputs, table_rows, back, base = rest
+    gating, turned, id_all, where, grads, inputs, table_rows, back, base, names = rest
     (blocks,) = call(
         blocks_kernel,
         [((8, 8, K * K * N), BF)],
-        (returned, turned, id_all, gating),
+        (returned, turned, gating),
         MIBS[3],
     )
     blocks, rest = lax.optimization_barrier((blocks, rest))
     gathered = exchange(blocks, "pipe")
     gathered, rest = lax.optimization_barrier((gathered, rest))
-    gating, turned, id_all, where, grads, inputs, table_rows, back, base = rest
+    gating, turned, id_all, where, grads, inputs, table_rows, back, base, names = rest
     coef_sent, coef = call(
         solve_kernel,
-        [((ALL, W), BF), ((N, W), BF)],
+        [((E, 8, 128), BF), ((N, W), BF)],
         (where, gathered, turned, id_all, gating),
         MIBS[4],
         smem=1,
     )
     coef_sent, coef, rest = lax.optimization_barrier((coef_sent, coef, rest))
-    coef_got = exchange(coef_sent.reshape(E, ROWS, W), "expert").reshape(ALL, W)
+    coef_got = exchange(coef_sent, "expert")
     coef_got, coef, rest = lax.optimization_barrier((coef_got, coef, rest))
-    gating, turned, id_all, where, grads, inputs, table_rows, back, base = rest
+    gating, turned, id_all, where, grads, inputs, table_rows, back, base, names = rest
     passed, parts = call(
         passed_kernel,
         [((N, width), BF), ((ALL, 2 * E), BF)],
@@ -426,7 +482,7 @@
     )
     wide = 256 * steps
     (answer,) = call(
-        answer_kernel, [((ALL, wide), BF)], (coef_got, base, back, parts), MIBS[6]
+        answer_kernel, [((ALL, wide), BF)], (coef_got, base, back, parts, names), MIBS[6]
     )
     answered = exchange(answer.reshape(E, ROWS, wide), "expert").reshape(ALL, wide)
     hidden_grads, grad_router = call(

time: 253 us -> 273 us (1.079)
  waiting for transfers between devices: 75.1 us -> 96 us
  blocking collectives: 115 us -> 102 us
  starting transfers between devices: 20.4 us -> 31.3 us
    ppermute x0 -> x5, waiting for transfers between devices: none -> 75.4 us  [on_device(): other = lax.ppermute(near, 'expert', [(i, i ^ 1 << bit) for i in range(E)])]
    all_to_all x1, waiting for transfers between devices: 59 us -> 0.01 us  [exchange(): return lax.all_to_all(x, axis, split_axis=0, concat_axis=0, tiled=True)]
    all_to_all x4, blocking collectives: 115 us -> 102 us  [exchange(): return lax.all_to_all(x, axis, split_axis=0, concat_axis=0, tiled=True)]
    ppermute x0 -> x5, starting transfers between devices: none -> 10.9 us  [on_device(): other = lax.ppermute(near, 'expert', [(i, i ^ 1 << bit) for i in range(E)])]
    ppermute x7, waiting for transfers between devices: 16.1 us -> 20.6 us  [on_device(): lax.ppermute(own, 'pipe', [(i, i - by) for i in range(by, pipe)])]
    pallas_call x8 -> x9, Pallas kernels: 25.2 us -> 27.8 us  [call(): pl.pallas_call(body, out_shape=[jax.ShapeDtypeStruct(s, d) for s, d in sh...]
    unnamed x44 -> x55, local copies, waits for them, and re-layouts: 14.2 us -> 13.5 us
  transfers between devices with their start and end apart: 8 -> 13, of which waited for: 6 -> 9; matrix products, arithmetic and copies ran while one was open for 1% -> 0% of each run, Pallas kernels for 1% -> 1%
where the time goes in v4:
time: 273 us; the launch traced here: 272 us
  blocking collectives  102 us (37%)
  waiting for transfers between devices  96 us (35%)
  starting transfers between devices  31.3 us (11%)
  Pallas kernels  27.8 us (10%)
  local copies, waits for them, and re-layouts  14 us (5%)
    all_to_all x4, blocking collectives, exchange(): return lax.all_to_all(x, axis, split_axis=0, concat_axis=0, tiled=True)  102 us
    ppermute x5, waiting for transfers between devices, on_device(): other = lax.ppermute(near, 'expert', [(i, i ^ 1 << bit) for i in range(E)])  75.4 us
    pallas_call x9, Pallas kernels, call(): pl.pallas_call(body, out_shape=[jax.ShapeDtypeStruct(s, d) for s, d in sh...  27.8 us
    ppermute x7, waiting for transfers between devices, on_device(): lax.ppermute(own, 'pipe', [(i, i - by) for i in range(by, pipe)])  20.6 us
    unnamed x55, local copies, waits for them, and re-layouts  13.5 us
    all_to_all x1, starting transfers between devices, exchange(): return lax.all_to_all(x, axis, split_axis=0, concat_axis=0, tiled=True)  11.4 us
    ppermute x5, starting transfers between devices, on_device(): other = lax.ppermute(near, 'expert', [(i, i ^ 1 << bit) for i in range(E)])  10.9 us
    ppermute x7, starting transfers between devices, on_device(): lax.ppermute(own, 'pipe', [(i, i - by) for i in range(by, pipe)])  9.02 us
  transfers between devices with their start and end apart: 13, of which 9 were waited for; matrix products, arithmetic and copies ran while one was open for 0% of the time, Pallas kernels for 1%

profile of v4, /device:TPU:32, one launch (start us, length us, event | category | flops | bytes accessed | tf_op | source)
XLA Modules:
  0.0 272.4 jit_solution(13925477693543601270)
XLA Ops:
  0.6 5.6 %shard_map.94 = bf16[32,544,128]{2,1,0:T(8,128)(2,1)} custom-call(s32[2,4,64]{2,1,0:T(4,128)} %bitcast.81, bf16[128,4,1440]{2,1,0:T(4,128)(2,1)} %bitcast.86, bf16[128,1440]{1,0:T(8,128)(2,1)} %bitcast.79), custom_call_target="tpu_custom_call" | custom-call | tf_op jit(solution)/shard_map/pallas_call | solution.py:368
  6.3 11.4 %all-to-all-start = ((bf16[32,544,128]{2,1,0:T(8,128)(2,1)}), bf16[32,544,128]{2,1,0:T(8,128)(2,1)}, u32[]{:S(2)}, u32[]{:S(2)}) async-start(bf16[32,544,128]{2,1,0:T(8,128)(2,1)} %shard_map.94), calls=%async_computation | async-start | bytes 8912896 | tf_op jit(solution)/shard_map/all_to_all | solution.py:379
  18.1 1.3 collective-permute-start
  19.4 1.3 collective-permute-start.1
  20.7 1.3 collective-permute-start.2
  22.0 1.3 collective-permute-start.3
  23.3 1.3 collective-permute-start.4
  24.7 1.3 collective-permute-start.5
  26.0 4.7 %collective-permute-done.1.refs_1_ = bf16[72,1440]{1,0:T(8,128)(2,1)S(1)} collective-permute-done((bf16[72,1440]{1,0:T(8,128)(2,1)S(1)}, bf16[72,1440]{1,0:T(8,128)(2,1)S(1)}, u32[]{:S(2)}, u32[]{:S(2)}) %collective-permute-start.1) | collective-permute-done | bytes 207392 | tf_op jit(solution)/shard_map/ppermute | solution.py:416
  30.8 1.3 collective-permute-start.6
  32.1 0.6 collective-permute-done.2.refs_2_
  32.7 5.3 %collective-permute-done.3.refs_3_ = bf16[72,1440]{1,0:T(8,128)(2,1)S(1)} collective-permute-done((bf16[72,1440]{1,0:T(8,128)(2,1)S(1)}, bf16[72,1440]{1,0:T(8,128)(2,1)S(1)}, u32[]{:S(2)}, u32[]{:S(2)}) %collective-permute-start.3) | collective-permute-done | bytes 207392 | tf_op jit(solution)/shard_map/ppermute | solution.py:416
  37.9 0.7 collective-permute-done.4.refs_4_
  38.7 9.3 %collective-permute-done.5.refs_5_ = bf16[72,1440]{1,0:T(8,128)(2,1)S(1)} collective-permute-done((bf16[72,1440]{1,0:T(8,128)(2,1)S(1)}, bf16[72,1440]{1,0:T(8,128)(2,1)S(1)}, u32[]{:S(2)}, u32[]{:S(2)}) %collective-permute-start.5) | collective-permute-done | bytes 207392 | tf_op jit(solution)/shard_map/ppermute | solution.py:416
  47.9 0.7 copy-done.17
  48.7 0.7 copy-done.19
  49.4 0.4 collective-permute-start.7
  49.7 65.8 %collective-permute-done.7 = bf16[32,128]{1,0:T(8,128)(2,1)S(1)} collective-permute-done((bf16[32,128]{1,0:T(8,128)(2,1)S(1)}, bf16[32,128]{1,0:T(8,128)(2,1)S(1)}, u32[]{:S(2)}, u32[]{:S(2)}) %collective-permute-start.7) | collective-permute-done | bytes 8224 | tf_op jit(solution)/shard_map/ppermute | solution.py:422
  115.6 1.6 collective-permute-start.8
  117.2 0.3 convolution_bitcast_fusion
  117.5 2.8 %collective-permute-done.8 = bf16[64,128]{1,0:T(8,128)(2,1)S(1)} collective-permute-done((bf16[64,128]{1,0:T(8,128)(2,1)S(1)}, bf16[64,128]{1,0:T(8,128)(2,1)S(1)}, u32[]{:S(2)}, u32[]{:S(2)}) %collective-permute-start.8) | collective-permute-done | bytes 16416 | tf_op jit(solution)/shard_map/ppermute | solution.py:422
  120.3 5.4 %collective-permute-start.9 = (bf16[128,128]{1,0:T(8,128)(2,1)S(1)}, bf16[128,128]{1,0:T(8,128)(2,1)S(1)}, u32[]{:S(2)}, u32[]{:S(2)}) collective-permute-start(bf16[128,128]{1,0:T(8,128)(2,1)S(1)} %maximum_select_fusion.3), channel_id=1, source_target_pairs={{0,4},{1,5},{2,6},{3,7},{4,0},{5,1},{6,2},{7,3},{8,12},{9,13},{10,... | collective-permute-start | bytes 98312 | tf_op jit(solution)/shard_map/ppermute | solution.py:422
  125.7 2.5 collective-permute-done.9
  128.4 0.1 copy.21
  128.6 4.2 %collective-permute-done.10 = bf16[256,128]{1,0:T(8,128)(2,1)S(1)} collective-permute-done((bf16[256,128]{1,0:T(8,128)(2,1)S(1)}, bf16[256,128]{1,0:T(8,128)(2,1)S(1)}, u32[]{:S(2)}, u32[]{:S(2)}) %collective-permute-start.10) | collective-permute-done | bytes 65568 | tf_op jit(solution)/shard_map/ppermute | solution.py:422
  132.9 3.4 %collective-permute-start.11 = (bf16[512,128]{1,0:T(8,128)(2,1)S(1)}, bf16[512,128]{1,0:T(8,128)(2,1)S(1)}, u32[]{:S(2)}, u32[]{:S(2)}) collective-permute-start(bf16[512,128]{1,0:T(8,128)(2,1)S(1)} %maximum_select_fusion.1), channel_id=1, source_target_pairs={{0,16},{1,17},{2,18},{3,19},{4,20},{5,21},{6,22},{7,23},{8,24},{9,... | collective-permute-start | bytes 393224 | tf_op jit(solution)/shard_map/ppermute | solution.py:422
  136.5 2.2 copy-done
  138.7 0.9 copy-done.6
  139.6 0.9 copy-done.8
  140.6 0.9 copy-done.10
  141.5 0.9 copy-done.12
  142.5 0.9 copy-done.14
  143.4 0.9 copy-done.16
  144.3 0.9 copy-done.18
  145.3 0.9 copy-done.20
  146.2 2.6 shard_map.95
  148.9 0.6 shard_map.96.names_ref
  149.6 2.2 copy-done.1
  151.8 8.9 %shard_map.97 = (bf16[768,1440]{1,0:T(8,128)(2,1)S(1)}, bf16[32,8,128]{2,1,0:T(8,128)(2,1)S(1)}) custom-call(bf16[32,544,128]{2,1,0:T(8,128)(2,1)} %all-to-all-done.got_ref, bf16[1440,1440]{1,0:T(8,128)(2,1)S(1)} %bitcast.75, bf16[512,1440]{1,0:T(8,128)(2,1)S(1)} %get-tuple-element.141.back_ref, bf16[768,32]{1,0:T(8,128)(2,1)S(1)} %shard_map.96.names_ref), custom_call_target="tpu_custom_call" | custom-call | tf_op jit(solution)/shard_map/pallas_call | solution.py:368
  160.7 16.9 %all_to_all.25.got_ref = bf16[32,8,128]{2,1,0:T(8,128)(2,1)S(1)} all-to-all(bf16[32,8,128]{2,1,0:T(8,128)(2,1)S(1)} %get-tuple-element.79), channel_id=1, replica_groups=mesh['pipe'=8,'expert'=32] {'expert'}, dimensions={0} | all-to-all | bytes 131072 | tf_op jit(solution)/shard_map/all_to_all | solution.py:379
  177.6 1.3 shard_map.98
  178.9 11.8 %all_to_all.26.got_ref = bf16[8,8,2048]{2,1,0:T(8,128)(2,1)S(1)} all-to-all(bf16[8,8,2048]{2,1,0:T(8,128)(2,1)S(1)} %shard_map.98), channel_id=1, replica_groups=mesh['pipe'=8,'expert'=32] {'pipe'}, dimensions={0} | all-to-all | bytes 524288 | tf_op jit(solution)/shard_map/all_to_all | solution.py:379
  190.7 1.2 shard_map.99
  192.0 13.1 %all_to_all.27.got_ref = bf16[32,8,128]{2,1,0:T(8,128)(2,1)S(1)} all-to-all(bf16[32,8,128]{2,1,0:T(8,128)(2,1)S(1)} %get-tuple-element.125), channel_id=1, replica_groups=mesh['pipe'=8,'expert'=32] {'expert'}, dimensions={0} | all-to-all | bytes 131072 | tf_op jit(solution)/shard_map/all_to_all | solution.py:379
  205.1 2.0 shard_map.100
  207.1 2.3 shard_map.101
  209.4 59.9 %all_to_all.28 = bf16[32,24,1536]{2,1,0:T(8,128)(2,1)S(1)} all-to-all(bf16[32,24,1536]{2,1,0:T(8,128)(2,1)S(1)} %bitcast.76), channel_id=1, replica_groups=mesh['pipe'=8,'expert'=32] {'expert'}, dimensions={0} | all-to-all | bytes 4718592 | tf_op jit(solution)/shard_map/all_to_all | solution.py:379
  269.2 3.2 %shard_map.102 = (bf16[128,4,1440]{2,1,0:T(4,128)(2,1)}, f32[32,45]{1,0:T(8,128)}) custom-call(bf16[768,1536]{1,0:T(8,128)(2,1)S(1)} %bitcast.77, s32[2,4,64]{2,1,0:T(4,128)S(1)} %bitcast.85), custom_call_target="tpu_custom_call" | custom-call | tf_op jit(solution)/shard_map/pallas_call | solution.py:368
  (69 shorter events, 1.1 us)
Async XLA Ops:
  6.3 11.4 %copy-start.21 = (s32[1,2,64,4]{2,3,1,0:T(4,128)S(1)}, s32[1,2,64,4]{2,3,1,0:T(4,128)}, u32[]{:S(2)}) copy-start(s32[1,2,64,4]{2,3,1,0:T(4,128)} %param.9) | copy-start | bytes 6148
  6.3 11.5 %copy-start.23 = (s32[1,2]{1,0:T(1,128)S(1)}, s32[1,2]{1,0:T(1,128)}, u32[]{:S(2)}) copy-start(s32[1,2]{1,0:T(1,128)} %param.10) | copy-start | bytes 28
  6.3 11.7 %copy-start.22 = (bf16[1,2,1440,32]{2,3,1,0:T(8,128)(2,1)S(1)}, bf16[1,2,1440,32]{2,3,1,0:T(8,128)(2,1)}, u32[]{:S(2)}) copy-start(bf16[1,2,1440,32]{2,3,1,0:T(8,128)(2,1)} %param.11) | copy-start | bytes 552964
  6.3 110.9 %copy-start.2 = (bf16[1,2,64,1440]{3,2,1,0:T(8,128)(2,1)S(1)}, bf16[1,2,64,1440]{3,2,1,0:T(8,128)(2,1)}, u32[]{:S(2)}) copy-start(bf16[1,2,64,1440]{3,2,1,0:T(8,128)(2,1)} %param.7) | copy-start | bytes 1105924
  6.3 143.3 %all-to-all-start = ((bf16[32,544,128]{2,1,0:T(8,128)(2,1)}), bf16[32,544,128]{2,1,0:T(8,128)(2,1)}, u32[]{:S(2)}, u32[]{:S(2)}) async-start(bf16[32,544,128]{2,1,0:T(8,128)(2,1)} %shard_map.94), calls=%async_computation | async-start | bytes 8912896 | tf_op jit(solution)/shard_map/all_to_all | solution.py:379
  18.1 118.3 %copy-start.5 = (bf16[72,1440]{1,0:T(8,128)(2,1)}, bf16[72,1440]{1,0:T(8,128)(2,1)S(1)}, u32[]{:S(2)}) copy-start(bf16[72,1440]{1,0:T(8,128)(2,1)S(1)} %fusion.1.refs_7_) | copy-start | bytes 622084
  18.1 6.6 %collective-permute-start = (bf16[72,1440]{1,0:T(8,128)(2,1)S(1)}, bf16[72,1440]{1,0:T(8,128)(2,1)S(1)}, u32[]{:S(2)}, u32[]{:S(2)}) collective-permute-start(bf16[72,1440]{1,0:T(8,128)(2,1)S(1)} %fusion.1.refs_7_), channel_id=1, source_target_pairs={{32,0},{64,32},{96,64},{128,96},{160,128},{192,160},{224,192},{33,... | collective-permute-start | bytes 622088 | tf_op jit(solution)/shard_map/ppermute | solution.py:416
  19.4 11.3 %collective-permute-start.1 = (bf16[72,1440]{1,0:T(8,128)(2,1)S(1)}, bf16[72,1440]{1,0:T(8,128)(2,1)S(1)}, u32[]{:S(2)}, u32[]{:S(2)}) collective-permute-start(bf16[72,1440]{1,0:T(8,128)(2,1)S(1)} %fusion.1.refs_7_), channel_id=1, source_target_pairs={{64,0},{96,32},{128,64},{160,96},{192,128},{224,160},{65,1},{97,33... | collective-permute-start | bytes 622088 | tf_op jit(solution)/shard_map/ppermute | solution.py:416
  20.7 11.9 %collective-permute-start.2 = (bf16[72,1440]{1,0:T(8,128)(2,1)S(1)}, bf16[72,1440]{1,0:T(8,128)(2,1)S(1)}, u32[]{:S(2)}, u32[]{:S(2)}) collective-permute-start(bf16[72,1440]{1,0:T(8,128)(2,1)S(1)} %fusion.1.refs_7_), channel_id=1, source_target_pairs={{96,0},{128,32},{160,64},{192,96},{224,128},{97,1},{129,33},{161,6... | collective-permute-start | bytes 622088 | tf_op jit(solution)/shard_map/ppermute | solution.py:416
  22.0 15.9 %collective-permute-start.3 = (bf16[72,1440]{1,0:T(8,128)(2,1)S(1)}, bf16[72,1440]{1,0:T(8,128)(2,1)S(1)}, u32[]{:S(2)}, u32[]{:S(2)}) collective-permute-start(bf16[72,1440]{1,0:T(8,128)(2,1)S(1)} %fusion.1.refs_7_), channel_id=1, source_target_pairs={{128,0},{160,32},{192,64},{224,96},{129,1},{161,33},{193,65},{225,... | collective-permute-start | bytes 622088 | tf_op jit(solution)/shard_map/ppermute | solution.py:416
  23.3 15.3 %collective-permute-start.4 = (bf16[72,1440]{1,0:T(8,128)(2,1)S(1)}, bf16[72,1440]{1,0:T(8,128)(2,1)S(1)}, u32[]{:S(2)}, u32[]{:S(2)}) collective-permute-start(bf16[72,1440]{1,0:T(8,128)(2,1)S(1)} %fusion.1.refs_7_), channel_id=1, source_target_pairs={{160,0},{192,32},{224,64},{161,1},{193,33},{225,65},{162,2},{194,3... | collective-permute-start | bytes 622088 | tf_op jit(solution)/shard_map/ppermute | solution.py:416
  24.7 111.7 %copy-start.7 = (bf16[72,1440]{1,0:T(8,128)(2,1)}, bf16[72,1440]{1,0:T(8,128)(2,1)S(1)}, u32[]{:S(2)}) copy-start(bf16[72,1440]{1,0:T(8,128)(2,1)S(1)} %collective-permute-done.refs_0_) | copy-start | bytes 622084
  24.7 23.2 %collective-permute-start.5 = (bf16[72,1440]{1,0:T(8,128)(2,1)S(1)}, bf16[72,1440]{1,0:T(8,128)(2,1)S(1)}, u32[]{:S(2)}, u32[]{:S(2)}) collective-permute-start(bf16[72,1440]{1,0:T(8,128)(2,1)S(1)} %fusion.1.refs_7_), channel_id=1, source_target_pairs={{192,0},{224,32},{193,1},{225,33},{194,2},{226,34},{195,3},{227,35... | collective-permute-start | bytes 622088 | tf_op jit(solution)/shard_map/ppermute | solution.py:416
  30.8 105.7 %copy-start.9 = (bf16[72,1440]{1,0:T(8,128)(2,1)}, bf16[72,1440]{1,0:T(8,128)(2,1)S(1)}, u32[]{:S(2)}) copy-start(bf16[72,1440]{1,0:T(8,128)(2,1)S(1)} %collective-permute-done.1.refs_1_) | copy-start | bytes 622084
  30.8 17.9 %collective-permute-start.6 = (bf16[72,1440]{1,0:T(8,128)(2,1)S(1)}, bf16[72,1440]{1,0:T(8,128)(2,1)S(1)}, u32[]{:S(2)}, u32[]{:S(2)}) collective-permute-start(bf16[72,1440]{1,0:T(8,128)(2,1)S(1)} %fusion.1.refs_7_), channel_id=1, source_target_pairs={{224,0},{225,1},{226,2},{227,3},{228,4},{229,5},{230,6},{231,7},{2... | collective-permute-start | bytes 622088 | tf_op jit(solution)/shard_map/ppermute | solution.py:416
  32.6 103.8 %copy-start.11 = (bf16[72,1440]{1,0:T(8,128)(2,1)}, bf16[72,1440]{1,0:T(8,128)(2,1)S(1)}, u32[]{:S(2)}) copy-start(bf16[72,1440]{1,0:T(8,128)(2,1)S(1)} %collective-permute-done.2.refs_2_) | copy-start | bytes 622084
  37.9 98.5 %copy-start.13 = (bf16[72,1440]{1,0:T(8,128)(2,1)}, bf16[72,1440]{1,0:T(8,128)(2,1)S(1)}, u32[]{:S(2)}) copy-start(bf16[72,1440]{1,0:T(8,128)(2,1)S(1)} %collective-permute-done.3.refs_3_) | copy-start | bytes 622084
  38.7 97.8 %copy-start.15 = (bf16[72,1440]{1,0:T(8,128)(2,1)}, bf16[72,1440]{1,0:T(8,128)(2,1)S(1)}, u32[]{:S(2)}) copy-start(bf16[72,1440]{1,0:T(8,128)(2,1)S(1)} %collective-permute-done.4.refs_4_) | copy-start | bytes 622084
  47.9 0.7 copy-start.17
  48.6 0.7 copy-start.19
  49.4 66.2 %collective-permute-start.7 = (bf16[32,128]{1,0:T(8,128)(2,1)S(1)}, bf16[32,128]{1,0:T(8,128)(2,1)S(1)}, u32[]{:S(2)}, u32[]{:S(2)}) collective-permute-start(bf16[32,128]{1,0:T(8,128)(2,1)S(1)} %get-tuple-element.152), channel_id=1, source_target_pairs={{0,1},{1,0},{2,3},{3,2},{4,5},{5,4},{6,7},{7,6},{8,9},{9,8},{10,11... | collective-permute-start | bytes 24584 | tf_op jit(solution)/shard_map/ppermute | solution.py:422
  115.6 4.7 %collective-permute-start.8 = (bf16[64,128]{1,0:T(8,128)(2,1)S(1)}, bf16[64,128]{1,0:T(8,128)(2,1)S(1)}, u32[]{:S(2)}, u32[]{:S(2)}) collective-permute-start(bf16[64,128]{1,0:T(8,128)(2,1)S(1)} %maximum_select_fusion.4), channel_id=1, source_target_pairs={{0,2},{1,3},{2,0},{3,1},{4,6},{5,7},{6,4},{7,5},{8,10},{9,11},{10,... | collective-permute-start | bytes 49160 | tf_op jit(solution)/shard_map/ppermute | solution.py:422
  120.3 7.9 %collective-permute-start.9 = (bf16[128,128]{1,0:T(8,128)(2,1)S(1)}, bf16[128,128]{1,0:T(8,128)(2,1)S(1)}, u32[]{:S(2)}, u32[]{:S(2)}) collective-permute-start(bf16[128,128]{1,0:T(8,128)(2,1)S(1)} %maximum_select_fusion.3), channel_id=1, source_target_pairs={{0,4},{1,5},{2,6},{3,7},{4,0},{5,1},{6,2},{7,3},{8,12},{9,13},{10,... | collective-permute-start | bytes 98312 | tf_op jit(solution)/shard_map/ppermute | solution.py:422
  128.3 4.6 %collective-permute-start.10 = (bf16[256,128]{1,0:T(8,128)(2,1)S(1)}, bf16[256,128]{1,0:T(8,128)(2,1)S(1)}, u32[]{:S(2)}, u32[]{:S(2)}) collective-permute-start(bf16[256,128]{1,0:T(8,128)(2,1)S(1)} %maximum_select_fusion.2), channel_id=1, source_target_pairs={{0,8},{1,9},{2,10},{3,11},{4,12},{5,13},{6,14},{7,15},{8,0},{9,1},... | collective-permute-start | bytes 196616 | tf_op jit(solution)/shard_map/ppermute | solution.py:422
  132.9 16.0 %collective-permute-start.11 = (bf16[512,128]{1,0:T(8,128)(2,1)S(1)}, bf16[512,128]{1,0:T(8,128)(2,1)S(1)}, u32[]{:S(2)}, u32[]{:S(2)}) collective-permute-start(bf16[512,128]{1,0:T(8,128)(2,1)S(1)} %maximum_select_fusion.1), channel_id=1, source_target_pairs={{0,16},{1,17},{2,18},{3,19},{4,20},{5,21},{6,22},{7,23},{8,24},{9,... | collective-permute-start | bytes 393224 | tf_op jit(solution)/shard_map/ppermute | solution.py:422
  136.5 2.3 copy-start
  138.7 0.9 copy-start.6
  139.6 0.9 copy-start.8
  140.6 0.9 copy-start.10
  141.5 0.9 copy-start.12
  142.5 0.9 copy-start.14
  143.4 0.9 copy-start.16
  144.3 0.9 copy-start.18
  145.3 0.9 copy-start.20
  149.6 2.3 copy-start.1
  151.8 53.3 %copy-start.3 = (bf16[1,2,64,1440]{3,2,1,0:T(8,128)(2,1)S(1)}, bf16[1,2,64,1440]{3,2,1,0:T(8,128)(2,1)}, u32[]{:S(2)}) copy-start(bf16[1,2,64,1440]{3,2,1,0:T(8,128)(2,1)} %param.7) | copy-start | bytes 1105924
  151.8 53.3 %copy-start.4 = (bf16[2,64,1440]{2,1,0:T(8,128)(2,1)S(1)}, bf16[2,64,1440]{2,1,0:T(8,128)(2,1)}, u32[]{:S(2)}) copy-start(bf16[2,64,1440]{2,1,0:T(8,128)(2,1)} %param.13) | copy-start | bytes 1105924

commit v5 on v3

--- a/solution.py
+++ b/solution.py
@@ -248,16 +248,24 @@
         wide = dot(high[:, cut], spread, TN) + dot(low[:, cut], spread, TN)
         coef = jnp.where(masks[j], wide, coef)
     coef_ref[...] = coef.astype(BF)
-    lane = iota((N, W), 1)
+    same = one(iota((32, 32), 0) == iota((32, 32), 1))
+    tall_high = jnp.concatenate([high[:, j * N : (j + 1) * N] for j in range(K)], axis=0)
+    tall_low = jnp.concatenate([low[:, j * N : (j + 1) * N] for j in range(K)], axis=0)
+    short = dot(tall_high, same, TN) + dot(tall_low, same, TN)
+    names = dot(ids_ref[...].astype(BF), same, TN)
+    col = iota((N, 32), 1)
     rows = []
     for k in range(K):
         gate = gate_ref[:, k : k + 1]
         up, rest = split(gate)
-        tail = jnp.where(lane == LATER, up.astype(F32), rest.astype(F32))
-        tail = jnp.where(lane < LATER + 2, tail, 0.0)
-        rows.append(jnp.where(lane < LATER, gate * coef, tail).astype(BF))
+        value = jnp.where(col == 7, up.astype(F32), gate * short)
+        value = jnp.where(col == 15, rest.astype(F32), value)
+        rows.append(jnp.concatenate([value, names], axis=1).astype(BF))
     pick = rows_by_slots(jnp.concatenate(slot_codes(row_ref), axis=1))
-    out_ref[...] = dot(pick, jnp.concatenate(rows, axis=0), NN).astype(BF)
+    sent = dot(pick, jnp.concatenate(rows, axis=0), NN).reshape(E, ROWS, 64)
+    out_ref[:, :, 0:64] = sent[:, 0:16].astype(BF)
+    rest = jnp.concatenate([sent[:, 16:24], jnp.zeros((E, 8, 64), F32)], axis=1)
+    out_ref[:, :, 64:128] = rest.astype(BF)
 
 
 def passed_kernel(coef_ref, tab_ref, grad_ref, acts_ref, pass_ref, part_ref):
@@ -269,21 +277,32 @@
     width = acts_ref.shape[1]
     router = (dot(acts_ref[...], own, TN) / T).astype(BF)
     each = width // E
-    row, col = iota((ALL, width), 0), iota((ALL, width), 1)
-    peer = divided(row, ROWS)
-    inner = row - ROWS * peer
-    source = peer * each + inner
-    first = dot(one(source == col), router, NN)
-    second = dot(one((source + ROWS == col) & (inner + ROWS < each)), router, NN)
-    part_ref[:, 0:E] = first.astype(BF)
-    part_ref[:, E : 2 * E] = second.astype(BF)
+    ahead = jnp.concatenate([router[ROWS:], router[:ROWS]], axis=0)
+    col = iota((ALL, width), 1)
+    peer = divided(iota((ALL, 1), 0), ROWS)
+    source = iota((ALL, 1), 0) + (each - ROWS) * peer
+    select = one(source == col)
+    part_ref[:, 0:E] = dot(select, router, NN).astype(BF)
+    part_ref[:, E : 2 * E] = dot(select, ahead, NN).astype(BF)
+
+
+def section_columns(j):
+    row, col = iota((W, 32), 0), iota((W, 32), 1)
+    return one((row < LATER) & ((row >> 5) + 8 * j == col))
 
 
 def answer_kernel(got_ref, base_ref, back_ref, part_ref, out_ref):
     width = base_ref.shape[1]
     got = got_ref[...].astype(F32)
-    gate = got[:, LATER : LATER + 1] + got[:, LATER + 1 : LATER + 2]
-    coef = jnp.where(iota((ALL, W), 1) < LATER, got, 0.0)
+    got = jnp.concatenate([got[:, :, 0:64], got[:, 0:8, 64:128]], axis=1).reshape(ALL, 64)
+    gate = got[:, 7:8] + got[:, 15:16]
+    got = got.astype(BF)
+    spread = one((iota((8, W), 1) >> 5) == iota((8, W), 0))
+    lane = (iota((ALL, W), 1) & (E - 1)).astype(F32)
+    coef = jnp.zeros((ALL, W), F32)
+    for j in range(K):
+        named = dot(got[:, 32 + 8 * j : 40 + 8 * j], spread, NN) == lane
+        coef = jnp.where(named, coef + dot(got[:, 0:32], section_columns(j), NT), coef)
     half = first_half(ALL, W)
     left = jnp.where(half, coef, 0.0).astype(BF)
     right = jnp.where(half, 0.0, coef).astype(BF)
@@ -409,13 +428,13 @@
     gating, turned, id_all, where, grads, inputs, table_rows, back, base = rest
     coef_sent, coef = call(
         solve_kernel,
-        [((ALL, W), BF), ((N, W), BF)],
+        [((E, 16, 128), BF), ((N, W), BF)],
         (where, gathered, turned, id_all, gating),
         MIBS[4],
         smem=1,
     )
     coef_sent, coef, rest = lax.optimization_barrier((coef_sent, coef, rest))
-    coef_got = exchange(coef_sent.reshape(E, ROWS, W), "expert").reshape(ALL, W)
+    coef_got = exchange(coef_sent, "expert")
     coef_got, coef, rest = lax.optimization_barrier((coef_got, coef, rest))
     gating, turned, id_all, where, grads, inputs, table_rows, back, base = rest
     passed, parts = call(

time: 253 us -> 249 us (0.984)
  blocking collectives: 115 us -> 109 us
    all_to_all x4, blocking collectives: 115 us -> 109 us  [exchange(): return lax.all_to_all(x, axis, split_axis=0, concat_axis=0, tiled=True)]
where the time goes in v5:
time: 249 us; the launch traced here: 248 us
  blocking collectives  109 us (44%)
  waiting for transfers between devices  75.1 us (30%)
  Pallas kernels  26.3 us (11%)
  starting transfers between devices  20.4 us (8%)
  local copies, waits for them, and re-layouts  14.7 us (6%)
    all_to_all x4, blocking collectives, exchange(): return lax.all_to_all(x, axis, split_axis=0, concat_axis=0, tiled=True)  109 us
    all_to_all x1, waiting for transfers between devices, exchange(): return lax.all_to_all(x, axis, split_axis=0, concat_axis=0, tiled=True)  59 us
    pallas_call x8, Pallas kernels, call(): pl.pallas_call(body, out_shape=[jax.ShapeDtypeStruct(s, d) for s, d in sh...  26.3 us
    ppermute x7, waiting for transfers between devices, on_device(): lax.ppermute(own, 'pipe', [(i, i - by) for i in range(by, pipe)])  16.1 us
    unnamed x44, local copies, waits for them, and re-layouts  14.2 us
    all_to_all x1, starting transfers between devices, exchange(): return lax.all_to_all(x, axis, split_axis=0, concat_axis=0, tiled=True)  11.4 us
    ppermute x7, starting transfers between devices, on_device(): lax.ppermute(own, 'pipe', [(i, i - by) for i in range(by, pipe)])  9.02 us
  transfers between devices with their start and end apart: 8, of which 6 were waited for; matrix products, arithmetic and copies ran while one was open for 1% of the time, Pallas kernels for 1%

profile of v5, /device:TPU:32, one launch (start us, length us, event | category | flops | bytes accessed | tf_op | source)
XLA Modules:
  0.0 247.8 jit_solution(18210444839518473095)
XLA Ops:
  0.6 5.6 %shard_map.94 = bf16[32,544,128]{2,1,0:T(8,128)(2,1)} custom-call(s32[2,4,64]{2,1,0:T(4,128)} %bitcast.52, bf16[128,4,1440]{2,1,0:T(4,128)(2,1)} %bitcast.57, bf16[128,1440]{1,0:T(8,128)(2,1)} %bitcast.49), custom_call_target="tpu_custom_call" | custom-call | tf_op jit(solution)/shard_map/pallas_call | solution.py:343
  6.3 11.4 %all-to-all-start = ((bf16[32,544,128]{2,1,0:T(8,128)(2,1)}), bf16[32,544,128]{2,1,0:T(8,128)(2,1)}, u32[]{:S(2)}, u32[]{:S(2)}) async-start(bf16[32,544,128]{2,1,0:T(8,128)(2,1)} %shard_map.94), calls=%async_computation | async-start | bytes 8912896 | tf_op jit(solution)/shard_map/all_to_all | solution.py:354
  17.7 0.1 convert_element_type.13
  17.8 0.1 broadcast_in_dim.64
  17.9 0.1 broadcast_in_dim.65
  18.0 0.1 bitcast_select_fusion
  18.1 1.3 collective-permute-start
  19.4 1.3 collective-permute-start.1
  20.7 1.3 collective-permute-start.2
  22.0 1.3 collective-permute-start.3
  23.3 1.3 collective-permute-start.4
  24.6 0.3 convolution_bitcast_fusion
  25.0 0.1 copy.16
  25.1 0.1 div.11
  25.2 0.7 copy-done.7
  25.9 1.3 collective-permute-start.5
  27.2 3.6 %collective-permute-done.1.refs_1_ = bf16[72,1440]{1,0:T(8,128)(2,1)S(1)} collective-permute-done((bf16[72,1440]{1,0:T(8,128)(2,1)S(1)}, bf16[72,1440]{1,0:T(8,128)(2,1)S(1)}, u32[]{:S(2)}, u32[]{:S(2)}) %collective-permute-start.1) | collective-permute-done | bytes 207392 | tf_op jit(solution)/shard_map/ppermute | solution.py:391
  30.7 0.7 copy-done.9
  31.4 1.3 collective-permute-start.6
  32.7 0.7 bitcast_divide_fusion.gate_ref
  33.4 0.7 copy-done.11
  34.1 3.8 %collective-permute-done.3.refs_3_ = bf16[72,1440]{1,0:T(8,128)(2,1)S(1)} collective-permute-done((bf16[72,1440]{1,0:T(8,128)(2,1)S(1)}, bf16[72,1440]{1,0:T(8,128)(2,1)S(1)}, u32[]{:S(2)}, u32[]{:S(2)}) %collective-permute-start.3) | collective-permute-done | bytes 207392 | tf_op jit(solution)/shard_map/ppermute | solution.py:391
  37.9 0.7 copy-done.13
  38.6 0.1 collective-permute-done.4.refs_4_
  38.6 0.7 copy-done.15
  39.3 8.6 %collective-permute-done.5.refs_5_ = bf16[72,1440]{1,0:T(8,128)(2,1)S(1)} collective-permute-done((bf16[72,1440]{1,0:T(8,128)(2,1)S(1)}, bf16[72,1440]{1,0:T(8,128)(2,1)S(1)}, u32[]{:S(2)}, u32[]{:S(2)}) %collective-permute-start.5) | collective-permute-done | bytes 207392 | tf_op jit(solution)/shard_map/ppermute | solution.py:391
  47.9 0.1 collective-permute-done.6.refs_6_
  48.0 2.3 copy-done
  50.3 0.9 copy-done.5
  51.2 0.9 copy-done.8
  52.1 0.9 copy-done.10
  53.1 0.9 copy-done.12
  54.0 0.9 copy-done.14
  55.0 0.9 copy-done.16
  55.9 2.6 %shard_map.95 = (bf16[512,1440]{1,0:T(8,128)(2,1)S(1)}, bf16[512,1440]{1,0:T(8,128)(2,1)S(1)}, f32[32,128]{1,0:T(8,128)S(1)}) custom-call(bf16[72,1440]{1,0:T(8,128)(2,1)S(1)} %copy-done.8, bf16[72,1440]{1,0:T(8,128)(2,1)S(1)} %copy-done.10, bf16[72,1440]{1,0:T(8,128)(2,1)S(1)} %copy-done.12, bf16[72,1440]{1,0:T(8,128)(2,1)S(1)} %copy-done.14, ...), custom_call_target="tpu_custom_call" | custom-call | tf_op jit(solution)/shard_map/pallas_call | solution.py:343
  58.6 0.6 copy-done.18
  59.2 59.0 %all-to-all-done.got_ref = bf16[32,544,128]{2,1,0:T(8,128)(2,1)} async-done(((bf16[32,544,128]{2,1,0:T(8,128)(2,1)}), bf16[32,544,128]{2,1,0:T(8,128)(2,1)}, u32[]{:S(2)}, u32[]{:S(2)}) %all-to-all-start) | async-done | bytes 4456480 | tf_op jit(solution)/shard_map/all_to_all | solution.py:354
  118.2 2.3 copy-done.1
  120.4 7.5 %shard_map.96 = (bf16[768,1440]{1,0:T(8,128)(2,1)S(1)}, bf16[768,256]{1,0:T(8,128)(2,1)S(1)}) custom-call(bf16[32,544,128]{2,1,0:T(8,128)(2,1)} %all-to-all-done.got_ref, bf16[1440,1440]{1,0:T(8,128)(2,1)S(1)} %bitcast.44, bf16[512,1440]{1,0:T(8,128)(2,1)S(1)} %get-tuple-element.132.back_ref), custom_call_target="tpu_custom_call" | custom-call | tf_op jit(solution)/shard_map/pallas_call | solution.py:343
  128.0 23.5 %all_to_all.25 = bf16[32,24,256]{2,1,0:T(8,128)(2,1)S(1)} all-to-all(bf16[32,24,256]{2,1,0:T(8,128)(2,1)S(1)} %bitcast.51), channel_id=1, replica_groups=mesh['pipe'=8,'expert'=32] {'expert'}, dimensions={0} | all-to-all | bytes 786432 | tf_op jit(solution)/shard_map/all_to_all | solution.py:354
  151.5 1.6 shard_map.97
  153.1 11.8 %all_to_all.26.got_ref = bf16[8,8,2048]{2,1,0:T(8,128)(2,1)S(1)} all-to-all(bf16[8,8,2048]{2,1,0:T(8,128)(2,1)S(1)} %shard_map.97), channel_id=1, replica_groups=mesh['pipe'=8,'expert'=32] {'pipe'}, dimensions={0} | all-to-all | bytes 524288 | tf_op jit(solution)/shard_map/all_to_all | solution.py:354
  164.9 1.2 shard_map.98
  166.1 14.2 %all_to_all.27.got_ref = bf16[32,16,128]{2,1,0:T(8,128)(2,1)S(1)} all-to-all(bf16[32,16,128]{2,1,0:T(8,128)(2,1)S(1)} %get-tuple-element.117), channel_id=1, replica_groups=mesh['pipe'=8,'expert'=32] {'expert'}, dimensions={0} | all-to-all | bytes 262144 | tf_op jit(solution)/shard_map/all_to_all | solution.py:354
  180.4 1.9 shard_map.99
  182.3 2.6 %shard_map.100 = bf16[768,1536]{1,0:T(8,128)(2,1)S(1)} custom-call(bf16[32,16,128]{2,1,0:T(8,128)(2,1)S(1)} %all_to_all.27.got_ref, bf16[768,1440]{1,0:T(8,128)(2,1)S(1)} %get-tuple-element.131.base_ref, bf16[512,1440]{1,0:T(8,128)(2,1)S(1)} %get-tuple-element.132.back_ref, bf16[768,64]{1,0:T(8,128)(2,1)S(1)} %get-tuple-element.133.part_ref), custom_call_target="tpu_custom_call" | custom-call | tf_op jit(solution)/shard_map/pallas_call | solution.py:343
  184.8 59.8 %all_to_all.28 = bf16[32,24,1536]{2,1,0:T(8,128)(2,1)S(1)} all-to-all(bf16[32,24,1536]{2,1,0:T(8,128)(2,1)S(1)} %bitcast.45), channel_id=1, replica_groups=mesh['pipe'=8,'expert'=32] {'expert'}, dimensions={0} | all-to-all | bytes 4718592 | tf_op jit(solution)/shard_map/all_to_all | solution.py:354
  244.6 3.2 %shard_map.101 = (bf16[128,4,1440]{2,1,0:T(4,128)(2,1)}, f32[32,45]{1,0:T(8,128)}) custom-call(bf16[768,1536]{1,0:T(8,128)(2,1)S(1)} %bitcast.46, s32[2,4,64]{2,1,0:T(4,128)S(1)} %bitcast.56), custom_call_target="tpu_custom_call" | custom-call | tf_op jit(solution)/shard_map/pallas_call | solution.py:343
  (39 shorter events, 0.2 us)
Async XLA Ops:
  6.2 11.4 %copy-start.17 = (s32[1,2,64,4]{2,3,1,0:T(4,128)S(1)}, s32[1,2,64,4]{2,3,1,0:T(4,128)}, u32[]{:S(2)}) copy-start(s32[1,2,64,4]{2,3,1,0:T(4,128)} %param.9) | copy-start | bytes 6148
  6.2 11.5 %copy-start.21 = (s32[1,2]{1,0:T(1,128)S(1)}, s32[1,2]{1,0:T(1,128)}, u32[]{:S(2)}) copy-start(s32[1,2]{1,0:T(1,128)} %param.10) | copy-start | bytes 28
  6.3 11.7 %copy-start.20 = (bf16[1,2,1440,32]{2,3,1,0:T(8,128)(2,1)S(1)}, bf16[1,2,1440,32]{2,3,1,0:T(8,128)(2,1)}, u32[]{:S(2)}) copy-start(bf16[1,2,1440,32]{2,3,1,0:T(8,128)(2,1)} %param.11) | copy-start | bytes 552964
  6.3 18.4 %copy-start.2 = (bf16[1,2,64,1440]{3,2,1,0:T(8,128)(2,1)S(1)}, bf16[1,2,64,1440]{3,2,1,0:T(8,128)(2,1)}, u32[]{:S(2)}) copy-start(bf16[1,2,64,1440]{3,2,1,0:T(8,128)(2,1)} %param.7) | copy-start | bytes 1105924
  6.3 111.9 %all-to-all-start = ((bf16[32,544,128]{2,1,0:T(8,128)(2,1)}), bf16[32,544,128]{2,1,0:T(8,128)(2,1)}, u32[]{:S(2)}, u32[]{:S(2)}) async-start(bf16[32,544,128]{2,1,0:T(8,128)(2,1)} %shard_map.94), calls=%async_computation | async-start | bytes 8912896 | tf_op jit(solution)/shard_map/all_to_all | solution.py:354
  18.1 29.9 %copy-start.4 = (bf16[72,1440]{1,0:T(8,128)(2,1)}, bf16[72,1440]{1,0:T(8,128)(2,1)S(1)}, u32[]{:S(2)}) copy-start(bf16[72,1440]{1,0:T(8,128)(2,1)S(1)} %fusion.1.refs_7_) | copy-start | bytes 622084
  18.1 7.1 %collective-permute-start = (bf16[72,1440]{1,0:T(8,128)(2,1)S(1)}, bf16[72,1440]{1,0:T(8,128)(2,1)S(1)}, u32[]{:S(2)}, u32[]{:S(2)}) collective-permute-start(bf16[72,1440]{1,0:T(8,128)(2,1)S(1)} %fusion.1.refs_7_), channel_id=1, source_target_pairs={{32,0},{64,32},{96,64},{128,96},{160,128},{192,160},{224,192},{33,... | collective-permute-start | bytes 622088 | tf_op jit(solution)/shard_map/ppermute | solution.py:391
  19.4 11.3 %collective-permute-start.1 = (bf16[72,1440]{1,0:T(8,128)(2,1)S(1)}, bf16[72,1440]{1,0:T(8,128)(2,1)S(1)}, u32[]{:S(2)}, u32[]{:S(2)}) collective-permute-start(bf16[72,1440]{1,0:T(8,128)(2,1)S(1)} %fusion.1.refs_7_), channel_id=1, source_target_pairs={{64,0},{96,32},{128,64},{160,96},{192,128},{224,160},{65,1},{97,33... | collective-permute-start | bytes 622088 | tf_op jit(solution)/shard_map/ppermute | solution.py:391
  20.7 12.7 %collective-permute-start.2 = (bf16[72,1440]{1,0:T(8,128)(2,1)S(1)}, bf16[72,1440]{1,0:T(8,128)(2,1)S(1)}, u32[]{:S(2)}, u32[]{:S(2)}) collective-permute-start(bf16[72,1440]{1,0:T(8,128)(2,1)S(1)} %fusion.1.refs_7_), channel_id=1, source_target_pairs={{96,0},{128,32},{160,64},{192,96},{224,128},{97,1},{129,33},{161,6... | collective-permute-start | bytes 622088 | tf_op jit(solution)/shard_map/ppermute | solution.py:391
  22.0 15.9 %collective-permute-start.3 = (bf16[72,1440]{1,0:T(8,128)(2,1)S(1)}, bf16[72,1440]{1,0:T(8,128)(2,1)S(1)}, u32[]{:S(2)}, u32[]{:S(2)}) collective-permute-start(bf16[72,1440]{1,0:T(8,128)(2,1)S(1)} %fusion.1.refs_7_), channel_id=1, source_target_pairs={{128,0},{160,32},{192,64},{224,96},{129,1},{161,33},{193,65},{225,... | collective-permute-start | bytes 622088 | tf_op jit(solution)/shard_map/ppermute | solution.py:391
  23.3 15.3 %collective-permute-start.4 = (bf16[72,1440]{1,0:T(8,128)(2,1)S(1)}, bf16[72,1440]{1,0:T(8,128)(2,1)S(1)}, u32[]{:S(2)}, u32[]{:S(2)}) collective-permute-start(bf16[72,1440]{1,0:T(8,128)(2,1)S(1)} %fusion.1.refs_7_), channel_id=1, source_target_pairs={{160,0},{192,32},{224,64},{161,1},{193,33},{225,65},{162,2},{194,3... | collective-permute-start | bytes 622088 | tf_op jit(solution)/shard_map/ppermute | solution.py:391
  25.2 0.7 copy-start.7
  25.9 22.0 %collective-permute-start.5 = (bf16[72,1440]{1,0:T(8,128)(2,1)S(1)}, bf16[72,1440]{1,0:T(8,128)(2,1)S(1)}, u32[]{:S(2)}, u32[]{:S(2)}) collective-permute-start(bf16[72,1440]{1,0:T(8,128)(2,1)S(1)} %fusion.1.refs_7_), channel_id=1, source_target_pairs={{192,0},{224,32},{193,1},{225,33},{194,2},{226,34},{195,3},{227,35... | collective-permute-start | bytes 622088 | tf_op jit(solution)/shard_map/ppermute | solution.py:391
  30.7 0.7 copy-start.9
  31.4 16.6 %collective-permute-start.6 = (bf16[72,1440]{1,0:T(8,128)(2,1)S(1)}, bf16[72,1440]{1,0:T(8,128)(2,1)S(1)}, u32[]{:S(2)}, u32[]{:S(2)}) collective-permute-start(bf16[72,1440]{1,0:T(8,128)(2,1)S(1)} %fusion.1.refs_7_), channel_id=1, source_target_pairs={{224,0},{225,1},{226,2},{227,3},{228,4},{229,5},{230,6},{231,7},{2... | collective-permute-start | bytes 622088 | tf_op jit(solution)/shard_map/ppermute | solution.py:391
  33.4 0.7 copy-start.11
  37.9 0.7 copy-start.13
  38.6 0.7 copy-start.15
  48.0 2.3 copy-start
  50.3 0.9 copy-start.5
  51.2 0.9 copy-start.8
  52.1 0.9 copy-start.10
  53.1 0.9 copy-start.12
  54.0 0.9 copy-start.14
  55.0 0.9 copy-start.16
  58.5 0.6 copy-start.18
  118.2 2.3 copy-start.1
  120.4 31.0 %copy-start.6 = (f32[128,4]{1,0:T(8,128)S(1)}, f32[128,4]{1,0:T(8,128)}, u32[]{:S(2)}) copy-start(f32[128,4]{1,0:T(8,128)} %bitcast_divide_fusion.gate_ref) | copy-start | bytes 6148
  120.4 31.0 %copy-start.19 = (f32[32,128]{1,0:T(8,128)S(1)}, f32[32,128]{1,0:T(8,128)}, u32[]{:S(2)}) copy-start(f32[32,128]{1,0:T(8,128)} %copy-done.18) | copy-start | bytes 49156
  128.0 52.4 %copy-start.3 = (bf16[2,64,1440]{2,1,0:T(8,128)(2,1)S(1)}, bf16[2,64,1440]{2,1,0:T(8,128)(2,1)}, u32[]{:S(2)}) copy-start(bf16[2,64,1440]{2,1,0:T(8,128)(2,1)} %param.13) | copy-start | bytes 1105924

commit v6 on v5

--- a/solution.py
+++ b/solution.py
@@ -21,7 +21,7 @@
 ROWS = 2 * HALF
 ALL = E * ROWS
 W = 256
-MIBS = (62, 20, 24, 12, 12, 16, 16, 20)
+MIBS = (62, 20, 60, 12, 12, 16, 16, 20)
 LATER = 224
 
 
@@ -96,36 +96,44 @@
         load.start()
     codes = slot_codes(ids_ref)
     tokens = rows_by_slots(functools.reduce(jnp.maximum, codes))
+    width = grad_ref.shape[1]
+    full = 128 * (width // 128)
+    last = 2 * ROWS * (full // 128)
+    loads[0].wait()
+    tail = None
+    for start in range(0, width, 256):
+        cols = slice(start, min(start + 256, width))
+        grad = dot(tokens, grad_ref[:, cols], NN)
+        for lanes in range(start, min(cols.stop, full), 128):
+            tile = grad[:, lanes - start : lanes - start + 128].reshape(E, ROWS, 128)
+            at = 2 * ROWS * (lanes // 128)
+            out_ref[:, at : at + ROWS, :] = tile.astype(BF)
+        if cols.stop > full:
+            tail = grad[:, full - start :].reshape(E, ROWS, width - full)
     pick = rows_by_slots(token_major(codes))
-    for load in loads:
-        load.wait()
-    width = grad_ref.shape[1]
+    loads[1].wait()
     stores = []
     for start in range(0, width, 256):
         cols = slice(start, min(start + 256, width))
         size = cols.stop - start
-        grad = dot(tokens, grad_ref[:, cols], NN)
         hid = dot(pick, hid_ref[:, :, cols].reshape(N * K, size), NN)
+        for lanes in range(start, min(cols.stop, full), 128):
+            tile = hid[:, lanes - start : lanes - start + 128].reshape(E, ROWS, 128)
+            at = 2 * ROWS * (lanes // 128) + ROWS
+            out_ref[:, at : at + ROWS, :] = tile.astype(BF)
         first = 2 * ROWS * (start // 128)
-        for lanes in range(0, size, 128):
-            at = 2 * ROWS * ((start + lanes) // 128)
-            cut = min(lanes + 128, size)
-            left = grad[:, lanes:cut].reshape(E, ROWS, cut - lanes)
-            right = hid[:, lanes:cut].reshape(E, ROWS, cut - lanes)
-            if cut - lanes == 128:
-                out_ref[:, at : at + ROWS, :] = left.astype(BF)
-                out_ref[:, at + ROWS : at + 2 * ROWS, :] = right.astype(BF)
-                last = at + 2 * ROWS
-            else:
-                tail = [
-                    left[:, 0:16],
-                    jnp.concatenate([left[:, 16:24], right[:, 0:8]], axis=1),
-                    right[:, 8:24],
-                    jnp.zeros((E, 16, 32), F32),
-                ]
-                out_ref[:, at : at + 16, :] = jnp.concatenate(tail, axis=2).astype(BF)
-                last = at + 16
-        part = pl.ds(first, last - first)
+        stop = min(first + 4 * ROWS, last)
+        if cols.stop > full:
+            right = hid[:, full - start :].reshape(E, ROWS, width - full)
+            parts = [
+                tail[:, 0:16],
+                jnp.concatenate([tail[:, 16:24], right[:, 0:8]], axis=1),
+                right[:, 8:24],
+                jnp.zeros((E, 16, 32), F32),
+            ]
+            out_ref[:, last : last + 16, :] = jnp.concatenate(parts, axis=2).astype(BF)
+            stop = last + 16
+        part = pl.ds(first, stop - first)
         store = pltpu.make_async_copy(
             out_ref.at[:, part, :], out_hbm.at[:, part, :], sems.at[2 + len(stores)]
         )
@@ -150,8 +158,18 @@
         ).astype(BF)
 
 
-def expert_kernel(got_ref, down_ref, back_ref, base_ref, out_ref, grad_ref, hid_ref):
+def expert_kernel(
+    got_ref, down_hbm, back_ref, base_ref, out_ref, grad_ref, hid_ref, down_ref, sems
+):
     inner = down_ref.shape[0]
+    loads = []
+    for start in range(0, inner, 256):
+        rows = pl.ds(start, min(256, inner - start))
+        load = pltpu.make_async_copy(
+            down_hbm.at[rows, :], down_ref.at[rows, :], sems.at[len(loads)]
+        )
+        load.start()
+        loads.append(load)
     full = 128 * (inner // 128)
     for lanes in range(0, full, 128):
         at = 2 * ROWS * (lanes // 128)
@@ -168,6 +186,7 @@
     total = jnp.zeros((ALL, 1), F32)
     for start in range(0, inner, 256):
         cols = slice(start, min(start + 256, inner))
+        loads[start // 256].wait()
         base = dot(grad_ref[...], down_ref[cols, :], NT)
         base_ref[:, cols] = base.astype(BF)
         total = total + jnp.sum(hid_ref[:, cols].astype(F32) * base, axis=1, keepdims=True)
@@ -181,6 +200,14 @@
     out_ref[...] = jnp.where(lane < LATER, proj, tail).astype(BF)
 
 
+def picks_kernel(ids_ref, first_ref, second_ref, third_ref):
+    codes = slot_codes(ids_ref)
+    wide = jnp.concatenate(codes, axis=1)
+    first_ref[...] = slots_by_rows(wide)
+    second_ref[...] = rows_by_slots(wide)
+    third_ref[...] = slots_by_rows(token_major(codes))
+
+
 def id_masks(ids_ref):
     spread = one(divided(iota((8, W), 1), E) == iota((8, W), 0))
     lane = iota((N, W), 1) & (E - 1)
@@ -191,9 +218,8 @@
     return masks, spread
 
 
-def blocks_kernel(got_ref, row_ref, ids_ref, gate_ref, out_ref):
-    pick = slots_by_rows(jnp.concatenate(slot_codes(row_ref), axis=1))
-    slots = dot(pick, got_ref[...], NN)
+def blocks_kernel(got_ref, pick_ref, ids_ref, gate_ref, out_ref):
+    slots = dot(pick_ref[...], got_ref[...], NN)
     gates = [gate_ref[:, k : k + 1] for k in range(K)]
     parts = [slots[k * N : (k + 1) * N] for k in range(K)]
     lane = iota((N, W), 1)
@@ -218,7 +244,7 @@
         out_ref[d] = packed
 
 
-def solve_kernel(at_ref, got_ref, row_ref, ids_ref, gate_ref, out_ref, coef_ref):
+def solve_kernel(at_ref, got_ref, pick_ref, ids_ref, gate_ref, out_ref, coef_ref):
     at = at_ref[0]
     depth = iota((8, K * N), 0)
     found = jnp.zeros((8, K * N), F32)
@@ -261,8 +287,7 @@
         value = jnp.where(col == 7, up.astype(F32), gate * short)
         value = jnp.where(col == 15, rest.astype(F32), value)
         rows.append(jnp.concatenate([value, names], axis=1).astype(BF))
-    pick = rows_by_slots(jnp.concatenate(slot_codes(row_ref), axis=1))
-    sent = dot(pick, jnp.concatenate(rows, axis=0), NN).reshape(E, ROWS, 64)
+    sent = dot(pick_ref[...], jnp.concatenate(rows, axis=0), NN).reshape(E, ROWS, 64)
     out_ref[:, :, 0:64] = sent[:, 0:16].astype(BF)
     rest = jnp.concatenate([sent[:, 16:24], jnp.zeros((E, 8, 64), F32)], axis=1)
     out_ref[:, :, 64:128] = rest.astype(BF)
@@ -314,12 +339,11 @@
     out_ref[:, width + 2 * E :] = jnp.zeros((ALL, out_ref.shape[1] - width - 2 * E), BF)
 
 
-def combine_kernel(got_ref, ids_ref, out_ref, router_ref):
-    pick = slots_by_rows(token_major(slot_codes(ids_ref)))
+def combine_kernel(got_ref, pick_ref, out_ref, router_ref):
     width = out_ref.shape[2]
     for start in range(0, width, 256):
         cols = slice(start, min(start + 256, width))
-        own = dot(pick, got_ref[:, cols], NN).astype(BF)
+        own = dot(pick_ref[...], got_ref[:, cols], NN).astype(BF)
         out_ref[:, :, cols] = own.reshape(N, K, cols.stop - start)
     parts = got_ref[:, width : width + 2 * E].astype(F32).reshape(E, ROWS, 2 * E)
     total = jnp.sum(parts, axis=0)
@@ -397,6 +421,12 @@
         MIBS[1],
     )
 
+    picks = call(
+        picks_kernel,
+        [((N * K, ALL), BF), ((ALL, N * K), BF), ((N * K, ALL), BF)],
+        (turned,),
+        12,
+    )
     logits = jnp.einsum("mtd,mde->mte", inputs, tables, preferred_element_type=F32)
     labels = jnp.arange(E, dtype=I32)
     picked = routes[:, :, :, None] == labels
@@ -409,34 +439,36 @@
         [((ALL, inner), BF), ((ALL, W), BF)],
         (arrived, mats, back),
         MIBS[2],
-        scratch=[((ALL, width), BF), ((ALL, inner), BF)],
-    )
-    rest = (gating, turned, id_all, section.reshape(1), grads, inputs, table_rows, back, base)
+        scratch=[((ALL, width), BF), ((ALL, inner), BF), ((inner, width), BF)],
+        sems=steps,
+        far=(1,),
+    )
+    rest = (gating, picks, id_all, section.reshape(1), grads, inputs, table_rows, back, base)
     proj, rest = lax.optimization_barrier((proj, rest))
     returned = exchange(proj.reshape(E, ROWS, W), "expert").reshape(ALL, W)
     returned, rest = lax.optimization_barrier((returned, rest))
-    gating, turned, id_all, where, grads, inputs, table_rows, back, base = rest
+    gating, picks, id_all, where, grads, inputs, table_rows, back, base = rest
     (blocks,) = call(
         blocks_kernel,
         [((8, 8, K * K * N), BF)],
-        (returned, turned, id_all, gating),
+        (returned, picks[0], id_all, gating),
         MIBS[3],
     )
     blocks, rest = lax.optimization_barrier((blocks, rest))
     gathered = exchange(blocks, "pipe")
     gathered, rest = lax.optimization_barrier((gathered, rest))
-    gating, turned, id_all, where, grads, inputs, table_rows, back, base = rest
+    gating, picks, id_all, where, grads, inputs, table_rows, back, base = rest
     coef_sent, coef = call(
         solve_kernel,
         [((E, 16, 128), BF), ((N, W), BF)],
-        (where, gathered, turned, id_all, gating),
+        (where, gathered, picks[1], id_all, gating),
         MIBS[4],
         smem=1,
     )
     coef_sent, coef, rest = lax.optimization_barrier((coef_sent, coef, rest))
     coef_got = exchange(coef_sent, "expert")
     coef_got, coef, rest = lax.optimization_barrier((coef_got, coef, rest))
-    gating, turned, id_all, where, grads, inputs, table_rows, back, base = rest
+    gating, picks, id_all, where, grads, inputs, table_rows, back, base = rest
     passed, parts = call(
         passed_kernel,
         [((N, width), BF), ((ALL, 2 * E), BF)],
@@ -449,7 +481,7 @@
     )
     answered = exchange(answer.reshape(E, ROWS, wide), "expert").reshape(ALL, wide)
     hidden_grads, grad_router = call(
-        combine_kernel, [((N, K, inner), BF), ((E, width // E), F32)], (answered, turned), MIBS[7]
+        combine_kernel, [((N, K, inner), BF), ((E, width // E), F32)], (answered, picks[2]), MIBS[7]
     )
     return (
         passed.reshape(1, 2, T, width),

time: 249 us -> 253 us (1.016)
  Pallas kernels: 26.3 us -> 34.3 us
  local copies, waits for them, and re-layouts: 14.7 us -> 10.6 us
    pallas_call x8 -> x9, Pallas kernels: 26.3 us -> 34.3 us  [call(): pl.pallas_call(body, out_shape=[jax.ShapeDtypeStruct(s, d) for s, d in sh...]
    unnamed x44 -> x38, local copies, waits for them, and re-layouts: 14.2 us -> 10.1 us
  transfers between devices with their start and end apart: 8 -> 8, of which waited for: 6 -> 7; matrix products, arithmetic and copies ran while one was open for 1% -> 0% of each run, Pallas kernels for 1% -> 2%
where the time goes in v6:
time: 253 us
  blocking collectives  110 us (43%)
  waiting for transfers between devices  76 us (30%)
  Pallas kernels  34.3 us (14%)
  starting transfers between devices  20.6 us (8%)
  local copies, waits for them, and re-layouts  10.6 us (4%)
    all_to_all x4, blocking collectives, exchange(): return lax.all_to_all(x, axis, split_axis=0, concat_axis=0, tiled=True)  110 us
    all_to_all x1, waiting for transfers between devices, exchange(): return lax.all_to_all(x, axis, split_axis=0, concat_axis=0, tiled=True)  61.2 us
    pallas_call x9, Pallas kernels, call(): pl.pallas_call(body, out_shape=[jax.ShapeDtypeStruct(s, d) for s, d in sh...  34.3 us
    ppermute x7, waiting for transfers between devices, on_device(): lax.ppermute(own, 'pipe', [(i, i - by) for i in range(by, pipe)])  14.7 us
    all_to_all x1, starting transfers between devices, exchange(): return lax.all_to_all(x, axis, split_axis=0, concat_axis=0, tiled=True)  11.4 us
    unnamed x38, local copies, waits for them, and re-layouts  10.1 us
    ppermute x7, starting transfers between devices, on_device(): lax.ppermute(own, 'pipe', [(i, i - by) for i in range(by, pipe)])  9.21 us
  transfers between devices with their start and end apart: 8, of which 7 were waited for; matrix products, arithmetic and copies ran while one was open for 0% of the time, Pallas kernels for 2%

profile of v6, /device:TPU:32, one launch (start us, length us, event | category | flops | bytes accessed | tf_op | source)
XLA Modules:
  0.0 252.9 jit_solution(6413382331949359371)
XLA Ops:
  0.6 5.6 %shard_map.94 = bf16[32,544,128]{2,1,0:T(8,128)(2,1)} custom-call(s32[2,4,64]{2,1,0:T(4,128)} %bitcast.51, bf16[128,4,1440]{2,1,0:T(4,128)(2,1)} %bitcast.54, bf16[128,1440]{1,0:T(8,128)(2,1)} %bitcast.49), custom_call_target="tpu_custom_call" | custom-call | tf_op jit(solution)/shard_map/pallas_call | solution.py:367
  6.3 0.0 copy-start.16
  6.3 0.0 copy-start.4
  6.3 11.4 %all-to-all-start = ((bf16[32,544,128]{2,1,0:T(8,128)(2,1)}), bf16[32,544,128]{2,1,0:T(8,128)(2,1)}, u32[]{:S(2)}, u32[]{:S(2)}) async-start(bf16[32,544,128]{2,1,0:T(8,128)(2,1)} %shard_map.94), calls=%async_computation | async-start | bytes 8912896 | tf_op jit(solution)/shard_map/all_to_all | solution.py:378
  17.7 0.1 convert_element_type.13
  17.8 0.1 broadcast_in_dim.64
  17.9 0.1 broadcast_in_dim.65
  18.0 0.1 bitcast_select_fusion
  18.1 1.3 collective-permute-start
  19.4 1.3 collective-permute-start.1
  20.7 1.3 collective-permute-start.2
  22.0 1.3 collective-permute-start.3
  23.3 1.3 collective-permute-start.4
  24.6 1.4 shard_map.97
  26.0 0.9 copy-done.6
  26.9 0.9 copy-done.8
  27.8 0.3 convolution_bitcast_fusion
  28.2 0.1 copy.16
  28.3 0.1 div.11
  28.4 1.3 collective-permute-start.5
  29.7 1.1 collective-permute-done.1.refs_1_
  30.8 1.5 collective-permute-start.6
  32.2 0.1 bitcast_divide_fusion.gate_ref
  32.3 0.3 collective-permute-done.2.refs_2_
  32.7 0.7 copy-done.10
  33.3 4.6 %collective-permute-done.3.refs_3_ = bf16[72,1440]{1,0:T(8,128)(2,1)S(1)} collective-permute-done((bf16[72,1440]{1,0:T(8,128)(2,1)S(1)}, bf16[72,1440]{1,0:T(8,128)(2,1)S(1)}, u32[]{:S(2)}, u32[]{:S(2)}) %collective-permute-start.3) | collective-permute-done | bytes 207392 | tf_op jit(solution)/shard_map/ppermute | solution.py:415
  37.9 0.7 copy-done.12
  38.6 0.1 collective-permute-done.4.refs_4_
  38.7 0.7 copy-done.14
  39.4 8.6 %collective-permute-done.5.refs_5_ = bf16[72,1440]{1,0:T(8,128)(2,1)S(1)} collective-permute-done((bf16[72,1440]{1,0:T(8,128)(2,1)S(1)}, bf16[72,1440]{1,0:T(8,128)(2,1)S(1)}, u32[]{:S(2)}, u32[]{:S(2)}) %collective-permute-start.5) | collective-permute-done | bytes 207392 | tf_op jit(solution)/shard_map/ppermute | solution.py:415
  47.9 0.1 collective-permute-done.6.refs_6_
  48.0 2.3 copy-done
  50.3 0.9 copy-done.11
  51.2 0.9 copy-done.13
  52.2 0.9 copy-done.15
  53.1 2.6 %shard_map.95 = (bf16[512,1440]{1,0:T(8,128)(2,1)S(1)}, bf16[512,1440]{1,0:T(8,128)(2,1)S(1)}, f32[32,128]{1,0:T(8,128)S(1)}) custom-call(bf16[72,1440]{1,0:T(8,128)(2,1)S(1)} %collective-permute-done.refs_0_, bf16[72,1440]{1,0:T(8,128)(2,1)S(1)} %collective-permute-done.1.refs_1_, bf16[72,1440]{1,0:T(8,128)(2,1)S(1)} %copy-done.11, ...), custom_call_target="tpu_custom_call" | custom-call | tf_op jit(solution)/shard_map/pallas_call | solution.py:367
  55.8 1.1 copy-done.1
  56.9 61.2 %all-to-all-done.got_ref = bf16[32,544,128]{2,1,0:T(8,128)(2,1)} async-done(((bf16[32,544,128]{2,1,0:T(8,128)(2,1)}), bf16[32,544,128]{2,1,0:T(8,128)(2,1)}, u32[]{:S(2)}, u32[]{:S(2)}) %all-to-all-start) | async-done | bytes 4456480 | tf_op jit(solution)/shard_map/all_to_all | solution.py:378
  118.1 15.4 %shard_map.96 = (bf16[768,1440]{1,0:T(8,128)(2,1)}, bf16[768,256]{1,0:T(8,128)(2,1)}) custom-call(bf16[32,544,128]{2,1,0:T(8,128)(2,1)} %all-to-all-done.got_ref, bf16[1440,1440]{1,0:T(8,128)(2,1)} %bitcast.43, bf16[512,1440]{1,0:T(8,128)(2,1)} %copy-done.1), custom_call_target="tpu_custom_call" | custom-call | tf_op jit(solution)/shard_map/pallas_call | solution.py:367
  133.6 23.8 %all_to_all.25 = bf16[32,24,256]{2,1,0:T(8,128)(2,1)S(1)} all-to-all(bf16[32,24,256]{2,1,0:T(8,128)(2,1)} %bitcast.55), channel_id=1, replica_groups=mesh['pipe'=8,'expert'=32] {'expert'}, dimensions={0} | all-to-all | bytes 786432 | tf_op jit(solution)/shard_map/all_to_all | solution.py:378
  157.3 1.2 shard_map.98
  158.6 12.1 %all_to_all.26.got_ref = bf16[8,8,2048]{2,1,0:T(8,128)(2,1)S(1)} all-to-all(bf16[8,8,2048]{2,1,0:T(8,128)(2,1)S(1)} %shard_map.98), channel_id=1, replica_groups=mesh['pipe'=8,'expert'=32] {'pipe'}, dimensions={0} | all-to-all | bytes 524288 | tf_op jit(solution)/shard_map/all_to_all | solution.py:378
  170.7 1.1 shard_map.99
  171.8 14.2 %all_to_all.27.got_ref = bf16[32,16,128]{2,1,0:T(8,128)(2,1)S(1)} all-to-all(bf16[32,16,128]{2,1,0:T(8,128)(2,1)S(1)} %get-tuple-element.135), channel_id=1, replica_groups=mesh['pipe'=8,'expert'=32] {'expert'}, dimensions={0} | all-to-all | bytes 262144 | tf_op jit(solution)/shard_map/all_to_all | solution.py:378
  186.0 1.9 shard_map.100
  187.9 2.5 shard_map.101
  190.4 59.9 %all_to_all.28 = bf16[32,24,1536]{2,1,0:T(8,128)(2,1)S(1)} all-to-all(bf16[32,24,1536]{2,1,0:T(8,128)(2,1)S(1)} %bitcast.45), channel_id=1, replica_groups=mesh['pipe'=8,'expert'=32] {'expert'}, dimensions={0} | all-to-all | bytes 4718592 | tf_op jit(solution)/shard_map/all_to_all | solution.py:378
  250.3 2.5 %shard_map.102 = (bf16[128,4,1440]{2,1,0:T(4,128)(2,1)}, f32[32,45]{1,0:T(8,128)}) custom-call(bf16[768,1536]{1,0:T(8,128)(2,1)S(1)} %bitcast.46, bf16[512,768]{1,0:T(8,128)(2,1)S(1)} %copy-done.9), custom_call_target="tpu_custom_call" | custom-call | tf_op jit(solution)/shard_map/pallas_call | solution.py:367
  (34 shorter events, 0.2 us)
Async XLA Ops:
  6.3 11.4 %copy-start.16 = (s32[1,2,64,4]{2,3,1,0:T(4,128)S(1)}, s32[1,2,64,4]{2,3,1,0:T(4,128)}, u32[]{:S(2)}) copy-start(s32[1,2,64,4]{2,3,1,0:T(4,128)} %param.9) | copy-start | bytes 6148
  6.3 11.5 %copy-start.18 = (s32[1,2]{1,0:T(1,128)S(1)}, s32[1,2]{1,0:T(1,128)}, u32[]{:S(2)}) copy-start(s32[1,2]{1,0:T(1,128)} %param.10) | copy-start | bytes 28
  6.3 11.7 %copy-start.17 = (bf16[1,2,1440,32]{2,3,1,0:T(8,128)(2,1)S(1)}, bf16[1,2,1440,32]{2,3,1,0:T(8,128)(2,1)}, u32[]{:S(2)}) copy-start(bf16[1,2,1440,32]{2,3,1,0:T(8,128)(2,1)} %param.11) | copy-start | bytes 552964
  6.3 21.5 %copy-start.4 = (bf16[1,2,64,1440]{3,2,1,0:T(8,128)(2,1)S(1)}, bf16[1,2,64,1440]{3,2,1,0:T(8,128)(2,1)}, u32[]{:S(2)}) copy-start(bf16[1,2,64,1440]{3,2,1,0:T(8,128)(2,1)} %param.7) | copy-start | bytes 1105924
  6.3 111.8 %all-to-all-start = ((bf16[32,544,128]{2,1,0:T(8,128)(2,1)}), bf16[32,544,128]{2,1,0:T(8,128)(2,1)}, u32[]{:S(2)}, u32[]{:S(2)}) async-start(bf16[32,544,128]{2,1,0:T(8,128)(2,1)} %shard_map.94), calls=%async_computation | async-start | bytes 8912896 | tf_op jit(solution)/shard_map/all_to_all | solution.py:378
  18.1 10.2 %collective-permute-start = (bf16[72,1440]{1,0:T(8,128)(2,1)S(1)}, bf16[72,1440]{1,0:T(8,128)(2,1)S(1)}, u32[]{:S(2)}, u32[]{:S(2)}) collective-permute-start(bf16[72,1440]{1,0:T(8,128)(2,1)S(1)} %fusion.1.refs_7_), channel_id=1, source_target_pairs={{32,0},{64,32},{96,64},{128,96},{160,128},{192,160},{224,192},{33,... | collective-permute-start | bytes 622088 | tf_op jit(solution)/shard_map/ppermute | solution.py:415
  19.4 11.3 %collective-permute-start.1 = (bf16[72,1440]{1,0:T(8,128)(2,1)S(1)}, bf16[72,1440]{1,0:T(8,128)(2,1)S(1)}, u32[]{:S(2)}, u32[]{:S(2)}) collective-permute-start(bf16[72,1440]{1,0:T(8,128)(2,1)S(1)} %fusion.1.refs_7_), channel_id=1, source_target_pairs={{64,0},{96,32},{128,64},{160,96},{192,128},{224,160},{65,1},{97,33... | collective-permute-start | bytes 622088 | tf_op jit(solution)/shard_map/ppermute | solution.py:415
  20.7 11.9 %collective-permute-start.2 = (bf16[72,1440]{1,0:T(8,128)(2,1)S(1)}, bf16[72,1440]{1,0:T(8,128)(2,1)S(1)}, u32[]{:S(2)}, u32[]{:S(2)}) collective-permute-start(bf16[72,1440]{1,0:T(8,128)(2,1)S(1)} %fusion.1.refs_7_), channel_id=1, source_target_pairs={{96,0},{128,32},{160,64},{192,96},{224,128},{97,1},{129,33},{161,6... | collective-permute-start | bytes 622088 | tf_op jit(solution)/shard_map/ppermute | solution.py:415
  22.0 15.9 %collective-permute-start.3 = (bf16[72,1440]{1,0:T(8,128)(2,1)S(1)}, bf16[72,1440]{1,0:T(8,128)(2,1)S(1)}, u32[]{:S(2)}, u32[]{:S(2)}) collective-permute-start(bf16[72,1440]{1,0:T(8,128)(2,1)S(1)} %fusion.1.refs_7_), channel_id=1, source_target_pairs={{128,0},{160,32},{192,64},{224,96},{129,1},{161,33},{193,65},{225,... | collective-permute-start | bytes 622088 | tf_op jit(solution)/shard_map/ppermute | solution.py:415
  23.3 15.3 %collective-permute-start.4 = (bf16[72,1440]{1,0:T(8,128)(2,1)S(1)}, bf16[72,1440]{1,0:T(8,128)(2,1)S(1)}, u32[]{:S(2)}, u32[]{:S(2)}) collective-permute-start(bf16[72,1440]{1,0:T(8,128)(2,1)S(1)} %fusion.1.refs_7_), channel_id=1, source_target_pairs={{160,0},{192,32},{224,64},{161,1},{193,33},{225,65},{162,2},{194,3... | collective-permute-start | bytes 622088 | tf_op jit(solution)/shard_map/ppermute | solution.py:415
  26.0 0.9 copy-start.6
  26.9 0.9 copy-start.8
  28.4 19.6 %collective-permute-start.5 = (bf16[72,1440]{1,0:T(8,128)(2,1)S(1)}, bf16[72,1440]{1,0:T(8,128)(2,1)S(1)}, u32[]{:S(2)}, u32[]{:S(2)}) collective-permute-start(bf16[72,1440]{1,0:T(8,128)(2,1)S(1)} %fusion.1.refs_7_), channel_id=1, source_target_pairs={{192,0},{224,32},{193,1},{225,33},{194,2},{226,34},{195,3},{227,35... | collective-permute-start | bytes 622088 | tf_op jit(solution)/shard_map/ppermute | solution.py:415
  30.8 17.3 %collective-permute-start.6 = (bf16[72,1440]{1,0:T(8,128)(2,1)S(1)}, bf16[72,1440]{1,0:T(8,128)(2,1)S(1)}, u32[]{:S(2)}, u32[]{:S(2)}) collective-permute-start(bf16[72,1440]{1,0:T(8,128)(2,1)S(1)} %fusion.1.refs_7_), channel_id=1, source_target_pairs={{224,0},{225,1},{226,2},{227,3},{228,4},{229,5},{230,6},{231,7},{2... | collective-permute-start | bytes 622088 | tf_op jit(solution)/shard_map/ppermute | solution.py:415
  32.7 0.7 copy-start.10
  37.9 0.7 copy-start.12
  38.7 0.7 copy-start.14
  48.0 2.3 copy-start
  50.3 0.9 copy-start.11
  51.2 0.9 copy-start.13
  52.2 0.9 copy-start.15
  55.8 1.1 copy-start.1
  133.5 37.1 %copy-start.7 = (bf16[768,512]{1,0:T(8,128)(2,1)S(1)}, bf16[768,512]{1,0:T(8,128)(2,1)}, u32[]{:S(2)}) copy-start(bf16[768,512]{1,0:T(8,128)(2,1)} %copy-done.6) | copy-start | bytes 2359300
  133.6 52.5 %copy-start.5 = (bf16[2,64,1440]{2,1,0:T(8,128)(2,1)S(1)}, bf16[2,64,1440]{2,1,0:T(8,128)(2,1)}, u32[]{:S(2)}) copy-start(bf16[2,64,1440]{2,1,0:T(8,128)(2,1)} %param.13) | copy-start | bytes 1105924
  158.6 29.3 %copy-start.2 = (bf16[512,1440]{1,0:T(8,128)(2,1)S(1)}, bf16[512,1440]{1,0:T(8,128)(2,1)}, u32[]{:S(2)}) copy-start(bf16[512,1440]{1,0:T(8,128)(2,1)} %copy-done.1) | copy-start | bytes 4423684
  158.6 29.3 %copy-start.3 = (bf16[768,1440]{1,0:T(8,128)(2,1)S(1)}, bf16[768,1440]{1,0:T(8,128)(2,1)}, u32[]{:S(2)}) copy-start(bf16[768,1440]{1,0:T(8,128)(2,1)} %get-tuple-element.149.base_ref) | copy-start | bytes 6635524
  190.4 59.9 %copy-start.9 = (bf16[512,768]{1,0:T(8,128)(2,1)S(1)}, bf16[512,768]{1,0:T(8,128)(2,1)}, u32[]{:S(2)}) copy-start(bf16[512,768]{1,0:T(8,128)(2,1)} %copy-done.8) | copy-start | bytes 2359300

commit v7 on v5

--- a/solution.py
+++ b/solution.py
@@ -21,7 +21,7 @@
 ROWS = 2 * HALF
 ALL = E * ROWS
 W = 256
-MIBS = (62, 20, 24, 12, 12, 16, 16, 20)
+MIBS = (62, 20, 24, 12, 12, 16, 20, 20)
 LATER = 224
 
 
@@ -181,6 +181,14 @@
     out_ref[...] = jnp.where(lane < LATER, proj, tail).astype(BF)
 
 
+def picks_kernel(ids_ref, first_ref, second_ref, third_ref):
+    codes = slot_codes(ids_ref)
+    wide = jnp.concatenate(codes, axis=1)
+    first_ref[...] = slots_by_rows(wide)
+    second_ref[...] = rows_by_slots(wide)
+    third_ref[...] = slots_by_rows(token_major(codes))
+
+
 def id_masks(ids_ref):
     spread = one(divided(iota((8, W), 1), E) == iota((8, W), 0))
     lane = iota((N, W), 1) & (E - 1)
@@ -191,9 +199,8 @@
     return masks, spread
 
 
-def blocks_kernel(got_ref, row_ref, ids_ref, gate_ref, out_ref):
-    pick = slots_by_rows(jnp.concatenate(slot_codes(row_ref), axis=1))
-    slots = dot(pick, got_ref[...], NN)
+def blocks_kernel(got_ref, pick_ref, ids_ref, gate_ref, out_ref):
+    slots = dot(pick_ref[...], got_ref[...], NN)
     gates = [gate_ref[:, k : k + 1] for k in range(K)]
     parts = [slots[k * N : (k + 1) * N] for k in range(K)]
     lane = iota((N, W), 1)
@@ -218,7 +225,7 @@
         out_ref[d] = packed
 
 
-def solve_kernel(at_ref, got_ref, row_ref, ids_ref, gate_ref, out_ref, coef_ref):
+def solve_kernel(at_ref, got_ref, pick_ref, ids_ref, gate_ref, out_ref, coef_ref):
     at = at_ref[0]
     depth = iota((8, K * N), 0)
     found = jnp.zeros((8, K * N), F32)
@@ -261,18 +268,26 @@
         value = jnp.where(col == 7, up.astype(F32), gate * short)
         value = jnp.where(col == 15, rest.astype(F32), value)
         rows.append(jnp.concatenate([value, names], axis=1).astype(BF))
-    pick = rows_by_slots(jnp.concatenate(slot_codes(row_ref), axis=1))
-    sent = dot(pick, jnp.concatenate(rows, axis=0), NN).reshape(E, ROWS, 64)
+    sent = dot(pick_ref[...], jnp.concatenate(rows, axis=0), NN).reshape(E, ROWS, 64)
     out_ref[:, :, 0:64] = sent[:, 0:16].astype(BF)
     rest = jnp.concatenate([sent[:, 16:24], jnp.zeros((E, 8, 64), F32)], axis=1)
     out_ref[:, :, 64:128] = rest.astype(BF)
 
 
-def passed_kernel(coef_ref, tab_ref, grad_ref, acts_ref, pass_ref, part_ref):
+def section_columns(j):
+    row, col = iota((W, 32), 0), iota((W, 32), 1)
+    return one((row < LATER) & ((row >> 5) + 8 * j == col))
+
+
+def answer_kernel(
+    got_ref, base_ref, back_ref, coef_ref, tab_ref, grad_ref, acts_ref, out_ref, pass_hbm, pass_ref, sems
+):
     for m in range(2):
         rows = slice(m * T, (m + 1) * T)
         moved = dot(coef_ref[rows, :], tab_ref[m * W : (m + 1) * W, :], NN)
         pass_ref[rows, :] = (grad_ref[rows, :].astype(F32) + moved).astype(BF)
+    store = pltpu.make_async_copy(pass_ref, pass_hbm, sems.at[0])
+    store.start()
     own = coef_ref[:, LATER:W]
     width = acts_ref.shape[1]
     router = (dot(acts_ref[...], own, TN) / T).astype(BF)
@@ -282,17 +297,9 @@
     peer = divided(iota((ALL, 1), 0), ROWS)
     source = iota((ALL, 1), 0) + (each - ROWS) * peer
     select = one(source == col)
-    part_ref[:, 0:E] = dot(select, router, NN).astype(BF)
-    part_ref[:, E : 2 * E] = dot(select, ahead, NN).astype(BF)
-
-
-def section_columns(j):
-    row, col = iota((W, 32), 0), iota((W, 32), 1)
-    return one((row < LATER) & ((row >> 5) + 8 * j == col))
-
-
-def answer_kernel(got_ref, base_ref, back_ref, part_ref, out_ref):
-    width = base_ref.shape[1]
+    out_ref[:, width : width + E] = dot(select, router, NN).astype(BF)
+    out_ref[:, width + E : width + 2 * E] = dot(select, ahead, NN).astype(BF)
+    out_ref[:, width + 2 * E :] = jnp.zeros((ALL, out_ref.shape[1] - width - 2 * E), BF)
     got = got_ref[...].astype(F32)
     got = jnp.concatenate([got[:, :, 0:64], got[:, 0:8, 64:128]], axis=1).reshape(ALL, 64)
     gate = got[:, 7:8] + got[:, 15:16]
@@ -310,16 +317,14 @@
         cols = slice(start, min(start + 256, width))
         moved = dot(left, back_ref[0:W, cols], NN) + dot(right, back_ref[W : 2 * W, cols], NN)
         out_ref[:, cols] = (gate * base_ref[:, cols].astype(F32) + moved).astype(BF)
-    out_ref[:, width : width + 2 * E] = part_ref[...]
-    out_ref[:, width + 2 * E :] = jnp.zeros((ALL, out_ref.shape[1] - width - 2 * E), BF)
-
-
-def combine_kernel(got_ref, ids_ref, out_ref, router_ref):
-    pick = slots_by_rows(token_major(slot_codes(ids_ref)))
+    store.wait()
+
+
+def combine_kernel(got_ref, pick_ref, out_ref, router_ref):
     width = out_ref.shape[2]
     for start in range(0, width, 256):
         cols = slice(start, min(start + 256, width))
-        own = dot(pick, got_ref[:, cols], NN).astype(BF)
+        own = dot(pick_ref[...], got_ref[:, cols], NN).astype(BF)
         out_ref[:, :, cols] = own.reshape(N, K, cols.stop - start)
     parts = got_ref[:, width : width + 2 * E].astype(F32).reshape(E, ROWS, 2 * E)
     total = jnp.sum(parts, axis=0)
@@ -397,6 +402,12 @@
         MIBS[1],
     )
 
+    picks = call(
+        picks_kernel,
+        [((N * K, ALL), BF), ((ALL, N * K), BF), ((N * K, ALL), BF)],
+        (turned,),
+        12,
+    )
     logits = jnp.einsum("mtd,mde->mte", inputs, tables, preferred_element_type=F32)
     labels = jnp.arange(E, dtype=I32)
     picked = routes[:, :, :, None] == labels
@@ -411,45 +422,45 @@
         MIBS[2],
         scratch=[((ALL, width), BF), ((ALL, inner), BF)],
     )
-    rest = (gating, turned, id_all, section.reshape(1), grads, inputs, table_rows, back, base)
+    rest = (gating, picks, id_all, section.reshape(1), grads, inputs, table_rows, back, base)
     proj, rest = lax.optimization_barrier((proj, rest))
     returned = exchange(proj.reshape(E, ROWS, W), "expert").reshape(ALL, W)
     returned, rest = lax.optimization_barrier((returned, rest))
-    gating, turned, id_all, where, grads, inputs, table_rows, back, base = rest
+    gating, picks, id_all, where, grads, inputs, table_rows, back, base = rest
     (blocks,) = call(
         blocks_kernel,
         [((8, 8, K * K * N), BF)],
-        (returned, turned, id_all, gating),
+        (returned, picks[0], id_all, gating),
         MIBS[3],
     )
     blocks, rest = lax.optimization_barrier((blocks, rest))
     gathered = exchange(blocks, "pipe")
     gathered, rest = lax.optimization_barrier((gathered, rest))
-    gating, turned, id_all, where, grads, inputs, table_rows, back, base = rest
+    gating, picks, id_all, where, grads, inputs, table_rows, back, base = rest
     coef_sent, coef = call(
         solve_kernel,
         [((E, 16, 128), BF), ((N, W), BF)],
-        (where, gathered, turned, id_all, gating),
+        (where, gathered, picks[1], id_all, gating),
         MIBS[4],
         smem=1,
     )
     coef_sent, coef, rest = lax.optimization_barrier((coef_sent, coef, rest))
     coef_got = exchange(coef_sent, "expert")
     coef_got, coef, rest = lax.optimization_barrier((coef_got, coef, rest))
-    gating, turned, id_all, where, grads, inputs, table_rows, back, base = rest
-    passed, parts = call(
-        passed_kernel,
-        [((N, width), BF), ((ALL, 2 * E), BF)],
-        (coef, table_rows, grads, inputs.reshape(N, width)),
-        MIBS[5],
-    )
+    gating, picks, id_all, where, grads, inputs, table_rows, back, base = rest
     wide = 256 * steps
-    (answer,) = call(
-        answer_kernel, [((ALL, wide), BF)], (coef_got, base, back, parts), MIBS[6]
+    answer, passed = call(
+        answer_kernel,
+        [((ALL, wide), BF), ((N, width), BF)],
+        (coef_got, base, back, coef, table_rows, grads, inputs.reshape(N, width)),
+        MIBS[6],
+        scratch=[((N, width), BF)],
+        sems=1,
+        far_out=(1,),
     )
     answered = exchange(answer.reshape(E, ROWS, wide), "expert").reshape(ALL, wide)
     hidden_grads, grad_router = call(
-        combine_kernel, [((N, K, inner), BF), ((E, width // E), F32)], (answered, turned), MIBS[7]
+        combine_kernel, [((N, K, inner), BF), ((E, width // E), F32)], (answered, picks[2]), MIBS[7]
     )
     return (
         passed.reshape(1, 2, T, width),

time: 249 us -> 247 us (level)
  waiting for transfers between devices: 75.1 us -> 71.7 us
    ppermute x7, waiting for transfers between devices: 16.1 us -> 12.1 us  [on_device(): lax.ppermute(own, 'pipe', [(i, i - by) for i in range(by, pipe)])]
    unnamed x44 -> x52, local copies, waits for them, and re-layouts: 14.2 us -> 16.2 us
  transfers between devices with their start and end apart: 8 -> 8, of which waited for: 6 -> 5; matrix products, arithmetic and copies ran while one was open for 1% -> 1% of each run, Pallas kernels for 1% -> 2%
where the time goes in v7:
time: 247 us; the launch traced here: 246 us
  blocking collectives  109 us (44%)
  waiting for transfers between devices  71.7 us (29%)
  Pallas kernels  25.9 us (10%)
  starting transfers between devices  20.4 us (8%)
  local copies, waits for them, and re-layouts  16.7 us (7%)
    all_to_all x4, blocking collectives, exchange(): return lax.all_to_all(x, axis, split_axis=0, concat_axis=0, tiled=True)  109 us
    all_to_all x1, waiting for transfers between devices, exchange(): return lax.all_to_all(x, axis, split_axis=0, concat_axis=0, tiled=True)  59.6 us
    pallas_call x8, Pallas kernels, call(): pl.pallas_call(body, out_shape=[jax.ShapeDtypeStruct(s, d) for s, d in sh...  25.9 us
    unnamed x52, local copies, waits for them, and re-layouts  16.2 us
    ppermute x7, waiting for transfers between devices, on_device(): lax.ppermute(own, 'pipe', [(i, i - by) for i in range(by, pipe)])  12.1 us
    all_to_all x1, starting transfers between devices, exchange(): return lax.all_to_all(x, axis, split_axis=0, concat_axis=0, tiled=True)  11.4 us
    ppermute x7, starting transfers between devices, on_device(): lax.ppermute(own, 'pipe', [(i, i - by) for i in range(by, pipe)])  9.02 us
  transfers between devices with their start and end apart: 8, of which 5 were waited for; matrix products, arithmetic and copies ran while one was open for 1% of the time, Pallas kernels for 2%

profile of v7, /device:TPU:32, one launch (start us, length us, event | category | flops | bytes accessed | tf_op | source)
XLA Modules:
  0.0 246.2 jit_solution(1472326392415789799)
XLA Ops:
  0.6 5.6 %shard_map.94 = bf16[32,544,128]{2,1,0:T(8,128)(2,1)} custom-call(s32[2,4,64]{2,1,0:T(4,128)} %bitcast.52, bf16[128,4,1440]{2,1,0:T(4,128)(2,1)} %bitcast.55, bf16[128,1440]{1,0:T(8,128)(2,1)} %bitcast.49), custom_call_target="tpu_custom_call" | custom-call | tf_op jit(solution)/shard_map/pallas_call | solution.py:348
  6.3 11.4 %all-to-all-start = ((bf16[32,544,128]{2,1,0:T(8,128)(2,1)}), bf16[32,544,128]{2,1,0:T(8,128)(2,1)}, u32[]{:S(2)}, u32[]{:S(2)}) async-start(bf16[32,544,128]{2,1,0:T(8,128)(2,1)} %shard_map.94), calls=%async_computation | async-start | bytes 8912896 | tf_op jit(solution)/shard_map/all_to_all | solution.py:359
  17.7 0.1 convert_element_type.13
  17.8 0.1 broadcast_in_dim.64
  17.9 0.1 broadcast_in_dim.65
  18.0 0.1 bitcast_select_fusion
  18.1 1.3 collective-permute-start
  19.4 1.3 collective-permute-start.1
  20.7 1.3 collective-permute-start.2
  22.0 1.3 collective-permute-start.3
  23.3 1.3 collective-permute-start.4
  24.6 1.4 shard_map.97
  26.0 0.9 copy-done.6
  26.9 0.9 copy-done.8
  27.8 0.9 copy-done.10
  28.7 0.3 convolution_bitcast_fusion
  29.0 0.1 copy.16
  29.1 0.1 div.11
  29.2 0.7 copy-done.13
  29.9 1.3 collective-permute-start.5
  31.2 0.7 copy-done.15
  31.9 1.3 collective-permute-start.6
  33.2 0.7 bitcast_divide_fusion.gate_ref
  33.9 0.7 copy-done.17
  34.6 3.3 %collective-permute-done.3.refs_3_ = bf16[72,1440]{1,0:T(8,128)(2,1)S(1)} collective-permute-done((bf16[72,1440]{1,0:T(8,128)(2,1)S(1)}, bf16[72,1440]{1,0:T(8,128)(2,1)S(1)}, u32[]{:S(2)}, u32[]{:S(2)}) %collective-permute-start.3) | collective-permute-done | bytes 207392 | tf_op jit(solution)/shard_map/ppermute | solution.py:396
  37.9 0.7 copy-done.19
  38.6 0.7 copy-done.21
  39.3 8.1 %collective-permute-done.5.refs_5_ = bf16[72,1440]{1,0:T(8,128)(2,1)S(1)} collective-permute-done((bf16[72,1440]{1,0:T(8,128)(2,1)S(1)}, bf16[72,1440]{1,0:T(8,128)(2,1)S(1)}, u32[]{:S(2)}, u32[]{:S(2)}) %collective-permute-start.5) | collective-permute-done | bytes 207392 | tf_op jit(solution)/shard_map/ppermute | solution.py:396
  47.4 0.6 collective-permute-done.6.refs_6_
  48.0 2.3 copy-done
  50.3 0.9 copy-done.5
  51.2 0.9 copy-done.14
  52.2 0.9 copy-done.16
  53.1 0.9 copy-done.18
  54.0 0.9 copy-done.20
  55.0 0.9 copy-done.22
  55.9 2.6 %shard_map.95 = (bf16[512,1440]{1,0:T(8,128)(2,1)S(1)}, bf16[512,1440]{1,0:T(8,128)(2,1)S(1)}, f32[32,128]{1,0:T(8,128)S(1)}) custom-call(bf16[72,1440]{1,0:T(8,128)(2,1)S(1)} %copy-done.14, bf16[72,1440]{1,0:T(8,128)(2,1)S(1)} %copy-done.16, bf16[72,1440]{1,0:T(8,128)(2,1)S(1)} %copy-done.18, bf16[72,1440]{1,0:T(8,128)(2,1)S(1)} %copy-done.20, ...), custom_call_target="tpu_custom_call" | custom-call | tf_op jit(solution)/shard_map/pallas_call | solution.py:348
  58.5 59.6 %all-to-all-done.got_ref = bf16[32,544,128]{2,1,0:T(8,128)(2,1)} async-done(((bf16[32,544,128]{2,1,0:T(8,128)(2,1)}), bf16[32,544,128]{2,1,0:T(8,128)(2,1)}, u32[]{:S(2)}, u32[]{:S(2)}) %all-to-all-start) | async-done | bytes 4456480 | tf_op jit(solution)/shard_map/all_to_all | solution.py:359
  118.2 2.3 copy-done.1
  120.4 7.5 %shard_map.96 = (bf16[768,1440]{1,0:T(8,128)(2,1)S(1)}, bf16[768,256]{1,0:T(8,128)(2,1)S(1)}) custom-call(bf16[32,544,128]{2,1,0:T(8,128)(2,1)} %all-to-all-done.got_ref, bf16[1440,1440]{1,0:T(8,128)(2,1)S(1)} %bitcast.44, bf16[512,1440]{1,0:T(8,128)(2,1)S(1)} %get-tuple-element.145.back_ref), custom_call_target="tpu_custom_call" | custom-call | tf_op jit(solution)/shard_map/pallas_call | solution.py:348
  128.0 23.5 %all_to_all.25 = bf16[32,24,256]{2,1,0:T(8,128)(2,1)S(1)} all-to-all(bf16[32,24,256]{2,1,0:T(8,128)(2,1)S(1)} %bitcast.51), channel_id=1, replica_groups=mesh['pipe'=8,'expert'=32] {'expert'}, dimensions={0} | all-to-all | bytes 786432 | tf_op jit(solution)/shard_map/all_to_all | solution.py:359
  151.5 1.2 shard_map.98
  152.7 11.8 %all_to_all.26.got_ref = bf16[8,8,2048]{2,1,0:T(8,128)(2,1)S(1)} all-to-all(bf16[8,8,2048]{2,1,0:T(8,128)(2,1)S(1)} %shard_map.98), channel_id=1, replica_groups=mesh['pipe'=8,'expert'=32] {'pipe'}, dimensions={0} | all-to-all | bytes 524288 | tf_op jit(solution)/shard_map/all_to_all | solution.py:359
  164.5 1.1 shard_map.99
  165.6 14.2 %all_to_all.27.got_ref = bf16[32,16,128]{2,1,0:T(8,128)(2,1)S(1)} all-to-all(bf16[32,16,128]{2,1,0:T(8,128)(2,1)S(1)} %get-tuple-element.135), channel_id=1, replica_groups=mesh['pipe'=8,'expert'=32] {'expert'}, dimensions={0} | all-to-all | bytes 262144 | tf_op jit(solution)/shard_map/all_to_all | solution.py:359
  179.9 3.9 %shard_map.100 = (bf16[768,1536]{1,0:T(8,128)(2,1)S(1)}, bf16[128,1440]{1,0:T(8,128)(2,1)}) custom-call(bf16[32,16,128]{2,1,0:T(8,128)(2,1)S(1)} %all_to_all.27.got_ref, bf16[768,1440]{1,0:T(8,128)(2,1)S(1)} %get-tuple-element.144.base_ref, bf16[512,1440]{1,0:T(8,128)(2,1)S(1)} %get-tuple-element.145.back_ref, ...), custom_call_target="tpu_custom_call" | custom-call | tf_op jit(solution)/shard_map/pallas_call | solution.py:348
  183.8 59.9 %all_to_all.28 = bf16[32,24,1536]{2,1,0:T(8,128)(2,1)S(1)} all-to-all(bf16[32,24,1536]{2,1,0:T(8,128)(2,1)S(1)} %bitcast.46), channel_id=1, replica_groups=mesh['pipe'=8,'expert'=32] {'expert'}, dimensions={0} | all-to-all | bytes 4718592 | tf_op jit(solution)/shard_map/all_to_all | solution.py:359
  243.7 2.5 %shard_map.101 = (bf16[128,4,1440]{2,1,0:T(4,128)(2,1)}, f32[32,45]{1,0:T(8,128)}) custom-call(bf16[768,1536]{1,0:T(8,128)(2,1)S(1)} %bitcast.45, bf16[512,768]{1,0:T(8,128)(2,1)S(1)} %copy-done.11), custom_call_target="tpu_custom_call" | custom-call | tf_op jit(solution)/shard_map/pallas_call | solution.py:348
  (47 shorter events, 0.3 us)
Async XLA Ops:
  6.2 11.4 %copy-start.23 = (s32[1,2,64,4]{2,3,1,0:T(4,128)S(1)}, s32[1,2,64,4]{2,3,1,0:T(4,128)}, u32[]{:S(2)}) copy-start(s32[1,2,64,4]{2,3,1,0:T(4,128)} %param.9) | copy-start | bytes 6148
  6.3 11.5 %copy-start.25 = (s32[1,2]{1,0:T(1,128)S(1)}, s32[1,2]{1,0:T(1,128)}, u32[]{:S(2)}) copy-start(s32[1,2]{1,0:T(1,128)} %param.10) | copy-start | bytes 28
  6.3 11.7 %copy-start.24 = (bf16[1,2,1440,32]{2,3,1,0:T(8,128)(2,1)S(1)}, bf16[1,2,1440,32]{2,3,1,0:T(8,128)(2,1)}, u32[]{:S(2)}) copy-start(bf16[1,2,1440,32]{2,3,1,0:T(8,128)(2,1)} %param.11) | copy-start | bytes 552964
  6.3 22.4 %copy-start.2 = (bf16[1,2,64,1440]{3,2,1,0:T(8,128)(2,1)S(1)}, bf16[1,2,64,1440]{3,2,1,0:T(8,128)(2,1)}, u32[]{:S(2)}) copy-start(bf16[1,2,64,1440]{3,2,1,0:T(8,128)(2,1)} %param.7) | copy-start | bytes 1105924
  6.3 111.9 %all-to-all-start = ((bf16[32,544,128]{2,1,0:T(8,128)(2,1)}), bf16[32,544,128]{2,1,0:T(8,128)(2,1)}, u32[]{:S(2)}, u32[]{:S(2)}) async-start(bf16[32,544,128]{2,1,0:T(8,128)(2,1)} %shard_map.94), calls=%async_computation | async-start | bytes 8912896 | tf_op jit(solution)/shard_map/all_to_all | solution.py:359
  18.1 29.9 %copy-start.4 = (bf16[72,1440]{1,0:T(8,128)(2,1)}, bf16[72,1440]{1,0:T(8,128)(2,1)S(1)}, u32[]{:S(2)}) copy-start(bf16[72,1440]{1,0:T(8,128)(2,1)S(1)} %fusion.1.refs_7_) | copy-start | bytes 622084
  18.1 11.1 %collective-permute-start = (bf16[72,1440]{1,0:T(8,128)(2,1)S(1)}, bf16[72,1440]{1,0:T(8,128)(2,1)S(1)}, u32[]{:S(2)}, u32[]{:S(2)}) collective-permute-start(bf16[72,1440]{1,0:T(8,128)(2,1)S(1)} %fusion.1.refs_7_), channel_id=1, source_target_pairs={{32,0},{64,32},{96,64},{128,96},{160,128},{192,160},{224,192},{33,... | collective-permute-start | bytes 622088 | tf_op jit(solution)/shard_map/ppermute | solution.py:396
  19.4 11.8 %collective-permute-start.1 = (bf16[72,1440]{1,0:T(8,128)(2,1)S(1)}, bf16[72,1440]{1,0:T(8,128)(2,1)S(1)}, u32[]{:S(2)}, u32[]{:S(2)}) collective-permute-start(bf16[72,1440]{1,0:T(8,128)(2,1)S(1)} %fusion.1.refs_7_), channel_id=1, source_target_pairs={{64,0},{96,32},{128,64},{160,96},{192,128},{224,160},{65,1},{97,33... | collective-permute-start | bytes 622088 | tf_op jit(solution)/shard_map/ppermute | solution.py:396
  20.7 13.2 %collective-permute-start.2 = (bf16[72,1440]{1,0:T(8,128)(2,1)S(1)}, bf16[72,1440]{1,0:T(8,128)(2,1)S(1)}, u32[]{:S(2)}, u32[]{:S(2)}) collective-permute-start(bf16[72,1440]{1,0:T(8,128)(2,1)S(1)} %fusion.1.refs_7_), channel_id=1, source_target_pairs={{96,0},{128,32},{160,64},{192,96},{224,128},{97,1},{129,33},{161,6... | collective-permute-start | bytes 622088 | tf_op jit(solution)/shard_map/ppermute | solution.py:396
  22.0 15.9 %collective-permute-start.3 = (bf16[72,1440]{1,0:T(8,128)(2,1)S(1)}, bf16[72,1440]{1,0:T(8,128)(2,1)S(1)}, u32[]{:S(2)}, u32[]{:S(2)}) collective-permute-start(bf16[72,1440]{1,0:T(8,128)(2,1)S(1)} %fusion.1.refs_7_), channel_id=1, source_target_pairs={{128,0},{160,32},{192,64},{224,96},{129,1},{161,33},{193,65},{225,... | collective-permute-start | bytes 622088 | tf_op jit(solution)/shard_map/ppermute | solution.py:396
  23.3 15.3 %collective-permute-start.4 = (bf16[72,1440]{1,0:T(8,128)(2,1)S(1)}, bf16[72,1440]{1,0:T(8,128)(2,1)S(1)}, u32[]{:S(2)}, u32[]{:S(2)}) collective-permute-start(bf16[72,1440]{1,0:T(8,128)(2,1)S(1)} %fusion.1.refs_7_), channel_id=1, source_target_pairs={{160,0},{192,32},{224,64},{161,1},{193,33},{225,65},{162,2},{194,3... | collective-permute-start | bytes 622088 | tf_op jit(solution)/shard_map/ppermute | solution.py:396
  26.0 0.9 copy-start.6
  26.9 0.9 copy-start.8
  27.8 0.9 copy-start.10
  29.2 0.7 copy-start.13
  29.9 17.5 %collective-permute-start.5 = (bf16[72,1440]{1,0:T(8,128)(2,1)S(1)}, bf16[72,1440]{1,0:T(8,128)(2,1)S(1)}, u32[]{:S(2)}, u32[]{:S(2)}) collective-permute-start(bf16[72,1440]{1,0:T(8,128)(2,1)S(1)} %fusion.1.refs_7_), channel_id=1, source_target_pairs={{192,0},{224,32},{193,1},{225,33},{194,2},{226,34},{195,3},{227,35... | collective-permute-start | bytes 622088 | tf_op jit(solution)/shard_map/ppermute | solution.py:396
  31.2 0.7 copy-start.15
  31.9 16.1 %collective-permute-start.6 = (bf16[72,1440]{1,0:T(8,128)(2,1)S(1)}, bf16[72,1440]{1,0:T(8,128)(2,1)S(1)}, u32[]{:S(2)}, u32[]{:S(2)}) collective-permute-start(bf16[72,1440]{1,0:T(8,128)(2,1)S(1)} %fusion.1.refs_7_), channel_id=1, source_target_pairs={{224,0},{225,1},{226,2},{227,3},{228,4},{229,5},{230,6},{231,7},{2... | collective-permute-start | bytes 622088 | tf_op jit(solution)/shard_map/ppermute | solution.py:396
  33.9 0.7 copy-start.17
  37.9 0.7 copy-start.19
  38.6 0.7 copy-start.21
  48.0 2.3 copy-start
  50.3 0.9 copy-start.5
  51.2 0.9 copy-start.14
  52.2 0.9 copy-start.16
  53.1 0.9 copy-start.18
  54.0 0.9 copy-start.20
  55.0 0.9 copy-start.22
  118.2 2.3 copy-start.1
  120.4 31.0 %copy-start.7 = (bf16[512,768]{1,0:T(8,128)(2,1)S(1)}, bf16[512,768]{1,0:T(8,128)(2,1)}, u32[]{:S(2)}) copy-start(bf16[512,768]{1,0:T(8,128)(2,1)} %copy-done.6) | copy-start | bytes 2359300
  120.4 31.0 %copy-start.12 = (f32[128,4]{1,0:T(8,128)S(1)}, f32[128,4]{1,0:T(8,128)}, u32[]{:S(2)}) copy-start(f32[128,4]{1,0:T(8,128)} %bitcast_divide_fusion.gate_ref) | copy-start | bytes 6148
  128.0 36.6 %copy-start.9 = (bf16[768,512]{1,0:T(8,128)(2,1)S(1)}, bf16[768,512]{1,0:T(8,128)(2,1)}, u32[]{:S(2)}) copy-start(bf16[768,512]{1,0:T(8,128)(2,1)} %copy-done.8) | copy-start | bytes 2359300
  128.0 51.9 %copy-start.3 = (bf16[2,64,1440]{2,1,0:T(8,128)(2,1)S(1)}, bf16[2,64,1440]{2,1,0:T(8,128)(2,1)}, u32[]{:S(2)}) copy-start(bf16[2,64,1440]{2,1,0:T(8,128)(2,1)} %param.13) | copy-start | bytes 1105924
  183.8 59.9 %copy-start.11 = (bf16[512,768]{1,0:T(8,128)(2,1)S(1)}, bf16[512,768]{1,0:T(8,128)(2,1)}, u32[]{:S(2)}) copy-start(bf16[512,768]{1,0:T(8,128)(2,1)} %copy-done.10) | copy-start | bytes 2359300

commit v8 on v7

--- a/solution.py
+++ b/solution.py
@@ -181,12 +181,16 @@
     out_ref[...] = jnp.where(lane < LATER, proj, tail).astype(BF)
 
 
-def picks_kernel(ids_ref, first_ref, second_ref, third_ref):
+def picks_kernel(ids_ref, first_ref, second_ref, third_ref, router_ref):
     codes = slot_codes(ids_ref)
     wide = jnp.concatenate(codes, axis=1)
     first_ref[...] = slots_by_rows(wide)
     second_ref[...] = rows_by_slots(wide)
     third_ref[...] = slots_by_rows(token_major(codes))
+    width = router_ref.shape[1]
+    peer = divided(iota((ALL, 1), 0), ROWS)
+    source = iota((ALL, 1), 0) + (width // E - ROWS) * peer
+    router_ref[...] = one(source == iota((ALL, width), 1))
 
 
 def id_masks(ids_ref):
@@ -280,7 +284,8 @@
 
 
 def answer_kernel(
-    got_ref, base_ref, back_ref, coef_ref, tab_ref, grad_ref, acts_ref, out_ref, pass_hbm, pass_ref, sems
+    got_ref, base_ref, back_ref, coef_ref, tab_ref, grad_ref, acts_ref, select_ref,
+    out_ref, pass_hbm, pass_ref, sems,
 ):
     for m in range(2):
         rows = slice(m * T, (m + 1) * T)
@@ -291,12 +296,8 @@
     own = coef_ref[:, LATER:W]
     width = acts_ref.shape[1]
     router = (dot(acts_ref[...], own, TN) / T).astype(BF)
-    each = width // E
     ahead = jnp.concatenate([router[ROWS:], router[:ROWS]], axis=0)
-    col = iota((ALL, width), 1)
-    peer = divided(iota((ALL, 1), 0), ROWS)
-    source = iota((ALL, 1), 0) + (each - ROWS) * peer
-    select = one(source == col)
+    select = select_ref[...]
     out_ref[:, width : width + E] = dot(select, router, NN).astype(BF)
     out_ref[:, width + E : width + 2 * E] = dot(select, ahead, NN).astype(BF)
     out_ref[:, width + 2 * E :] = jnp.zeros((ALL, out_ref.shape[1] - width - 2 * E), BF)
@@ -404,7 +405,7 @@
 
     picks = call(
         picks_kernel,
-        [((N * K, ALL), BF), ((ALL, N * K), BF), ((N * K, ALL), BF)],
+        [((N * K, ALL), BF), ((ALL, N * K), BF), ((N * K, ALL), BF), ((ALL, width), BF)],
         (turned,),
         12,
     )
@@ -452,7 +453,7 @@
     answer, passed = call(
         answer_kernel,
         [((ALL, wide), BF), ((N, width), BF)],
-        (coef_got, base, back, coef, table_rows, grads, inputs.reshape(N, width)),
+        (coef_got, base, back, coef, table_rows, grads, inputs.reshape(N, width), picks[3]),
         MIBS[6],
         scratch=[((N, width), BF)],
         sems=1,

time: 247 us -> 247 us (level)
  waiting for transfers between devices: 71.7 us -> 68.9 us
    unnamed x52 -> x56, local copies, waits for them, and re-layouts: 16.2 us -> 18.4 us
where the time goes in v8:
time: 247 us; the launch traced here: 246 us
  blocking collectives  110 us (45%)
  waiting for transfers between devices  68.9 us (28%)
  Pallas kernels  26.6 us (11%)
  starting transfers between devices  20.4 us (8%)
  local copies, waits for them, and re-layouts  18.8 us (8%)
    all_to_all x4, blocking collectives, exchange(): return lax.all_to_all(x, axis, split_axis=0, concat_axis=0, tiled=True)  110 us
    all_to_all x1, waiting for transfers between devices, exchange(): return lax.all_to_all(x, axis, split_axis=0, concat_axis=0, tiled=True)  59.3 us
    pallas_call x8, Pallas kernels, call(): pl.pallas_call(body, out_shape=[jax.ShapeDtypeStruct(s, d) for s, d in sh...  26.6 us
    unnamed x56, local copies, waits for them, and re-layouts  18.4 us
    all_to_all x1, starting transfers between devices, exchange(): return lax.all_to_all(x, axis, split_axis=0, concat_axis=0, tiled=True)  11.4 us
    ppermute x7, waiting for transfers between devices, on_device(): lax.ppermute(own, 'pipe', [(i, i - by) for i in range(by, pipe)])  9.61 us
    ppermute x7, starting transfers between devices, on_device(): lax.ppermute(own, 'pipe', [(i, i - by) for i in range(by, pipe)])  9.02 us
  transfers between devices with their start and end apart: 8, of which 5 were waited for; matrix products, arithmetic and copies ran while one was open for 1% of the time, Pallas kernels for 2%

profile of v8, /device:TPU:32, one launch (start us, length us, event | category | flops | bytes accessed | tf_op | source)
XLA Modules:
  0.0 246.4 jit_solution(13429936605766713271)
XLA Ops:
  0.6 5.6 %shard_map.94 = bf16[32,544,128]{2,1,0:T(8,128)(2,1)} custom-call(s32[2,4,64]{2,1,0:T(4,128)} %bitcast.52, bf16[128,4,1440]{2,1,0:T(4,128)(2,1)} %bitcast.55, bf16[128,1440]{1,0:T(8,128)(2,1)} %bitcast.48), custom_call_target="tpu_custom_call" | custom-call | tf_op jit(solution)/shard_map/pallas_call | solution.py:349
  6.3 11.4 %all-to-all-start = ((bf16[32,544,128]{2,1,0:T(8,128)(2,1)}), bf16[32,544,128]{2,1,0:T(8,128)(2,1)}, u32[]{:S(2)}, u32[]{:S(2)}) async-start(bf16[32,544,128]{2,1,0:T(8,128)(2,1)} %shard_map.94), calls=%async_computation | async-start | bytes 8912896 | tf_op jit(solution)/shard_map/all_to_all | solution.py:360
  17.7 0.1 convert_element_type.13
  17.9 0.1 broadcast_in_dim.65
  18.0 0.1 bitcast_select_fusion
  18.1 1.3 collective-permute-start
  19.4 1.3 collective-permute-start.1
  20.7 1.3 collective-permute-start.2
  22.0 1.3 collective-permute-start.3
  23.3 1.3 collective-permute-start.4
  24.6 2.1 shard_map.97
  26.7 1.4 copy-done.2
  28.1 0.9 copy-done.8
  29.0 0.9 copy-done.10
  29.9 0.9 copy-done.12
  30.8 0.3 convolution_bitcast_fusion
  31.2 0.1 copy.16
  31.4 0.7 copy-done.15
  32.0 1.3 collective-permute-start.5
  33.4 0.7 copy-done.17
  34.0 1.3 collective-permute-start.6
  35.3 0.7 copy-done.6
  36.0 0.7 bitcast_divide_fusion.gate_ref
  36.7 0.7 copy-done.19
  37.4 0.5 collective-permute-done.3.refs_3_
  37.9 0.7 copy-done.21
  38.6 0.7 copy-done.23
  39.3 6.7 %collective-permute-done.5.refs_5_ = bf16[72,1440]{1,0:T(8,128)(2,1)S(1)} collective-permute-done((bf16[72,1440]{1,0:T(8,128)(2,1)S(1)}, bf16[72,1440]{1,0:T(8,128)(2,1)S(1)}, u32[]{:S(2)}, u32[]{:S(2)}) %collective-permute-start.5) | collective-permute-done | bytes 207392 | tf_op jit(solution)/shard_map/ppermute | solution.py:397
  46.0 2.4 collective-permute-done.6.refs_6_
  48.4 2.3 copy-done
  50.6 0.9 copy-done.7
  51.6 0.9 copy-done.16
  52.5 0.9 copy-done.18
  53.4 0.9 copy-done.20
  54.4 0.9 copy-done.22
  55.3 0.9 copy-done.24
  56.2 2.6 %shard_map.95 = (bf16[512,1440]{1,0:T(8,128)(2,1)S(1)}, bf16[512,1440]{1,0:T(8,128)(2,1)S(1)}, f32[32,128]{1,0:T(8,128)S(1)}) custom-call(bf16[72,1440]{1,0:T(8,128)(2,1)S(1)} %copy-done.16, bf16[72,1440]{1,0:T(8,128)(2,1)S(1)} %copy-done.18, bf16[72,1440]{1,0:T(8,128)(2,1)S(1)} %copy-done.20, bf16[72,1440]{1,0:T(8,128)(2,1)S(1)} %copy-done.22, ...), custom_call_target="tpu_custom_call" | custom-call | tf_op jit(solution)/shard_map/pallas_call | solution.py:349
  58.9 59.3 %all-to-all-done.got_ref = bf16[32,544,128]{2,1,0:T(8,128)(2,1)} async-done(((bf16[32,544,128]{2,1,0:T(8,128)(2,1)}), bf16[32,544,128]{2,1,0:T(8,128)(2,1)}, u32[]{:S(2)}, u32[]{:S(2)}) %all-to-all-start) | async-done | bytes 4456480 | tf_op jit(solution)/shard_map/all_to_all | solution.py:360
  118.2 2.3 copy-done.1
  120.4 7.6 %shard_map.96 = (bf16[768,1440]{1,0:T(8,128)(2,1)S(1)}, bf16[768,256]{1,0:T(8,128)(2,1)S(1)}) custom-call(bf16[32,544,128]{2,1,0:T(8,128)(2,1)} %all-to-all-done.got_ref, bf16[1440,1440]{1,0:T(8,128)(2,1)S(1)} %bitcast.44, bf16[512,1440]{1,0:T(8,128)(2,1)S(1)} %get-tuple-element.158.back_ref), custom_call_target="tpu_custom_call" | custom-call | tf_op jit(solution)/shard_map/pallas_call | solution.py:349
  128.0 23.6 %all_to_all.25 = bf16[32,24,256]{2,1,0:T(8,128)(2,1)S(1)} all-to-all(bf16[32,24,256]{2,1,0:T(8,128)(2,1)S(1)} %bitcast.51), channel_id=1, replica_groups=mesh['pipe'=8,'expert'=32] {'expert'}, dimensions={0} | all-to-all | bytes 786432 | tf_op jit(solution)/shard_map/all_to_all | solution.py:360
  151.6 1.2 shard_map.98
  152.9 11.8 %all_to_all.26.got_ref = bf16[8,8,2048]{2,1,0:T(8,128)(2,1)S(1)} all-to-all(bf16[8,8,2048]{2,1,0:T(8,128)(2,1)S(1)} %shard_map.98), channel_id=1, replica_groups=mesh['pipe'=8,'expert'=32] {'pipe'}, dimensions={0} | all-to-all | bytes 524288 | tf_op jit(solution)/shard_map/all_to_all | solution.py:360
  164.7 1.1 shard_map.99
  165.8 14.2 %all_to_all.27.got_ref = bf16[32,16,128]{2,1,0:T(8,128)(2,1)S(1)} all-to-all(bf16[32,16,128]{2,1,0:T(8,128)(2,1)S(1)} %get-tuple-element.147), channel_id=1, replica_groups=mesh['pipe'=8,'expert'=32] {'expert'}, dimensions={0} | all-to-all | bytes 262144 | tf_op jit(solution)/shard_map/all_to_all | solution.py:360
  180.0 3.9 %shard_map.100 = (bf16[768,1536]{1,0:T(8,128)(2,1)S(1)}, bf16[128,1440]{1,0:T(8,128)(2,1)}) custom-call(bf16[32,16,128]{2,1,0:T(8,128)(2,1)S(1)} %all_to_all.27.got_ref, bf16[768,1440]{1,0:T(8,128)(2,1)S(1)} %get-tuple-element.157.base_ref, bf16[512,1440]{1,0:T(8,128)(2,1)S(1)} %get-tuple-element.158.back_ref, ...), custom_call_target="tpu_custom_call" | custom-call | tf_op jit(solution)/shard_map/pallas_call | solution.py:349
  183.9 59.9 %all_to_all.28 = bf16[32,24,1536]{2,1,0:T(8,128)(2,1)S(1)} all-to-all(bf16[32,24,1536]{2,1,0:T(8,128)(2,1)S(1)} %bitcast.46), channel_id=1, replica_groups=mesh['pipe'=8,'expert'=32] {'expert'}, dimensions={0} | all-to-all | bytes 4718592 | tf_op jit(solution)/shard_map/all_to_all | solution.py:360
  243.8 2.5 %shard_map.101 = (bf16[128,4,1440]{2,1,0:T(4,128)(2,1)}, f32[32,45]{1,0:T(8,128)}) custom-call(bf16[768,1536]{1,0:T(8,128)(2,1)S(1)} %bitcast.45, bf16[512,768]{1,0:T(8,128)(2,1)S(1)} %copy-done.13), custom_call_target="tpu_custom_call" | custom-call | tf_op jit(solution)/shard_map/pallas_call | solution.py:349
  (51 shorter events, 0.4 us)
Async XLA Ops:
  6.2 11.4 %copy-start.25 = (s32[1,2,64,4]{2,3,1,0:T(4,128)S(1)}, s32[1,2,64,4]{2,3,1,0:T(4,128)}, u32[]{:S(2)}) copy-start(s32[1,2,64,4]{2,3,1,0:T(4,128)} %param.9) | copy-start | bytes 6148
  6.2 11.5 %copy-start.27 = (s32[1,2]{1,0:T(1,128)S(1)}, s32[1,2]{1,0:T(1,128)}, u32[]{:S(2)}) copy-start(s32[1,2]{1,0:T(1,128)} %param.10) | copy-start | bytes 28
  6.2 11.7 %copy-start.26 = (bf16[1,2,1440,32]{2,3,1,0:T(8,128)(2,1)S(1)}, bf16[1,2,1440,32]{2,3,1,0:T(8,128)(2,1)}, u32[]{:S(2)}) copy-start(bf16[1,2,1440,32]{2,3,1,0:T(8,128)(2,1)} %param.11) | copy-start | bytes 552964
  6.3 24.6 %copy-start.4 = (bf16[1,2,64,1440]{3,2,1,0:T(8,128)(2,1)S(1)}, bf16[1,2,64,1440]{3,2,1,0:T(8,128)(2,1)}, u32[]{:S(2)}) copy-start(bf16[1,2,64,1440]{3,2,1,0:T(8,128)(2,1)} %param.7) | copy-start | bytes 1105924
  6.3 111.9 %all-to-all-start = ((bf16[32,544,128]{2,1,0:T(8,128)(2,1)}), bf16[32,544,128]{2,1,0:T(8,128)(2,1)}, u32[]{:S(2)}, u32[]{:S(2)}) async-start(bf16[32,544,128]{2,1,0:T(8,128)(2,1)} %shard_map.94), calls=%async_computation | async-start | bytes 8912896 | tf_op jit(solution)/shard_map/all_to_all | solution.py:360
  18.1 13.3 %collective-permute-start = (bf16[72,1440]{1,0:T(8,128)(2,1)S(1)}, bf16[72,1440]{1,0:T(8,128)(2,1)S(1)}, u32[]{:S(2)}, u32[]{:S(2)}) collective-permute-start(bf16[72,1440]{1,0:T(8,128)(2,1)S(1)} %fusion.1.refs_7_), channel_id=1, source_target_pairs={{32,0},{64,32},{96,64},{128,96},{160,128},{192,160},{224,192},{33,... | collective-permute-start | bytes 622088 | tf_op jit(solution)/shard_map/ppermute | solution.py:397
  19.4 13.9 %collective-permute-start.1 = (bf16[72,1440]{1,0:T(8,128)(2,1)S(1)}, bf16[72,1440]{1,0:T(8,128)(2,1)S(1)}, u32[]{:S(2)}, u32[]{:S(2)}) collective-permute-start(bf16[72,1440]{1,0:T(8,128)(2,1)S(1)} %fusion.1.refs_7_), channel_id=1, source_target_pairs={{64,0},{96,32},{128,64},{160,96},{192,128},{224,160},{65,1},{97,33... | collective-permute-start | bytes 622088 | tf_op jit(solution)/shard_map/ppermute | solution.py:397
  20.7 16.0 %collective-permute-start.2 = (bf16[72,1440]{1,0:T(8,128)(2,1)S(1)}, bf16[72,1440]{1,0:T(8,128)(2,1)S(1)}, u32[]{:S(2)}, u32[]{:S(2)}) collective-permute-start(bf16[72,1440]{1,0:T(8,128)(2,1)S(1)} %fusion.1.refs_7_), channel_id=1, source_target_pairs={{96,0},{128,32},{160,64},{192,96},{224,128},{97,1},{129,33},{161,6... | collective-permute-start | bytes 622088 | tf_op jit(solution)/shard_map/ppermute | solution.py:397
  22.0 15.9 %collective-permute-start.3 = (bf16[72,1440]{1,0:T(8,128)(2,1)S(1)}, bf16[72,1440]{1,0:T(8,128)(2,1)S(1)}, u32[]{:S(2)}, u32[]{:S(2)}) collective-permute-start(bf16[72,1440]{1,0:T(8,128)(2,1)S(1)} %fusion.1.refs_7_), channel_id=1, source_target_pairs={{128,0},{160,32},{192,64},{224,96},{129,1},{161,33},{193,65},{225,... | collective-permute-start | bytes 622088 | tf_op jit(solution)/shard_map/ppermute | solution.py:397
  23.3 15.3 %collective-permute-start.4 = (bf16[72,1440]{1,0:T(8,128)(2,1)S(1)}, bf16[72,1440]{1,0:T(8,128)(2,1)S(1)}, u32[]{:S(2)}, u32[]{:S(2)}) collective-permute-start(bf16[72,1440]{1,0:T(8,128)(2,1)S(1)} %fusion.1.refs_7_), channel_id=1, source_target_pairs={{160,0},{192,32},{224,64},{161,1},{193,33},{225,65},{162,2},{194,3... | collective-permute-start | bytes 622088 | tf_op jit(solution)/shard_map/ppermute | solution.py:397
  26.7 1.4 copy-start.2
  28.1 0.9 copy-start.8
  29.0 0.9 copy-start.10
  29.9 0.9 copy-start.12
  31.4 0.7 copy-start.15
  32.0 13.9 %collective-permute-start.5 = (bf16[72,1440]{1,0:T(8,128)(2,1)S(1)}, bf16[72,1440]{1,0:T(8,128)(2,1)S(1)}, u32[]{:S(2)}, u32[]{:S(2)}) collective-permute-start(bf16[72,1440]{1,0:T(8,128)(2,1)S(1)} %fusion.1.refs_7_), channel_id=1, source_target_pairs={{192,0},{224,32},{193,1},{225,33},{194,2},{226,34},{195,3},{227,35... | collective-permute-start | bytes 622088 | tf_op jit(solution)/shard_map/ppermute | solution.py:397
  33.3 0.7 copy-start.17
  34.0 14.3 %collective-permute-start.6 = (bf16[72,1440]{1,0:T(8,128)(2,1)S(1)}, bf16[72,1440]{1,0:T(8,128)(2,1)S(1)}, u32[]{:S(2)}, u32[]{:S(2)}) collective-permute-start(bf16[72,1440]{1,0:T(8,128)(2,1)S(1)} %fusion.1.refs_7_), channel_id=1, source_target_pairs={{224,0},{225,1},{226,2},{227,3},{228,4},{229,5},{230,6},{231,7},{2... | collective-permute-start | bytes 622088 | tf_op jit(solution)/shard_map/ppermute | solution.py:397
  35.3 0.7 copy-start.6
  36.7 0.7 copy-start.19
  37.9 0.7 copy-start.21
  38.6 0.7 copy-start.23
  48.4 2.3 copy-start
  50.6 0.9 copy-start.7
  51.6 0.9 copy-start.16
  52.5 0.9 copy-start.18
  53.4 0.9 copy-start.20
  54.4 0.9 copy-start.22
  55.3 0.9 copy-start.24
  118.2 2.3 copy-start.1
  120.4 31.2 %copy-start.9 = (bf16[512,768]{1,0:T(8,128)(2,1)S(1)}, bf16[512,768]{1,0:T(8,128)(2,1)}, u32[]{:S(2)}) copy-start(bf16[512,768]{1,0:T(8,128)(2,1)} %copy-done.8) | copy-start | bytes 2359300
  120.4 31.2 %copy-start.14 = (f32[128,4]{1,0:T(8,128)S(1)}, f32[128,4]{1,0:T(8,128)}, u32[]{:S(2)}) copy-start(f32[128,4]{1,0:T(8,128)} %bitcast_divide_fusion.gate_ref) | copy-start | bytes 6148
  120.4 44.3 %copy-start.11 = (bf16[768,512]{1,0:T(8,128)(2,1)S(1)}, bf16[768,512]{1,0:T(8,128)(2,1)}, u32[]{:S(2)}) copy-start(bf16[768,512]{1,0:T(8,128)(2,1)} %copy-done.10) | copy-start | bytes 2359300
  128.0 52.0 %copy-start.3 = (bf16[768,1440]{1,0:T(8,128)(2,1)S(1)}, bf16[768,1440]{1,0:T(8,128)(2,1)}, u32[]{:S(2)}) copy-start(bf16[768,1440]{1,0:T(8,128)(2,1)} %copy-done.2) | copy-start | bytes 6635524
  128.0 52.0 %copy-start.5 = (bf16[2,64,1440]{2,1,0:T(8,128)(2,1)S(1)}, bf16[2,64,1440]{2,1,0:T(8,128)(2,1)}, u32[]{:S(2)}) copy-start(bf16[2,64,1440]{2,1,0:T(8,128)(2,1)} %param.13) | copy-start | bytes 1105924
  183.9 59.9 %copy-start.13 = (bf16[512,768]{1,0:T(8,128)(2,1)S(1)}, bf16[512,768]{1,0:T(8,128)(2,1)}, u32[]{:S(2)}) copy-start(bf16[512,768]{1,0:T(8,128)(2,1)} %copy-done.12) | copy-start | bytes 2359300
